TPU v7x, 32 devices: a whole 2x2x4 slice. The times are simulated.
32 devices in a mesh: heads: 4 (over y, x), fsdp: 8 (over z, core).
Axes of the slice: x: 2, y: 2, z: 4, core: 2. Of those that a mesh axis runs over, the one named last changes fastest.
Arguments:
- inputs: bfloat16 [8, 3072, 1280], P('fsdp', 'heads'), may hold values from -6 to 6
- cotangent: bfloat16 [8, 3072, 1280], P('fsdp', 'heads'), may hold values from -6 to 6
- lengths: int32 [8, 3], P('fsdp'), may hold values from 1 to 1024, 1536 in all within a row
- adapter_ids: int32 [8, 4], P('fsdp'), may hold values from 0 to 7
- query_weight: bfloat16 [1280, 1280], P('fsdp'), may hold values from -0.15625 to 0.15625
- key_weight: bfloat16 [1280, 1280], P('fsdp'), may hold values from -0.15625 to 0.15625
- value_weight: bfloat16 [1280, 1280], P('fsdp'), may hold values from -0.15625 to 0.15625
- out_weight: bfloat16 [1280, 1280], P('fsdp'), may hold values from -1.25 to 1.25
- up_weight: bfloat16 [1280, 1280], P('fsdp'), may hold values from -0.15625 to 0.15625
- down_weight: bfloat16 [1280, 1280], P('fsdp'), may hold values from -0.15625 to 0.15625
- attn_gain: bfloat16 [1280], replicated, may hold values from 0.099609375 to 1.8984375
- mlp_gain: bfloat16 [1280], replicated, may hold values from 0.099609375 to 1.8984375
- query_scale: float32 [80], replicated, may hold values from 0.5 to 2
- adapter_in: bfloat16 [4, 8, 1280, 16], replicated, may hold values from -0.15625 to 0.15625
- adapter_out: bfloat16 [4, 8, 16, 1280], replicated, may hold values from -1.5 to 1.5
Outputs:
- outputs: bfloat16 [8, 3072, 1280], P('fsdp', 'heads')
- grad_inputs: float32 [8, 3072, 1280], P('fsdp', 'heads')
- grad_adapter_in: float32 [4, 8, 1280, 16], replicated
- grad_adapter_out: float32 [4, 8, 16, 1280], replicated
Inputs may be any that keep to these rules, and one draw needn't show every extreme that they name: In every group the 3 lengths sum to 1536, and the longest is 1024.
All inputs are finite; a program needn't handle non-finite values.
Results may differ from a plain program's by a relative error of at most 0.015.
The roundings to bfloat16 on the way count: a program that leaves them out, or rounds other values in their place, can miss the bound.
Values may be sent and summed in bfloat16 or wider, within the bound.
No kernel may reach another device: no remote copies, remote signals or barrier semaphores. Data moves between devices by JAX's collectives and lax.ppermute only.
A program may use at most 256 MiB of HBM per device.

v0:
```python
import jax
import jax.numpy as jnp
from jax import lax
from jax.experimental import pallas as pl
from jax.experimental.pallas import tpu as pltpu
from jax.sharding import PartitionSpec as P

D = 1280
HEADS = 16
HD = 80
RANK = 16
ADAPTERS = 8
AR = ADAPTERS * RANK
TOK = 3072
PROMPT = 1536
ROWS = 768
QB = 256
PARTS = TOK // ROWS
LH = HEADS // PARTS
HALF = ROWS // 2
PH = LH // 2
PW = PH * HD
WIDTH = LH * HD
SR = WIDTH * 128 // D
EPSILON = 1e-06
B = 256
f32, bf16 = jnp.float32, jnp.bfloat16


def nt(a, b):
    return lax.dot_general(a, b, (((1,), (1,)), ((), ())), preferred_element_type=f32)


def tn(a, b):
    return lax.dot_general(a, b, (((0,), (0,)), ((), ())), preferred_element_type=f32)


def nn(a, b):
    return lax.dot_general(a, b, (((1,), (0,)), ((), ())), preferred_element_type=f32)

def start_row(qpos, b1, b2):
    return jnp.where(qpos < PROMPT, 0, jnp.where(qpos < b1, PROMPT, jnp.where(qpos < b2, b1, b2)))

def first_block(i, b1, b2):
    q0 = i * B
    return jnp.where(q0 < b1, PROMPT, jnp.where(q0 < b2, b1, b2)) // B


def token_adapter(pos, meta):
    return jnp.where(
        pos < PROMPT, meta[2], jnp.where(pos < meta[0], meta[3], jnp.where(pos < meta[1], meta[4], meta[5]))
    )


def qkv_kernel(meta, first, low_ref, high_ref, gain_ref, wt_ref, down_ref, up_ref, scale_ref, *refs):
    out_ref, normed_ref, inner_ref, rows = refs[-4:]
    step = pl.program_id(0)

    @pl.when(step == 0)
    def _():
        rows[0:HALF, :] = low_ref[...]
        rows[HALF:ROWS, :] = high_ref[...]

    x = rows[pl.ds(pl.multiple_of(step * QB, QB), QB), :].astype(f32)
    q = lax.rsqrt(jnp.mean(x * x, axis=1, keepdims=True) + EPSILON)
    normed = (x * q * gain_ref[...]).astype(bf16)
    normed_ref[...] = normed
    pos = (first[0] + step) * QB + lax.broadcasted_iota(jnp.int32, (QB, 1), 0)
    lane = lax.broadcasted_iota(jnp.int32, (QB, 2 * AR), 1)
    chosen = (lane % AR) // RANK == token_adapter(pos, meta)
    inner = jnp.where(chosen, nn(normed, down_ref[...]), 0.0).astype(bf16)
    inner_ref[...] = inner
    out = nt(wt_ref[...], normed)
    query = out[:WIDTH] + nt(up_ref[0], inner[:, :AR])
    out_ref[0:WIDTH, :] = (query * scale_ref[...]).astype(bf16)
    out_ref[WIDTH : 2 * WIDTH, :] = out[WIDTH : 2 * WIDTH].astype(bf16)
    out_ref[2 * WIDTH :, :] = (out[2 * WIDTH :] + nt(up_ref[1], inner[:, AR:])).astype(bf16)


def qkv_project(meta, chunk, low, high, gain, wt, down, up, scale, done):
    whole = lambda shape: pl.BlockSpec(shape, lambda i, *_: (0, 0))
    second = 1 if high is None else 0
    first = (chunk * (ROWS // QB))[None].astype(jnp.int32)
    return pl.pallas_call(
        qkv_kernel,
        out_shape=(
            jax.ShapeDtypeStruct((3 * WIDTH, TOK), bf16),
            jax.ShapeDtypeStruct((TOK, D), bf16),
            jax.ShapeDtypeStruct((TOK, 2 * AR), bf16),
        ),
        grid_spec=pltpu.PrefetchScalarGridSpec(
            num_scalar_prefetch=2,
            grid=(ROWS // QB,),
            in_specs=[
                whole((HALF, D)),
                pl.BlockSpec((HALF, D), lambda i, *_: (second, 0)),
                whole((1, D)),
                whole((3 * WIDTH, D)),
                whole((D, 2 * AR)),
                pl.BlockSpec((2, WIDTH, AR), lambda i, *_: (0, 0, 0)),
                whole((WIDTH, 1)),
            ]
            + [pl.BlockSpec(memory_space=pl.ANY)] * len(done),
            out_specs=[
                pl.BlockSpec((3 * WIDTH, QB), lambda i, m, first: (0, first[0] + i)),
                pl.BlockSpec((QB, D), lambda i, m, first: (first[0] + i, 0)),
                pl.BlockSpec((QB, 2 * AR), lambda i, m, first: (first[0] + i, 0)),
            ],
            scratch_shapes=[pltpu.VMEM((ROWS, D), bf16)],
        ),
        input_output_aliases={9 + i: i for i in range(len(done))},
        compiler_params=pltpu.CompilerParams(dimension_semantics=("arbitrary",), vmem_limit_bytes=60 << 20),
        cost_estimate=pl.CostEstimate(flops=2 * ROWS * D * (3 * WIDTH + 2 * AR), bytes_accessed=8 << 20, transcendentals=0),
        name="qkv_project",
    )(meta, first, low, low if high is None else high, gain, wt, down, up, scale, *done)


def adapter_kernel(meta, g0_ref, g1_ref, normed_ref, inner_ref, up_ref, keep_ref, send_ref, facc, sacc):
    step = pl.program_id(0)

    @pl.when(step == 0)
    def _():
        facc[...] = jnp.zeros_like(facc)
        sacc[...] = jnp.zeros_like(sacc)

    query = jnp.concatenate([g0_ref[0, 0], g1_ref[0, 0]], axis=0)
    value = jnp.concatenate([g0_ref[0, 2], g1_ref[0, 2]], axis=0)
    pos = step * ROWS + lax.broadcasted_iota(jnp.int32, (1, ROWS), 1)
    rank = lax.broadcasted_iota(jnp.int32, (AR, ROWS), 0)
    chosen = rank // RANK == token_adapter(pos, meta)
    for a, grad in enumerate((query, value)):
        spread = jnp.where(chosen, nn(up_ref[a], grad), 0.0).astype(bf16)
        facc[a] += nn(spread, normed_ref[...])
        sacc[a] += nn(grad, inner_ref[:, a * AR : (a + 1) * AR])

    @pl.when(step == PARTS - 1)
    def _():
        for ref, a in ((keep_ref, meta[7]), (send_ref, 1 - meta[7])):
            ref[0:AR, :] = facc[a].astype(bf16)
            for c in range(D // 128):
                ref[AR : AR + SR, c * 128 : (c + 1) * 128] = sacc[a, c * SR : (c + 1) * SR, :].astype(bf16)


def adapter_grads(meta, grads, normed, inner, up):
    return pl.pallas_call(
        adapter_kernel,
        out_shape=[jax.ShapeDtypeStruct((AR + SR, D), bf16)] * 2,
        grid_spec=pltpu.PrefetchScalarGridSpec(
            num_scalar_prefetch=1,
            grid=(PARTS,),
            in_specs=[pl.BlockSpec((1, 3, PW, ROWS), lambda i, m: (i, 0, 0, 0))] * 2
            + [
                pl.BlockSpec((ROWS, D), lambda i, m: (i, 0)),
                pl.BlockSpec((ROWS, 2 * AR), lambda i, m: (i, 0)),
                pl.BlockSpec((2, AR, WIDTH), lambda i, m: (0, 0, 0)),
            ],
            out_specs=[pl.BlockSpec((AR + SR, D), lambda i, m: (0, 0))] * 2,
            scratch_shapes=[pltpu.VMEM((2, AR, D), f32), pltpu.VMEM((2, WIDTH, AR), f32)],
        ),
        compiler_params=pltpu.CompilerParams(dimension_semantics=("arbitrary",), vmem_limit_bytes=60 << 20),
        cost_estimate=pl.CostEstimate(flops=4 * TOK * D * 2 * AR, bytes_accessed=20 << 20, transcendentals=0),
        name="adapter_grads",
    )(meta, *grads, normed, inner, up)


def back_kernel(meta, b0_ref, b1_ref, w_ref, up_ref, down_ref, rows_ref, gain_ref, middle_ref, out_ref, cols, total, spread):
    step = pl.program_id(0)
    for s in range(PARTS):
        for p, ref in enumerate((b0_ref, b1_ref)):
            r = (2 * s + p) * PW
            cols[r : r + PW, :] = ref[s, 0]

    part_sum = nn(w_ref[...], cols[...])

    @pl.when(step == 0)
    def _():
        total[...] = part_sum
        spread[0] = nn(up_ref[0], cols[...])

    @pl.when(step > 0)
    def _():
        total[...] += part_sum

    @pl.when(step == 2)
    def _():
        spread[1] = nn(up_ref[1], cols[...])
        pos = meta[6] * ROWS + lax.broadcasted_iota(jnp.int32, (1, ROWS), 1)
        rank = lax.broadcasted_iota(jnp.int32, (AR, ROWS), 0)
        chosen = rank // RANK == token_adapter(pos, meta)
        both = jnp.concatenate([jnp.where(chosen, spread[a], 0.0).astype(bf16) for a in range(2)], axis=0)
        total[...] += nn(down_ref[...], both)
        gain = gain_ref[...]
        for t in range(ROWS // 128):
            own = slice(t * 128, (t + 1) * 128)
            x = rows_ref[own, :].astype(f32)
            q = lax.rsqrt(jnp.mean(x * x, axis=1, keepdims=True) + EPSILON)
            weighted = gain * total[:, own].T
            inside = jnp.mean(x * weighted, axis=1, keepdims=True)
            out_ref[own, :] = middle_ref[own, :] + (q * weighted - x * (q * q * q * inside))


def back_inputs(meta, arrived, weights, up, down, rows, gain, grad_middle):
    whole = lambda shape: pl.BlockSpec(shape, lambda i, m: (0,) * len(shape))
    return pl.pallas_call(
        back_kernel,
        out_shape=jax.ShapeDtypeStruct((ROWS, D), f32),
        grid_spec=pltpu.PrefetchScalarGridSpec(
            num_scalar_prefetch=1,
            grid=(3,),
            in_specs=[pl.BlockSpec((PARTS, 1, PW, ROWS), lambda i, m: (0, i, 0, 0))] * 2
            + [
                pl.BlockSpec((D, D), lambda i, m: (0, i)),
                whole((2, AR, D)),
                whole((D, 2 * AR)),
                whole((ROWS, D)),
                whole((1, D)),
                whole((ROWS, D)),
            ],
            out_specs=whole((ROWS, D)),
            scratch_shapes=[pltpu.VMEM((D, ROWS), bf16), pltpu.VMEM((D, ROWS), f32), pltpu.VMEM((2, AR, ROWS), f32)],
        ),
        compiler_params=pltpu.CompilerParams(dimension_semantics=("arbitrary",), vmem_limit_bytes=60 << 20),
        cost_estimate=pl.CostEstimate(flops=6 * ROWS * D * D, bytes_accessed=24 << 20, transcendentals=0),
        name="back_inputs",
    )(meta, *arrived, weights, up, down, rows, gain, grad_middle)


def assemble_kernel(meta, own_ref, other_ref, first_ref, second_ref, turned):
    part, core = meta[6], meta[7]
    for ref, a in ((own_ref, core), (other_ref, 1 - core)):
        for m in range(PARTS):
            where = part ^ m
            piece_rows = lambda n: pl.ds(pl.multiple_of(where * n, n), n)
            first_ref[a, piece_rows(SR), :] = ref[m, 0:SR, :].astype(f32)
            for c in range(D // 128):
                turned[pl.ds(pl.multiple_of(where * WIDTH + c * SR, SR), SR), :] = ref[m, SR : 2 * SR, c * 128 : (c + 1) * 128]
            rows = pl.ds(pl.multiple_of((where % 2) * 2 * SR, 2 * SR), 2 * SR)
            mlp = ref[m, 2 * SR :, :].astype(f32)

            @pl.when(a == 0)
            def _(mlp=mlp, rows=rows, where=where):
                first_ref[2 + where // 2, rows, :] = mlp

            @pl.when(a == 1)
            def _(mlp=mlp, rows=rows, where=where):
                second_ref[2 + where // 2, rows, :] = mlp

        for c in range(D // 128):
            second_ref[a, :, c * 128 : (c + 1) * 128] = turned[c * 128 : (c + 1) * 128, :].T.astype(f32)


def assemble(meta, own, other):
    whole = lambda shape: pl.BlockSpec(shape, lambda i, m: (0,) * len(shape))
    return pl.pallas_call(
        assemble_kernel,
        out_shape=[jax.ShapeDtypeStruct((4, AR, D), f32)] * 2,
        grid_spec=pltpu.PrefetchScalarGridSpec(
            num_scalar_prefetch=1,
            grid=(1,),
            in_specs=[whole((PARTS, 4 * SR, D))] * 2,
            out_specs=[whole((4, AR, D))] * 2,
            scratch_shapes=[pltpu.VMEM((D, AR), bf16)],
        ),
        compiler_params=pltpu.CompilerParams(dimension_semantics=("arbitrary",), vmem_limit_bytes=60 << 20),
        cost_estimate=pl.CostEstimate(flops=1 << 20, bytes_accessed=8 << 20, transcendentals=0),
        name="assemble",
    )(meta, own, other)


HPB = LH
BLOCKS = ROWS // B
NEG = -1e30
FW = 512
NH = 2


def fwd_kernel(bounds, q_ref, k_ref, v_ref, o_ref, lse_ref, kp, qt, vt):
    b1, b2 = bounds[0], bounds[1]
    zpad = jnp.zeros((128 - HD, 128), bf16)
    for h in range(HPB):
        own = slice(h * HD, (h + 1) * HD)
        qt[h, 0:HD, :] = q_ref[own, :]
        qt[h, HD:128, :] = jnp.zeros((128 - HD, TOK), bf16)
        vt[h, 0:HD, :] = v_ref[own, :]
        vt[h, HD:96, :] = (lax.broadcasted_iota(jnp.int32, (16, TOK), 0) == 0).astype(bf16)
        for t in range(TOK // 128):
            kt = k_ref[own, t * 128:(t + 1) * 128]
            kp[h, t * 128:(t + 1) * 128, :] = jnp.concatenate([kt, zpad], axis=0).T

    subs = o_ref.shape[2] // B
    base = 0 if subs > 1 else BLOCKS - 1

    def qblock(n, _):
        chunk, sub = n // subs, n % subs
        i = chunk * BLOCKS + base + sub
        q0 = pl.multiple_of(i * B, B)
        here = pl.ds(pl.multiple_of(sub * B, B), B)
        qpos = q0 + lax.broadcasted_iota(jnp.int32, (1, B), 1)
        srow = start_row(qpos, b1, b2)

        def step(k0, width, masked, carry):
            ks = pl.ds(k0, width)
            ss = [nn(kp[h, ks, :], qt[h, :, pl.ds(q0, B)]) for h in range(HPB)]
            if masked:
                kpos = k0 + lax.broadcasted_iota(jnp.int32, (width, B), 0)
                ok = (kpos >= srow) & (kpos <= qpos)
                ss = [jnp.where(ok, s, NEG) for s in ss]
            out = []
            for h in range(HPB):
                m, acc = carry[h]
                m_new = jnp.maximum(m, jnp.max(ss[h], axis=0, keepdims=True))
                p = jnp.exp(ss[h] - m_new).astype(bf16)
                a = jnp.exp(m - m_new)
                out.append((m_new, acc * a + nn(vt[h, :, ks], p)))
            return tuple(out)

        full = jnp.minimum(i * B // FW, PROMPT // FW)
        lo = jnp.where(i < PROMPT // B, (FW // B) * (i * B // FW), first_block(i, b1, b2))
        carry = tuple((jnp.full((1, B), NEG, f32), jnp.zeros((96, B), f32)) for _ in range(HPB))
        carry = lax.fori_loop(0, full, lambda j, c: step(pl.multiple_of(j * FW, FW), FW, False, c), carry)
        carry = lax.fori_loop(lo, i + 1, lambda j, c: step(pl.multiple_of(j * B, B), B, True, c), carry)
        for h in range(HPB):
            m, acc = carry[h]
            l = acc[HD:HD + 1, :]
            o_ref[chunk, h * HD:(h + 1) * HD, here] = (acc[0:HD, :] / l).astype(bf16)
            lse_ref[h, chunk, :, here] = m + jnp.log(l)
        return 0
    lax.fori_loop(0, PARTS * subs, qblock, 0)

def attn_fwd(bounds, qkvt, subs):
    rows = lambda a: pl.BlockSpec((WIDTH, TOK), lambda i, b: (a, 0))
    width = subs * B
    return pl.pallas_call(
        fwd_kernel,
        out_shape=(jax.ShapeDtypeStruct((PARTS, WIDTH, width), bf16), jax.ShapeDtypeStruct((LH, PARTS, 1, width), f32)),
        grid_spec=pltpu.PrefetchScalarGridSpec(
            num_scalar_prefetch=1,
            grid=(1,),
            in_specs=[rows(0), rows(1), rows(2)],
            out_specs=[
                pl.BlockSpec((PARTS, WIDTH, width), lambda i, b: (0, 0, 0)),
                pl.BlockSpec((LH, PARTS, 1, width), lambda i, b: (0, 0, 0, 0)),
            ],
            scratch_shapes=[pltpu.VMEM((HPB, TOK, 128), bf16), pltpu.VMEM((HPB, 128, TOK), bf16), pltpu.VMEM((HPB, 96, TOK), bf16)],
        ),
        compiler_params=pltpu.CompilerParams(dimension_semantics=("arbitrary",), vmem_limit_bytes=60 << 20),
        cost_estimate=pl.CostEstimate(flops=subs * 13 * 10**9, bytes_accessed=5 << 20, transcendentals=0),
        name="attn_fwd",
    )(bounds, qkvt, qkvt, qkvt)


def parts3(x):
    hi = x.astype(bf16)
    r = x - hi.astype(f32)
    mid = r.astype(bf16)
    lo = (r - mid.astype(f32)).astype(bf16)
    return hi, mid, lo

def bwd_kernel(meta, scale_ref, q_ref, k_ref, v_ref, do_ref, o_ref, lse_ref, out_ref, kp, vp, qt, dot, dkt, dvt, dqt):
    b1, b2 = meta[0], meta[1]
    row16 = lax.broadcasted_iota(jnp.int32, (16, 128), 0)
    ones3 = (row16 < 3).astype(bf16)
    pad = jnp.zeros((32, 128), bf16)
    scale = scale_ref[...]

    def tail(x):
        hi, mid, lo = parts3(-x)
        rest = jnp.where(row16 == 1, mid.astype(f32), jnp.where(row16 == 2, lo.astype(f32), 0.0))
        return jnp.where(row16 == 0, hi.astype(f32), rest).astype(bf16)

    @pl.loop(0, 2 * PARTS)
    def _(step):
        chunk = step // 2
        for t in range(3):
            off = pl.multiple_of((step % 2) * HALF + t * 128, 128)
            sl, here = pl.ds(pl.multiple_of(chunk * ROWS + off, 128), 128), pl.ds(off, 128)
            for h in range(NH):
                own = slice(h * HD, (h + 1) * HD)
                do, o = do_ref[chunk, own, here], o_ref[chunk, own, here]
                delta = jnp.sum(do.astype(f32) * o.astype(f32), axis=0, keepdims=True)
                qt[h, :, sl] = jnp.concatenate([q_ref[own, sl], tail(lse_ref[h, chunk, :, here]), pad], axis=0)
                dot[h, :, sl] = jnp.concatenate([do, tail(delta), pad], axis=0)
                kp[h, sl, :] = jnp.concatenate([k_ref[own, sl], ones3, pad], axis=0).T
                vp[h, sl, :] = jnp.concatenate([v_ref[own, sl], ones3, pad], axis=0).T

    dkt[...] = jnp.zeros_like(dkt)
    dvt[...] = jnp.zeros_like(dvt)
    dqt[...] = jnp.zeros_like(dqt)

    def block(k0, q0, kw, qw, masked):
        k0, q0 = pl.multiple_of(k0, B), pl.multiple_of(q0, B)
        ks, qs = pl.ds(k0, kw), pl.ds(q0, qw)
        if masked:
            qpos = q0 + lax.broadcasted_iota(jnp.int32, (1, qw), 1)
            kpos = k0 + lax.broadcasted_iota(jnp.int32, (kw, qw), 0)
            ok = (kpos >= start_row(qpos, b1, b2)) & (kpos <= qpos)
        for h in range(NH):
            p = jnp.exp(nn(kp[h, ks, :], qt[h, :, qs]))
            if masked:
                p = jnp.where(ok, p, 0.0)
            ds = (p * nn(vp[h, ks, :], dot[h, :, qs])).astype(bf16)
            dvt[h, :, ks] += nt(dot[h, 0:HD, qs], p.astype(bf16))
            dkt[h, :, ks] += nt(qt[h, 0:HD, qs], ds)
            dqt[h, :, qs] += nn(k_ref[h * HD : (h + 1) * HD, ks], ds)

    @pl.loop(0, 12)
    def _(n):
        qb = jnp.where(n < 9, 3 + n // 3, jnp.where(n == 9, 1, 2))
        kb = jnp.where(n < 9, n % 3, jnp.where(n == 11, 1, 0))
        block(kb * FW, qb * FW, FW, FW, False)

    @pl.loop(0, TOK // FW)
    def _(i):
        lo = jnp.where(i < PROMPT // FW, i, first_block(i * (FW // B), b1, b2) * B // FW)

        @pl.loop(lo, i + 1)
        def _(j):
            block(j * FW, i * FW, FW, FW, True)

    @pl.loop(0, 2 * PARTS)
    def _(step):
        chunk = step // 2
        off = pl.multiple_of((step % 2) * HALF, 128)
        sl, here = pl.ds(pl.multiple_of(chunk * ROWS + off, 128), HALF), pl.ds(off, HALF)
        for h in range(NH):
            own = slice(h * HD, (h + 1) * HD)
            dq = dqt[h, :, sl].astype(bf16).astype(f32) * scale
            out_ref[chunk, 0, own, here] = dq.astype(bf16)
            out_ref[chunk, 1, own, here] = dkt[h, :, sl].astype(bf16)
            out_ref[chunk, 2, own, here] = dvt[h, :, sl].astype(bf16)


def attn_bwd(meta, scale, qkvt, grad, mixture, logsum, pair):
    steps = PH // NH
    rows = lambda a: pl.BlockSpec((NH * HD, TOK), lambda i, b: (steps * (2 * a + pair) + i, 0))
    return pl.pallas_call(
        bwd_kernel,
        out_shape=jax.ShapeDtypeStruct((PARTS, 3, PW, ROWS), bf16),
        grid_spec=pltpu.PrefetchScalarGridSpec(
            num_scalar_prefetch=1,
            grid=(steps,),
            in_specs=[
                pl.BlockSpec((HD, 1), lambda i, b: (0, 0)),
                rows(0),
                rows(1),
                rows(2),
                pl.BlockSpec((PARTS, NH * HD, ROWS), lambda i, b: (0, i, 0)),
                pl.BlockSpec((PARTS, NH * HD, ROWS), lambda i, b: (0, steps * pair + i, 0)),
                pl.BlockSpec((NH, PARTS, 1, ROWS), lambda i, b: (steps * pair + i, 0, 0, 0)),
            ],
            out_specs=pl.BlockSpec((PARTS, 3, NH * HD, ROWS), lambda i, b: (0, 0, i, 0)),
            scratch_shapes=[pltpu.VMEM((NH, TOK, 128), bf16)] * 2
            + [pltpu.VMEM((NH, 128, TOK), bf16)] * 2
            + [pltpu.VMEM((NH, HD, TOK), f32)] * 3,
        ),
        compiler_params=pltpu.CompilerParams(dimension_semantics=("arbitrary",), vmem_limit_bytes=60 << 20),
        cost_estimate=pl.CostEstimate(flops=36 * 10**9, bytes_accessed=16 << 20, transcendentals=0),
        name="attn_bwd",
    )(meta, scale, qkvt, qkvt, qkvt, grad, mixture, logsum)


def mlp_kernel(meta, head_ref, tail_ref, rows_ref, cot_ref, gain_ref, out_ref, up_ref, down_ref, fd_ref, fu_ref,
               hidden_ref, inner_ref, middle_ref, grad_ref, g0_ref, g1_ref, terms_ref, mixed, sums):
    step = pl.program_id(0)

    @pl.when(step == 0)
    def _():
        sums[...] = jnp.zeros_like(sums)

    @pl.when(step < 2)
    def _():
        mixed[...] = head_ref[...]

    @pl.when(step == 2)
    def _():
        mixed[...] = tail_ref[...]

    pos = meta[6] * ROWS + step * B + lax.broadcasted_iota(jnp.int32, (B, AR), 0)
    chosen = lax.broadcasted_iota(jnp.int32, (B, AR), 1) // RANK == token_adapter(pos, meta)
    choose = lambda x: jnp.where(chosen, x, 0.0).astype(bf16)
    gain = gain_ref[...]

    middle = rows_ref[...].astype(f32) + nn(mixed[...].T, out_ref[...])
    middle_ref[...] = middle
    q = lax.rsqrt(jnp.mean(middle * middle, axis=1, keepdims=True) + EPSILON)
    normed = (middle * q * gain).astype(bf16)
    inner_up = choose(nn(normed, fd_ref[0]))
    before = nn(normed, up_ref[...]) + nn(inner_up, fu_ref[0])
    gate = jax.nn.sigmoid(before)
    hidden = (before * gate).astype(bf16)
    hidden_ref[...] = hidden
    inner_down = choose(nn(hidden, fd_ref[1]))
    inner_ref[...] = inner_down

    after = cot_ref[...]
    spread_down = choose(nt(after, fu_ref[1]))
    grad_hidden = nt(after, down_ref[...]) + nt(spread_down, fd_ref[1])
    grad_before = (grad_hidden * gate * (1.0 + before * (1.0 - gate))).astype(bf16)
    spread_up = choose(nt(grad_before, fu_ref[0]))
    weighted = gain * (nt(grad_before, up_ref[...]) + nt(spread_up, fd_ref[0]))
    middle = middle_ref[...]
    inside = jnp.mean(middle * weighted, axis=1, keepdims=True)
    grad_middle = after.astype(f32) + (q * weighted - middle * (q * q * q * inside))
    grad_ref[...] = grad_middle
    grad_mixed = nt(out_ref[...], grad_middle.astype(bf16)).astype(bf16)
    for s in range(PARTS):
        g0_ref[s] = grad_mixed[2 * s * PW : (2 * s + 1) * PW]
        g1_ref[s] = grad_mixed[(2 * s + 1) * PW : (2 * s + 2) * PW]

    for n, (a, b) in enumerate(((spread_up, normed), (spread_down, hidden), (inner_up, grad_before), (inner_down, after))):
        sums[n] += nn(a.T, b)

    @pl.when(step == 2)
    def _():
        for n in range(4):
            terms_ref[n * AR : (n + 1) * AR, :] = sums[n].astype(bf16)


def mlp(meta, mixed_head, mixed_tail, rows, cotangent, gain, w_out, w_up, w_down, flat_down, flat_up):
    whole = lambda shape: pl.BlockSpec(shape, lambda i, m: (0,) * len(shape))
    block = pl.BlockSpec((B, D), lambda i, m: (i, 0))
    pair = pl.BlockSpec((PARTS, PW, B), lambda i, m: (0, 0, i))
    return pl.pallas_call(
        mlp_kernel,
        out_shape=[
            jax.ShapeDtypeStruct((ROWS, D), bf16),
            jax.ShapeDtypeStruct((ROWS, AR), bf16),
            jax.ShapeDtypeStruct((ROWS, D), f32),
            jax.ShapeDtypeStruct((ROWS, D), f32),
            jax.ShapeDtypeStruct((PARTS, PW, ROWS), bf16),
            jax.ShapeDtypeStruct((PARTS, PW, ROWS), bf16),
            jax.ShapeDtypeStruct((4 * AR, D), bf16),
        ],
        grid_spec=pltpu.PrefetchScalarGridSpec(
            num_scalar_prefetch=1,
            grid=(ROWS // B,),
            in_specs=[
                pl.BlockSpec((D, B), lambda i, m: (0, jnp.minimum(i, 1))),
                whole((D, B)),
                block,
                block,
                whole((1, D)),
                whole((D, D)),
                whole((D, D)),
                whole((D, D)),
                whole((2, D, AR)),
                whole((2, AR, D)),
            ],
            out_specs=[block, pl.BlockSpec((B, AR), lambda i, m: (i, 0)), block, block, pair, pair, whole((4 * AR, D))],
            scratch_shapes=[pltpu.VMEM((D, B), bf16), pltpu.VMEM((4, AR, D), f32)],
        ),
        compiler_params=pltpu.CompilerParams(dimension_semantics=("arbitrary",), vmem_limit_bytes=60 << 20),
        cost_estimate=pl.CostEstimate(flops=17 * 10**9, bytes_accessed=32 << 20, transcendentals=0),
        name="mlp",
    )(meta, mixed_head, mixed_tail, rows, cotangent, gain, w_out, w_up, w_down, flat_down, flat_up)


def exchange(value):
    return lax.all_to_all(value, "heads", split_axis=0, concat_axis=0, tiled=True)


def swap(value, axis, mask):
    count = lax.axis_size(axis)
    return lax.ppermute(value, axis, [(i, i ^ mask) for i in range(count)])


def piece(value, index, count):
    rows = value.shape[-2] // count
    return lax.dynamic_slice_in_dim(value, index * rows, rows, axis=value.ndim - 2)


def sum_low(*terms):
    total = terms[0].astype(f32)
    for term in terms[1:]:
        total = total + term.astype(f32)
    return total.astype(bf16)


def far_bits():
    bits = [2]
    while bits[-1] * 2 < lax.axis_size("fsdp"):
        bits.append(bits[-1] * 2)
    return bits


def sum_far(value):
    bits = far_bits()
    for bit, twice in zip(bits[0::2], bits[1::2]):
        value = sum_low(value, *[swap(value, "fsdp", m) for m in (bit, twice, bit | twice)])
    if len(bits) % 2:
        value = sum_low(value, swap(value, "fsdp", bits[-1]))
    return value


def scatter_near(value):
    core = lax.axis_index("fsdp") & 1
    return sum_low(piece(value, core, 2), swap(piece(value, 1 - core, 2), "fsdp", 1))


def scatter_heads(value):
    part = lax.axis_index("heads")
    terms = [swap(piece(value, part ^ m, PARTS), "heads", m) for m in (1, 2, 3)]
    return sum_low(piece(value, part, PARTS), *terms)


def body(
    inputs,
    cotangent,
    lengths,
    adapter_ids,
    query_weight,
    key_weight,
    value_weight,
    out_weight,
    up_weight,
    down_weight,
    attn_gain,
    mlp_gain,
    query_scale,
    adapter_in,
    adapter_out,
):
    part = lax.axis_index("heads")
    rows = inputs[0]
    low, high = rows[:HALF], rows[HALF:]
    near_high = swap(high, "heads", 1)
    far_low = swap(low, "heads", 2)
    ends = PROMPT + jnp.cumsum(lengths[0])
    bounds = ends[:2].astype(jnp.int32)
    ids = adapter_ids[0]
    core = lax.axis_index("fsdp") & 1
    meta = jnp.concatenate([bounds, ids, jnp.stack([part, core]).astype(jnp.int32)])
    flat_down = jnp.transpose(adapter_in, (0, 2, 1, 3)).reshape(4, D, AR)
    flat_up = adapter_out.reshape(4, AR, D)
    gain_attn = attn_gain.astype(f32)
    gain_mlp = mlp_gain.astype(f32)

    def mine(weight):
        return lax.dynamic_slice_in_dim(weight, part * WIDTH, WIDTH, axis=1)

    weights_mine = jnp.concatenate([mine(query_weight), mine(key_weight), mine(value_weight)], axis=1)
    weights_mine = lax.all_gather(weights_mine, "fsdp", axis=0, tiled=True)
    w_out = lax.all_gather(out_weight, "fsdp", axis=0, tiled=True)
    w_up = lax.all_gather(up_weight, "fsdp", axis=0, tiled=True)
    w_down = lax.all_gather(down_weight, "fsdp", axis=0, tiled=True)
    weights_all = lax.all_gather(jnp.concatenate([query_weight, key_weight, value_weight], axis=1), "fsdp", axis=0, tiled=True)

    down_pair = jnp.concatenate([flat_down[0], flat_down[1]], axis=1)
    up_mine = lax.dynamic_slice_in_dim(flat_up[:2], part * WIDTH, WIDTH, axis=2)
    low_late, high_late, down_pair = lax.optimization_barrier((low, high, down_pair))
    near_low = swap(low_late, "heads", 1)
    far_high = swap(high_late, "heads", 2)
    both_low = swap(far_low, "heads", 1)
    both_high = swap(near_high, "heads", 2)
    scale_row = query_scale * HD ** (-0.5)
    scale_mine = jnp.tile(scale_row, LH)[:, None]

    wt, ut = weights_mine.T, jnp.transpose(up_mine, (0, 2, 1))
    done = ()
    for m, low, high in ((0, rows, None), (1, near_low, near_high), (2, far_low, far_high), (3, both_low, both_high)):
        done = qkv_project(meta, part ^ m, low, high, gain_attn[None, :], wt, down_pair, ut, scale_mine, done)
    qkvt, normed_all, inner_all = done
    head_mix, head_log = attn_fwd(bounds, qkvt, 2)
    mixed_head = exchange(head_mix)
    later, head_log = lax.optimization_barrier((bounds, head_log))
    tail_mix, tail_log = attn_fwd(later, qkvt, 1)
    tail_sent, mixed_head = lax.optimization_barrier((tail_mix, mixed_head))
    mixed_tail = exchange(tail_sent)
    mixture = jnp.concatenate([head_mix, tail_mix], axis=2)
    logsum = jnp.concatenate([head_log, tail_log], axis=3)

    hidden_low, inner_down, middle, grad_middle, grad_first_heads, grad_second_heads, terms = mlp(
        meta, mixed_head.reshape(D, -1), mixed_tail.reshape(D, -1), rows, cotangent[0], gain_mlp[None, :],
        w_out, w_up, w_down, flat_down[2:], flat_up[2:],
    )
    grad_heads = [exchange(grad_first_heads), exchange(grad_second_heads)]

    mlp_total = scatter_near(terms)
    mlp_total, grad_heads[0] = lax.optimization_barrier((mlp_total, grad_heads[0]))
    mlp_total = scatter_heads(mlp_total)
    grad_first_pair = attn_bwd(meta, scale_row[:, None], qkvt, grad_heads[0], mixture, logsum, 0)
    mlp_total, grad_first_pair = lax.optimization_barrier((mlp_total, grad_first_pair))
    arrived = [exchange(grad_first_pair.reshape(PARTS, 3 * PW, ROWS))]
    mlp_total = sum_far(mlp_total)
    meta, _ = lax.optimization_barrier((meta, grad_first_pair))
    grad_second_pair = attn_bwd(meta, scale_row[:, None], qkvt, grad_heads[1], mixture, logsum, 1)
    mlp_total, grad_second_pair = lax.optimization_barrier((mlp_total, grad_second_pair))
    arrived.append(exchange(grad_second_pair.reshape(PARTS, 3 * PW, ROWS)))

    meta, arrived[0] = lax.optimization_barrier((meta, arrived[0]))
    keep, send = adapter_grads(meta, [grad_first_pair, grad_second_pair], normed_all, inner_all, up_mine)
    hidden_late, inner_late, keep = lax.optimization_barrier((hidden_low, inner_down, keep))
    outputs = (middle + (nn(hidden_late, w_down) + nn(inner_late, flat_up[3]))).astype(bf16)
    total = sum_low(keep, swap(send, "fsdp", 1))
    total = jnp.concatenate([scatter_heads(total[:AR]), total[AR:]])
    total, arrived, outputs = lax.optimization_barrier((total, arrived, outputs))
    total = sum_far(total)
    meta, total = lax.optimization_barrier((meta, total))
    own = jnp.concatenate([total, mlp_total])
    pieces = [own] + [swap(own, "heads", m) for m in (1, 2, 3)]
    arrived = [a.reshape(PARTS, 3, PW, ROWS) for a in arrived]
    grad_inputs = back_inputs(meta, arrived, weights_all, flat_up[:2], down_pair, rows, gain_attn[None, :], grad_middle)
    pieces, grad_inputs = lax.optimization_barrier((pieces, grad_inputs))
    own = jnp.stack(pieces)
    grad_first, grad_second = assemble(meta, own, swap(own, "fsdp", 1))
    grad_first = jnp.transpose(grad_first.reshape(4, ADAPTERS, RANK, D), (0, 1, 3, 2))
    grad_second = grad_second.reshape(4, ADAPTERS, RANK, D)
    return (outputs[None], grad_inputs[None], grad_first, grad_second)


def solution(mesh):
    placed = (
        P("fsdp", "heads", None),
        P("fsdp", "heads", None),
        P("fsdp", None),
        P("fsdp", None),
        P("fsdp", None),
        P("fsdp", None),
        P("fsdp", None),
        P("fsdp", None),
        P("fsdp", None),
        P("fsdp", None),
        P(),
        P(),
        P(),
        P(),
        P(),
    )
    return jax.shard_map(
        body,
        mesh=mesh,
        in_specs=placed,
        out_specs=(P("fsdp", "heads", None), P("fsdp", "heads", None), P(), P()),
        check_vma=False,
    )
```

profile of v0, /device:TPU:9, one launch (start us, length us, event | category | flops | bytes accessed | tf_op | source)
XLA Modules:
  0.0 420.0 jit_solution(12223018591179776343)
XLA Ops:
  24.0 13.8 %collective-permute-done.low_ref = bf16[384,1280]{1,0:T(8,128)(2,1)} collective-permute-done((bf16[384,1280]{1,0:T(8,128)(2,1)}, bf16[384,1280]{1,0:T(8,128)(2,1)}, u32[]{:S(2)}, u32[]{:S(2)}) %collective-permute-start) | collective-permute-done | bytes 983072 | tf_op jit(solution)/shard_map/ppermute | solution.py:564
  40.0 5.3 %all-gather.6.cloned.1.call-done = bf16[1280,960]{1,0:T(8,128)(2,1)} async-done(((bf16[160,960]{1,0:T(8,128)(2,1)}), bf16[1280,960]{1,0:T(8,128)(2,1)}) %all-gather.6.cloned.1.call-update) | async-done | bytes 2457616 | tf_op jit(solution)/shard_map/all_gather | solution.py:642
  45.3 4.3 %copy.56 = bf16[1280,960]{0,1:T(8,128)(2,1)} copy(bf16[1280,960]{1,0:T(8,128)(2,1)} %all-gather.6.cloned.1.call-done) | data formatting | bytes 4915200 | tf_op jit(solution)/shard_map/all_gather | solution.py:642
  49.6 8.0 %qkv_project.4 = (bf16[960,3072]{1,0:T(8,128)(2,1)}, bf16[3072,1280]{1,0:T(8,128)(2,1)}, bf16[3072,256]{1,0:T(8,128)(2,1)}) custom-call(s32[8]{0:T(128)} %pad_add_fusion.meta, s32[1]{0:T(128)} %bitcast.16.first, bf16[768,1280]{1,0:T(8,128)(2,1)} %bitcast.58, bf16[768,1280]{1,0:T(8,128)(2,1)} %bitcast.59, f32[1,1280]{1,0:T(1,128)} %reshape.83.gain_ref, ...), custom_call_target="tpu_custom_call" | custom-call | flops 2390753280 | bytes 8388608 | tf_op jit(solution)/shard_map/qkv_project/pallas_call | solution.py:84
  58.0 8.1 %qkv_project.5 = (bf16[960,3072]{1,0:T(8,128)(2,1)}, bf16[3072,1280]{1,0:T(8,128)(2,1)}, bf16[3072,256]{1,0:T(8,128)(2,1)}) custom-call(s32[8]{0:T(128)} %pad_add_fusion.meta, s32[1]{0:T(128)} %bitcast.15.first, bf16[384,1280]{1,0:T(8,128)(2,1)} %collective-permute-done.5.low_ref, ...), custom_call_target="tpu_custom_call", output_to_operand_aliasing={{0}: (9, {}), {1}: (10, {}), {2}: (11, {})} | custom-call | flops 2390753280 | bytes 8388608 | tf_op jit(solution)/shard_map/qkv_project/pallas_call | solution.py:84
  67.0 8.0 %qkv_project.6 = (bf16[960,3072]{1,0:T(8,128)(2,1)}, bf16[3072,1280]{1,0:T(8,128)(2,1)}, bf16[3072,256]{1,0:T(8,128)(2,1)}) custom-call(s32[8]{0:T(128)} %pad_add_fusion.meta, s32[1]{0:T(128)} %bitcast.14.first, bf16[384,1280]{1,0:T(8,128)(2,1)} %collective-permute-done.low_ref, ...), custom_call_target="tpu_custom_call", output_to_operand_aliasing={{0}: (9, {}), {1}: (10, {}), {2}: (11, {})} | custom-call | flops 2390753280 | bytes 8388608 | tf_op jit(solution)/shard_map/qkv_project/pallas_call | solution.py:84
  75.0 4.0 collective-permute-done.1.low_ref
  80.0 8.0 %qkv_project.7 = (bf16[960,3072]{1,0:T(8,128)(2,1)}, bf16[3072,1280]{1,0:T(8,128)(2,1)}, bf16[3072,256]{1,0:T(8,128)(2,1)}) custom-call(s32[8]{0:T(128)} %pad_add_fusion.meta, s32[1]{0:T(128)} %bitcast.5.first, bf16[384,1280]{1,0:T(8,128)(2,1)} %collective-permute-done.1.low_ref, ...), custom_call_target="tpu_custom_call", output_to_operand_aliasing={{0}: (9, {}), {1}: (10, {}), {2}: (11, {})} | custom-call | flops 2390753280 | bytes 8388608 | tf_op jit(solution)/shard_map/qkv_project/pallas_call | solution.py:84
  88.0 31.0 %attn_fwd.2 = (bf16[4,320,512]{2,1,0:T(8,128)(2,1)}, f32[4,4,1,512]{3,2,1,0:T(1,128)}) custom-call(s32[2]{0:T(128)} %copy-done.25, bf16[960,3072]{1,0:T(8,128)(2,1)} %get-tuple-element.73.q_ref.k_ref.v_ref, bf16[960,3072]{1,0:T(8,128)(2,1)} %get-tuple-element.73.q_ref.k_ref.v_ref, bf16[960,3072]{1,0:T(8,128)(2,1)} %get-tuple-element.73.q_ref.k_ref.v_ref), custom_call_target="tpu_custom_call" | custom-call | flops 25999998976 | bytes 5242880 | tf_op jit(solution)/shard_map/attn_fwd/pallas_call | solution.py:333
  118.9 3.7 all-to-all-start
  122.7 20.3 %attn_fwd.3 = (bf16[4,320,256]{2,1,0:T(8,128)(2,1)}, f32[4,4,1,256]{3,2,1,0:T(1,128)}) custom-call(s32[2]{0:T(128)} %copy-done.25, bf16[960,3072]{1,0:T(8,128)(2,1)} %get-tuple-element.73.q_ref.k_ref.v_ref, bf16[960,3072]{1,0:T(8,128)(2,1)} %get-tuple-element.73.q_ref.k_ref.v_ref, bf16[960,3072]{1,0:T(8,128)(2,1)} %get-tuple-element.73.q_ref.k_ref.v_ref), custom_call_target="tpu_custom_call" | custom-call | flops 12999999488 | bytes 5242880 | tf_op jit(solution)/shard_map/attn_fwd/pallas_call | solution.py:333
  144.0 4.2 all-to-all-start.1
  151.0 13.5 %all-gather.8.cloned.1.call-done.out_ref = bf16[1280,1280]{1,0:T(8,128)(2,1)} async-done(((bf16[160,1280]{1,0:T(8,128)(2,1)}), bf16[1280,1280]{1,0:T(8,128)(2,1)}) %all-gather.8.cloned.1.call-update) | async-done | bytes 3276816 | tf_op jit(solution)/shard_map/all_gather | solution.py:643
  164.6 37.5 %mlp.1 = (bf16[768,1280]{1,0:T(8,128)(2,1)}, bf16[768,128]{1,0:T(8,128)(2,1)}, f32[768,1280]{1,0:T(8,128)}, f32[768,1280]{1,0:T(8,128)}, bf16[4,160,768]{2,1,0:T...) custom-call(s32[8]{0:T(128)} %pad_add_fusion.meta, bf16[1280,512]{1,0:T(8,128)(2,1)} %bitcast.69, ...), custom_call_target="tpu_custom_call" | custom-call | flops 16999999488 | bytes 33554432 | tf_op jit(solution)/shard_map/mlp/pallas_call | solution.py:523
  207.1 4.4 %all-to-all-start.2 = ((bf16[4,160,768]{2,1,0:T(8,128)(2,1)}), bf16[4,160,768]{2,1,0:T(8,128)(2,1)}, u32[]{:S(2)}, u32[]{:S(2)}) async-start(bf16[4,160,768]{2,1,0:T(8,128)(2,1)} %get-tuple-element.83), calls=%async_computation.2 | async-start | bytes 1966080 | tf_op jit(solution)/shard_map/all_to_all | solution.py:559
  213.7 10.7 %all-to-all-done.2.do_ref = bf16[4,160,768]{2,1,0:T(8,128)(2,1)} async-done(((bf16[4,160,768]{2,1,0:T(8,128)(2,1)}), bf16[4,160,768]{2,1,0:T(8,128)(2,1)}, u32[]{:S(2)}, u32[]{:S(2)}) %all-to-all-start.2) | async-done | bytes 983072 | tf_op jit(solution)/shard_map/all_to_all | solution.py:559
  224.4 3.7 all-to-all-start.4
  230.9 35.9 %attn_bwd.2.g0_ref = bf16[4,3,160,768]{3,2,1,0:T(8,128)(2,1)} custom-call(s32[8]{0:T(128)} %pad_add_fusion.meta, f32[80,1]{1,0:T(8,128)} %copy.68.scale_ref, bf16[960,3072]{1,0:T(8,128)(2,1)} %get-tuple-element.73.q_ref.k_ref.v_ref, bf16[960,3072]{1,0:T(8,128)(2,1)} %get-tuple-element.73.q_ref.k_ref.v_ref, ...), custom_call_target="tpu_custom_call" | custom-call | flops 35999997952 | bytes 16777216 | tf_op jit(solution)/shard_map/attn_bwd/pallas_call | solution.py:436
  267.0 4.5 %collective-permute-start.10 = (bf16[64,1280]{1,0:T(8,128)(2,1)S(1)}, bf16[64,1280]{1,0:T(8,128)(2,1)S(1)}, u32[]{:S(2)}, u32[]{:S(2)}) collective-permute-start(bf16[64,1280]{1,0:T(8,128)(2,1)S(1)} %add_convert_fusion.4), channel_id=1, source_target_pairs={{0,2},{1,3},{2,0},{3,1},{4,6},{5,7},{6,4},{7,5},{8,10},{9,11},{10,... | collective-permute-start | bytes 491528 | tf_op jit(solution)/shard_map/ppermute | solution.py:564
  273.7 3.7 all-to-all-start.3
  277.4 36.0 %attn_bwd.3.g1_ref = bf16[4,3,160,768]{3,2,1,0:T(8,128)(2,1)} custom-call(s32[8]{0:T(128)} %pad_add_fusion.meta, f32[80,1]{1,0:T(8,128)} %copy.68.scale_ref, bf16[960,3072]{1,0:T(8,128)(2,1)} %get-tuple-element.73.q_ref.k_ref.v_ref, bf16[960,3072]{1,0:T(8,128)(2,1)} %get-tuple-element.73.q_ref.k_ref.v_ref, ...), custom_call_target="tpu_custom_call" | custom-call | flops 35999997952 | bytes 16777216 | tf_op jit(solution)/shard_map/attn_bwd/pallas_call | solution.py:436
  316.8 4.9 %all-to-all-start.5 = ((bf16[4,480,768]{2,1,0:T(8,128)(2,1)}), bf16[4,480,768]{2,1,0:T(8,128)(2,1)}, u32[]{:S(2)}, u32[]{:S(2)}) async-start(bf16[4,480,768]{2,1,0:T(8,128)(2,1)} %bitcast.52), calls=%async_computation.5 | async-start | bytes 5898240 | tf_op jit(solution)/shard_map/all_to_all | solution.py:559
  321.7 10.5 %adapter_grads.1 = (bf16[160,1280]{1,0:T(8,128)(2,1)}, bf16[160,1280]{1,0:T(8,128)(2,1)}) custom-call(s32[8]{0:T(128)} %pad_add_fusion.meta, bf16[4,3,160,768]{3,2,1,0:T(8,128)(2,1)} %attn_bwd.2.g0_ref, bf16[4,3,160,768]{3,2,1,0:T(8,128)(2,1)} %attn_bwd.3.g1_ref, bf16[3072,1280]{1,0:T(8,128)(2,1)} %get-tuple-element.94.normed_ref, ...), custom_call_target="tpu_custom_call" | custom-call | flops 4026531840 | bytes 20971520 | tf_op jit(solution)/shard_map/adapter_grads/pallas_call | solution.py:145
  332.4 4.4 %fusion.5 = f32[768,1280]{1,0:T(8,128)S(1)} fusion(bf16[768,1280]{1,0:T(8,128)(2,1)} %get-tuple-element.101, bf16[1280,1280]{1,0:T(8,128)(2,1)S(1)} %copy-done.26), kind=kOutput, calls=%fused_computation.40 | convolution fusion | flops 2516582400 | bytes 9175040 | tf_op jit(solution)/shard_map/dot_general | solution.py:39
  342.0 15.3 %collective-permute-done.14 = bf16[32,1280]{1,0:T(8,128)(2,1)S(1)} collective-permute-done((bf16[32,1280]{1,0:T(8,128)(2,1)S(1)}, bf16[32,1280]{1,0:T(8,128)(2,1)S(1)}, u32[]{:S(2)}, u32[]{:S(2)}) %collective-permute-start.14) | collective-permute-done | bytes 81952 | tf_op jit(solution)/shard_map/ppermute | solution.py:564
  360.0 3.1 collective-permute-start.17
  364.4 3.5 collective-permute-done.17
  367.9 3.5 collective-permute-done.18
  371.4 8.2 %collective-permute-done.19 = bf16[64,1280]{1,0:T(8,128)(2,1)S(1)} collective-permute-done((bf16[64,1280]{1,0:T(8,128)(2,1)S(1)}, bf16[64,1280]{1,0:T(8,128)(2,1)S(1)}, u32[]{:S(2)}, u32[]{:S(2)}) %collective-permute-start.19) | collective-permute-done | bytes 163872 | tf_op jit(solution)/shard_map/ppermute | solution.py:564
  382.4 20.0 %back_inputs.1 = f32[768,1280]{1,0:T(8,128)} custom-call(s32[8]{0:T(128)} %pad_add_fusion.meta, bf16[4,3,160,768]{3,2,1,0:T(8,128)(2,1)} %bitcast.54, bf16[4,3,160,768]{3,2,1,0:T(8,128)(2,1)} %bitcast.29.b1_ref, bf16[1280,3840]{1,0:T(8,128)(2,1)} %all-gather.14.cloned.1.call-done.w_ref, bf16[2,128,1280]{2,1,0:T(8,128)(2,1)} %bitcast.64, ...), custom_call_target="tpu_custom_call" | custom-call | flops 7549747200 | bytes 25165824 | tf_op jit(solution)/shard_map/back_inputs/pallas_call | solution.py:204
  404.0 2.7 collective-permute-done.23.other_ref
  407.8 5.3 %assemble.1 = (f32[4,128,1280]{2,1,0:T(8,128)}, f32[4,128,1280]{2,1,0:T(8,128)}) custom-call(s32[8]{0:T(128)} %pad_add_fusion.meta, bf16[4,128,1280]{2,1,0:T(8,128)(2,1)} %copy-done.1, bf16[4,128,1280]{2,1,0:T(8,128)(2,1)} %copy-done.11), custom_call_target="tpu_custom_call" | custom-call | flops 1048576 | bytes 8388608 | tf_op jit(solution)/shard_map/assemble/pallas_call | solution.py:254
  (162 shorter events, 55.3 us)
Async XLA Ops:
  7.2 38.1 %all-gather.6.cloned.1.call-start = ((), (), s32[]{:S(2)}) async-start(), calls=%async_computation.6 | async-start | bytes 2949120 | tf_op jit(solution)/shard_map/all_gather | solution.py:642
  10.4 140.6 %all-gather.12.cloned.1.call-start = ((), (), s32[]{:S(2)}) async-start(), calls=%async_computation.9 | async-start | bytes 3686400 | tf_op jit(solution)/shard_map/all_gather | solution.py:645
  11.2 139.9 %all-gather.10.cloned.1.call-start = ((), (), s32[]{:S(2)}) async-start(), calls=%async_computation.8 | async-start | bytes 3686400 | tf_op jit(solution)/shard_map/all_gather | solution.py:644
  11.9 152.7 %all-gather.8.cloned.1.call-start = ((), (), s32[]{:S(2)}) async-start(), calls=%async_computation.7 | async-start | bytes 3686400 | tf_op jit(solution)/shard_map/all_gather | solution.py:643
  12.5 370.0 %all-gather.14.cloned.1.call-start = ((), (), s32[]{:S(2)}) async-start(), calls=%async_computation.10 | async-start | bytes 11059200 | tf_op jit(solution)/shard_map/all_gather | solution.py:646
  13.9 24.1 %collective-permute-start.2 = (bf16[384,1280]{1,0:T(8,128)(2,1)}, bf16[384,1280]{1,0:T(8,128)(2,1)}, u32[]{:S(2)}, u32[]{:S(2)}) collective-permute-start(bf16[384,1280]{1,0:T(8,128)(2,1)} %get-tuple-element.62), channel_id=1, source_target_pairs={{0,8},{8,0},{16,24},{24,16},{1,9},{9,1},{17,25},{25,17},{2,10},{10... | collective-permute-start | bytes 2949128 | tf_op jit(solution)/shard_map/ppermute | solution.py:564
  15.1 22.7 %collective-permute-start = (bf16[384,1280]{1,0:T(8,128)(2,1)}, bf16[384,1280]{1,0:T(8,128)(2,1)}, u32[]{:S(2)}, u32[]{:S(2)}) collective-permute-start(bf16[384,1280]{1,0:T(8,128)(2,1)} %get-tuple-element.63), channel_id=1, source_target_pairs={{0,16},{8,24},{16,0},{24,8},{1,17},{9,25},{17,1},{25,9},{2,18},{10... | collective-permute-start | bytes 2949128 | tf_op jit(solution)/shard_map/ppermute | solution.py:564
  17.7 40.2 %collective-permute-start.5 = (bf16[384,1280]{1,0:T(8,128)(2,1)}, bf16[384,1280]{1,0:T(8,128)(2,1)}, u32[]{:S(2)}, u32[]{:S(2)}) collective-permute-start(bf16[384,1280]{1,0:T(8,128)(2,1)} %get-tuple-element.63), channel_id=1, source_target_pairs={{0,8},{8,0},{16,24},{24,16},{1,9},{9,1},{17,25},{25,17},{2,10},{10... | collective-permute-start | bytes 2949128 | tf_op jit(solution)/shard_map/ppermute | solution.py:564
  18.1 48.0 %collective-permute-start.4 = (bf16[384,1280]{1,0:T(8,128)(2,1)}, bf16[384,1280]{1,0:T(8,128)(2,1)S(1)}, u32[]{:S(2)}, u32[]{:S(2)}) collective-permute-start(bf16[384,1280]{1,0:T(8,128)(2,1)} %get-tuple-element.62), channel_id=1, source_target_pairs={{0,16},{8,24},{16,0},{24,8},{1,17},{9,25},{17,1},{25,9},{2,18},{10... | collective-permute-start | bytes 2949128 | tf_op jit(solution)/shard_map/ppermute | solution.py:564
  37.8 41.2 %collective-permute-start.1 = (bf16[384,1280]{1,0:T(8,128)(2,1)}, bf16[384,1280]{1,0:T(8,128)(2,1)}, u32[]{:S(2)}, u32[]{:S(2)}) collective-permute-start(bf16[384,1280]{1,0:T(8,128)(2,1)} %collective-permute-done.low_ref), channel_id=1, source_target_pairs={{0,8},{8,0},{16,24},{24,16},{1,9},{9,1},{17,25},{25,17},{2,10},{10... | collective-permute-start | bytes 2949128 | tf_op jit(solution)/shard_map/ppermute | solution.py:564
  38.1 41.9 %collective-permute-start.3 = (bf16[384,1280]{1,0:T(8,128)(2,1)}, bf16[384,1280]{1,0:T(8,128)(2,1)}, u32[]{:S(2)}, u32[]{:S(2)}) collective-permute-start(bf16[384,1280]{1,0:T(8,128)(2,1)} %collective-permute-done.2.high_ref), channel_id=1, source_target_pairs={{0,16},{8,24},{16,0},{24,8},{1,17},{9,25},{17,1},{25,9},{2,18},{10... | collective-permute-start | bytes 2949128 | tf_op jit(solution)/shard_map/ppermute | solution.py:564
  118.9 24.0 %all-to-all-start = ((bf16[4,320,512]{2,1,0:T(8,128)(2,1)}), bf16[4,320,512]{2,1,0:T(8,128)(2,1)S(1)}, u32[]{:S(2)}, u32[]{:S(2)}) async-start(bf16[4,320,512]{2,1,0:T(8,128)(2,1)} %get-tuple-element.77), calls=%async_computation | async-start | bytes 2621440 | tf_op jit(solution)/shard_map/all_to_all | solution.py:559
  144.0 20.5 %all-to-all-start.1 = ((bf16[4,320,256]{2,1,0:T(8,128)(2,1)}), bf16[4,320,256]{2,1,0:T(8,128)(2,1)}, u32[]{:S(2)}, u32[]{:S(2)}) async-start(bf16[4,320,256]{2,1,0:T(8,128)(2,1)} %get-tuple-element.79), calls=%async_computation.1 | async-start | bytes 1310720 | tf_op jit(solution)/shard_map/all_to_all | solution.py:559
  204.1 8.3 %collective-permute-start.6 = (bf16[256,1280]{1,0:T(8,128)(2,1)}, bf16[256,1280]{1,0:T(8,128)(2,1)}, u32[]{:S(2)}, u32[]{:S(2)}) collective-permute-start(bf16[256,1280]{1,0:T(8,128)(2,1)} %constant_dynamic-slice_fusion.6), channel_id=1, source_target_pairs={{0,1},{1,0},{2,3},{3,2},{4,5},{5,4},{6,7},{7,6},{8,9},{9,8},{10,11... | collective-permute-start | bytes 1966088 | tf_op jit(solution)/shard_map/ppermute | solution.py:564
  207.1 17.3 %all-to-all-start.2 = ((bf16[4,160,768]{2,1,0:T(8,128)(2,1)}), bf16[4,160,768]{2,1,0:T(8,128)(2,1)}, u32[]{:S(2)}, u32[]{:S(2)}) async-start(bf16[4,160,768]{2,1,0:T(8,128)(2,1)} %get-tuple-element.83), calls=%async_computation.2 | async-start | bytes 1966080 | tf_op jit(solution)/shard_map/all_to_all | solution.py:559
  224.4 48.3 %all-to-all-start.4 = ((bf16[4,160,768]{2,1,0:T(8,128)(2,1)}), bf16[4,160,768]{2,1,0:T(8,128)(2,1)S(1)}, u32[]{:S(2)}, u32[]{:S(2)}) async-start(bf16[4,160,768]{2,1,0:T(8,128)(2,1)} %get-tuple-element.92), calls=%async_computation.4 | async-start | bytes 1966080 | tf_op jit(solution)/shard_map/all_to_all | solution.py:559
  228.2 38.7 %collective-permute-start.7 = (bf16[64,1280]{1,0:T(8,128)(2,1)S(1)}, bf16[64,1280]{1,0:T(8,128)(2,1)S(1)}, u32[]{:S(2)}, u32[]{:S(2)}) collective-permute-start(bf16[64,1280]{1,0:T(8,128)(2,1)S(1)} %get-tuple-element.124), channel_id=1, source_target_pairs={{0,8},{8,0},{16,24},{24,16},{1,9},{9,1},{17,25},{25,17},{2,10},{10... | collective-permute-start | bytes 491528 | tf_op jit(solution)/shard_map/ppermute | solution.py:564
  229.7 37.2 %collective-permute-start.8 = (bf16[64,1280]{1,0:T(8,128)(2,1)S(1)}, bf16[64,1280]{1,0:T(8,128)(2,1)S(1)}, u32[]{:S(2)}, u32[]{:S(2)}) collective-permute-start(bf16[64,1280]{1,0:T(8,128)(2,1)S(1)} %get-tuple-element.126), channel_id=1, source_target_pairs={{0,16},{8,24},{16,0},{24,8},{1,17},{9,25},{17,1},{25,9},{2,18},{10... | collective-permute-start | bytes 491528 | tf_op jit(solution)/shard_map/ppermute | solution.py:564
  230.9 36.0 %collective-permute-start.9 = (bf16[64,1280]{1,0:T(8,128)(2,1)S(1)}, bf16[64,1280]{1,0:T(8,128)(2,1)S(1)}, u32[]{:S(2)}, u32[]{:S(2)}) collective-permute-start(bf16[64,1280]{1,0:T(8,128)(2,1)S(1)} %get-tuple-element.125), channel_id=1, source_target_pairs={{0,24},{8,16},{16,8},{24,0},{1,25},{9,17},{17,9},{25,1},{2,26},{10... | collective-permute-start | bytes 491528 | tf_op jit(solution)/shard_map/ppermute | solution.py:564
  267.0 46.4 %collective-permute-start.10 = (bf16[64,1280]{1,0:T(8,128)(2,1)S(1)}, bf16[64,1280]{1,0:T(8,128)(2,1)S(1)}, u32[]{:S(2)}, u32[]{:S(2)}) collective-permute-start(bf16[64,1280]{1,0:T(8,128)(2,1)S(1)} %add_convert_fusion.4), channel_id=1, source_target_pairs={{0,2},{1,3},{2,0},{3,1},{4,6},{5,7},{6,4},{7,5},{8,10},{9,11},{10,... | collective-permute-start | bytes 491528 | tf_op jit(solution)/shard_map/ppermute | solution.py:564
  271.5 41.9 %collective-permute-start.11 = (bf16[64,1280]{1,0:T(8,128)(2,1)S(1)}, bf16[64,1280]{1,0:T(8,128)(2,1)S(1)}, u32[]{:S(2)}, u32[]{:S(2)}) collective-permute-start(bf16[64,1280]{1,0:T(8,128)(2,1)S(1)} %add_convert_fusion.4), channel_id=1, source_target_pairs={{0,4},{1,5},{2,6},{3,7},{4,0},{5,1},{6,2},{7,3},{8,12},{9,13},{10,... | collective-permute-start | bytes 491528 | tf_op jit(solution)/shard_map/ppermute | solution.py:564
  272.4 41.6 %collective-permute-start.12 = (bf16[64,1280]{1,0:T(8,128)(2,1)S(1)}, bf16[64,1280]{1,0:T(8,128)(2,1)}, u32[]{:S(2)}, u32[]{:S(2)}) collective-permute-start(bf16[64,1280]{1,0:T(8,128)(2,1)S(1)} %add_convert_fusion.4), channel_id=1, source_target_pairs={{0,6},{1,7},{2,4},{3,5},{4,2},{5,3},{6,0},{7,1},{8,14},{9,15},{10,... | collective-permute-start | bytes 491528 | tf_op jit(solution)/shard_map/ppermute | solution.py:564
  273.7 41.4 %all-to-all-start.3 = ((bf16[4,480,768]{2,1,0:T(8,128)(2,1)}), bf16[4,480,768]{2,1,0:T(8,128)(2,1)S(1)}, u32[]{:S(2)}, u32[]{:S(2)}) async-start(bf16[4,480,768]{2,1,0:T(8,128)(2,1)} %bitcast.53), calls=%async_computation.3 | async-start | bytes 5898240 | tf_op jit(solution)/shard_map/all_to_all | solution.py:559
  316.8 43.2 %all-to-all-start.5 = ((bf16[4,480,768]{2,1,0:T(8,128)(2,1)}), bf16[4,480,768]{2,1,0:T(8,128)(2,1)}, u32[]{:S(2)}, u32[]{:S(2)}) async-start(bf16[4,480,768]{2,1,0:T(8,128)(2,1)} %bitcast.52), calls=%async_computation.5 | async-start | bytes 5898240 | tf_op jit(solution)/shard_map/all_to_all | solution.py:559
  337.0 20.3 %collective-permute-start.14 = (bf16[32,1280]{1,0:T(8,128)(2,1)S(1)}, bf16[32,1280]{1,0:T(8,128)(2,1)S(1)}, u32[]{:S(2)}, u32[]{:S(2)}) collective-permute-start(bf16[32,1280]{1,0:T(8,128)(2,1)S(1)} %get-tuple-element.127), channel_id=1, source_target_pairs={{0,8},{8,0},{16,24},{24,16},{1,9},{9,1},{17,25},{25,17},{2,10},{10... | collective-permute-start | bytes 245768 | tf_op jit(solution)/shard_map/ppermute | solution.py:564
  338.7 18.5 %collective-permute-start.15 = (bf16[32,1280]{1,0:T(8,128)(2,1)S(1)}, bf16[32,1280]{1,0:T(8,128)(2,1)S(1)}, u32[]{:S(2)}, u32[]{:S(2)}) collective-permute-start(bf16[32,1280]{1,0:T(8,128)(2,1)S(1)} %get-tuple-element.129), channel_id=1, source_target_pairs={{0,16},{8,24},{16,0},{24,8},{1,17},{9,25},{17,1},{25,9},{2,18},{10... | collective-permute-start | bytes 245768 | tf_op jit(solution)/shard_map/ppermute | solution.py:564
  339.9 20.0 %collective-permute-start.16 = (bf16[32,1280]{1,0:T(8,128)(2,1)S(1)}, bf16[32,1280]{1,0:T(8,128)(2,1)S(1)}, u32[]{:S(2)}, u32[]{:S(2)}) collective-permute-start(bf16[32,1280]{1,0:T(8,128)(2,1)S(1)} %get-tuple-element.128), channel_id=1, source_target_pairs={{0,24},{8,16},{16,8},{24,0},{1,25},{9,17},{17,9},{25,1},{2,26},{10... | collective-permute-start | bytes 245768 | tf_op jit(solution)/shard_map/ppermute | solution.py:564
  363.1 8.3 %collective-permute-start.18 = (bf16[64,1280]{1,0:T(8,128)(2,1)S(1)}, bf16[64,1280]{1,0:T(8,128)(2,1)S(1)}, u32[]{:S(2)}, u32[]{:S(2)}) collective-permute-start(bf16[64,1280]{1,0:T(8,128)(2,1)S(1)} %pad_maximum_fusion.4), channel_id=1, source_target_pairs={{0,4},{1,5},{2,6},{3,7},{4,0},{5,1},{6,2},{7,3},{8,12},{9,13},{10,... | collective-permute-start | bytes 491528 | tf_op jit(solution)/shard_map/ppermute | solution.py:564
  363.2 16.4 %collective-permute-start.19 = (bf16[64,1280]{1,0:T(8,128)(2,1)S(1)}, bf16[64,1280]{1,0:T(8,128)(2,1)S(1)}, u32[]{:S(2)}, u32[]{:S(2)}) collective-permute-start(bf16[64,1280]{1,0:T(8,128)(2,1)S(1)} %pad_maximum_fusion.4), channel_id=1, source_target_pairs={{0,6},{1,7},{2,4},{3,5},{4,2},{5,3},{6,0},{7,1},{8,14},{9,15},{10,... | collective-permute-start | bytes 491528 | tf_op jit(solution)/shard_map/ppermute | solution.py:564
  379.7 22.7 %collective-permute-start.20 = (bf16[128,1280]{1,0:T(8,128)(2,1)S(1)}, bf16[128,1280]{1,0:T(8,128)(2,1)S(1)}, u32[]{:S(2)}, u32[]{:S(2)}) collective-permute-start(bf16[128,1280]{1,0:T(8,128)(2,1)S(1)} %constant_dynamic-update-slice_fusion.4), channel_id=1, source_target_pairs={{0,8},{8,0},{16,24},{24,16},{1,9},{9,1},{17,25},{25,17},{2,10},{10... | collective-permute-start | bytes 983048 | tf_op jit(solution)/shard_map/ppermute | solution.py:564
  379.9 22.5 %collective-permute-start.21 = (bf16[128,1280]{1,0:T(8,128)(2,1)S(1)}, bf16[128,1280]{1,0:T(8,128)(2,1)S(1)}, u32[]{:S(2)}, u32[]{:S(2)}) collective-permute-start(bf16[128,1280]{1,0:T(8,128)(2,1)S(1)} %constant_dynamic-update-slice_fusion.4), channel_id=1, source_target_pairs={{0,16},{8,24},{16,0},{24,8},{1,17},{9,25},{17,1},{25,9},{2,18},{10... | collective-permute-start | bytes 983048 | tf_op jit(solution)/shard_map/ppermute | solution.py:564
  380.3 22.1 %collective-permute-start.22 = (bf16[128,1280]{1,0:T(8,128)(2,1)S(1)}, bf16[128,1280]{1,0:T(8,128)(2,1)S(1)}, u32[]{:S(2)}, u32[]{:S(2)}) collective-permute-start(bf16[128,1280]{1,0:T(8,128)(2,1)S(1)} %constant_dynamic-update-slice_fusion.4), channel_id=1, source_target_pairs={{0,24},{8,16},{16,8},{24,0},{1,25},{9,17},{17,9},{25,1},{2,26},{10... | collective-permute-start | bytes 983048 | tf_op jit(solution)/shard_map/ppermute | solution.py:564
  (33 other events, 336.6 us)
Sparse Core Ops, SparseCore 0:
  10.5 34.7 all-gather.5
  47.0 37.9 all-gather.11
  86.6 38.1 all-gather.9
  126.3 38.1 all-gather.7
  166.0 90.9 all-gather.13
where the time goes:
time: 428 us; the launch traced here: 420 us
  Pallas kernels  229 us (54%)
  waiting for transfers between devices  86.4 us (20%)
  starting transfers between devices  49.7 us (12%)
  local copies, waits for them, and re-layouts  26.8 us (6%)
  between operations  14.7 us (3%)
  other arithmetic  7.56 us (2%)
  matrix products  6.33 us (1%)
    pallas_call x2, Pallas kernels, attn_bwd(): pl.pallas_call(bwd_kernel, out_shape=jax.ShapeDtypeStruct((PARTS, 3, PW,...  71.9 us
    ppermute x24, waiting for transfers between devices, swap(): return lax.ppermute(value, axis, [(i, i ^ mask) for i in range(count)])  54.9 us
    pallas_call x2, Pallas kernels, attn_fwd(): pl.pallas_call(fwd_kernel, out_shape=(jax.ShapeDtypeStruct((PARTS, WIDTH,...  51.3 us
    pallas_call x1, Pallas kernels, mlp(): pl.pallas_call(mlp_kernel, out_shape=[jax.ShapeDtypeStruct((ROWS, D), bf1...  37.5 us
    pallas_call x4, Pallas kernels, qkv_project(): pl.pallas_call(qkv_kernel, out_shape=(jax.ShapeDtypeStruct((3 * WIDTH, TO...  32.2 us
    ppermute x24, starting transfers between devices, swap(): return lax.ppermute(value, axis, [(i, i ^ mask) for i in range(count)])  25 us
    all_to_all x6, starting transfers between devices, exchange(): lax.all_to_all(value, 'heads', split_axis=0, concat_axis=0, tiled=True)  24.5 us
    pallas_call x1, Pallas kernels, back_inputs(): pl.pallas_call(back_kernel, out_shape=jax.ShapeDtypeStruct((ROWS, D), f32...  20 us
  transfers between devices with their start and end apart: 35, of which 13 were waited for; matrix products, arithmetic and copies ran while one was open for 7% of the time, Pallas kernels for 53%

commit v1 on v0

--- a/solution.py
+++ b/solution.py
@@ -115,7 +115,8 @@
     )(meta, first, low, low if high is None else high, gain, wt, down, up, scale, *done)
 
 
-def adapter_kernel(meta, g0_ref, g1_ref, normed_ref, inner_ref, up_ref, keep_ref, send_ref, facc, sacc):
+def adapter_kernel(meta, *refs):
+    grad_refs, (normed_ref, inner_ref, up_ref, keep_ref, send_ref, facc, sacc) = refs[:-7], refs[-7:]
     step = pl.program_id(0)
 
     @pl.when(step == 0)
@@ -123,8 +124,8 @@
         facc[...] = jnp.zeros_like(facc)
         sacc[...] = jnp.zeros_like(sacc)
 
-    query = jnp.concatenate([g0_ref[0, 0], g1_ref[0, 0]], axis=0)
-    value = jnp.concatenate([g0_ref[0, 2], g1_ref[0, 2]], axis=0)
+    query = jnp.concatenate([ref[0, 0] for ref in grad_refs], axis=0)
+    value = jnp.concatenate([ref[0, 2] for ref in grad_refs], axis=0)
     pos = step * ROWS + lax.broadcasted_iota(jnp.int32, (1, ROWS), 1)
     rank = lax.broadcasted_iota(jnp.int32, (AR, ROWS), 0)
     chosen = rank // RANK == token_adapter(pos, meta)
@@ -148,7 +149,7 @@
         grid_spec=pltpu.PrefetchScalarGridSpec(
             num_scalar_prefetch=1,
             grid=(PARTS,),
-            in_specs=[pl.BlockSpec((1, 3, PW, ROWS), lambda i, m: (i, 0, 0, 0))] * 2
+            in_specs=[pl.BlockSpec((1,) + g.shape[1:], lambda i, m: (i, 0, 0, 0)) for g in grads]
             + [
                 pl.BlockSpec((ROWS, D), lambda i, m: (i, 0)),
                 pl.BlockSpec((ROWS, 2 * AR), lambda i, m: (i, 0)),
@@ -163,12 +164,15 @@
     )(meta, *grads, normed, inner, up)
 
 
-def back_kernel(meta, b0_ref, b1_ref, w_ref, up_ref, down_ref, rows_ref, gain_ref, middle_ref, out_ref, cols, total, spread):
+def back_kernel(meta, *refs):
+    grad_refs, rest = refs[:-10], refs[-10:]
+    w_ref, up_ref, down_ref, rows_ref, gain_ref, middle_ref, out_ref, cols, total, spread = rest
     step = pl.program_id(0)
     for s in range(PARTS):
-        for p, ref in enumerate((b0_ref, b1_ref)):
-            r = (2 * s + p) * PW
-            cols[r : r + PW, :] = ref[s, 0]
+        r = s * WIDTH
+        for ref in grad_refs:
+            cols[r : r + ref.shape[2], :] = ref[s, 0]
+            r += ref.shape[2]
 
     part_sum = nn(w_ref[...], cols[...])
 
@@ -207,7 +211,7 @@
         grid_spec=pltpu.PrefetchScalarGridSpec(
             num_scalar_prefetch=1,
             grid=(3,),
-            in_specs=[pl.BlockSpec((PARTS, 1, PW, ROWS), lambda i, m: (0, i, 0, 0))] * 2
+            in_specs=[pl.BlockSpec((PARTS, 1) + g.shape[2:], lambda i, m: (0, i, 0, 0)) for g in arrived]
             + [
                 pl.BlockSpec((D, D), lambda i, m: (0, i)),
                 whole((2, AR, D)),
@@ -271,7 +275,6 @@
 BLOCKS = ROWS // B
 NEG = -1e30
 FW = 512
-NH = 2
 
 
 def fwd_kernel(bounds, q_ref, k_ref, v_ref, o_ref, lse_ref, kp, qt, vt):
@@ -357,6 +360,7 @@
     return hi, mid, lo
 
 def bwd_kernel(meta, scale_ref, q_ref, k_ref, v_ref, do_ref, o_ref, lse_ref, out_ref, kp, vp, qt, dot, dkt, dvt, dqt):
+    NH = kp.shape[0]
     b1, b2 = meta[0], meta[1]
     row16 = lax.broadcasted_iota(jnp.int32, (16, 128), 0)
     ones3 = (row16 < 3).astype(bf16)
@@ -430,37 +434,36 @@
             out_ref[chunk, 2, own, here] = dvt[h, :, sl].astype(bf16)
 
 
-def attn_bwd(meta, scale, qkvt, grad, mixture, logsum, pair):
-    steps = PH // NH
-    rows = lambda a: pl.BlockSpec((NH * HD, TOK), lambda i, b: (steps * (2 * a + pair) + i, 0))
+def attn_bwd(meta, scale, qkvt, grad, mixture, logsum, first, count, slot):
+    rows = lambda a: pl.BlockSpec((count * HD, TOK), lambda i, b: ((LH * a + first) // count, 0))
     return pl.pallas_call(
         bwd_kernel,
-        out_shape=jax.ShapeDtypeStruct((PARTS, 3, PW, ROWS), bf16),
+        out_shape=jax.ShapeDtypeStruct((PARTS, 3, count * HD, ROWS), bf16),
         grid_spec=pltpu.PrefetchScalarGridSpec(
             num_scalar_prefetch=1,
-            grid=(steps,),
+            grid=(1,),
             in_specs=[
                 pl.BlockSpec((HD, 1), lambda i, b: (0, 0)),
                 rows(0),
                 rows(1),
                 rows(2),
-                pl.BlockSpec((PARTS, NH * HD, ROWS), lambda i, b: (0, i, 0)),
-                pl.BlockSpec((PARTS, NH * HD, ROWS), lambda i, b: (0, steps * pair + i, 0)),
-                pl.BlockSpec((NH, PARTS, 1, ROWS), lambda i, b: (steps * pair + i, 0, 0, 0)),
+                pl.BlockSpec((PARTS, count * HD, ROWS), lambda i, b: (0, slot // count, 0)),
+                pl.BlockSpec((PARTS, count * HD, ROWS), lambda i, b: (0, first // count, 0)),
+                pl.BlockSpec((count, PARTS, 1, ROWS), lambda i, b: (first // count, 0, 0, 0)),
             ],
-            out_specs=pl.BlockSpec((PARTS, 3, NH * HD, ROWS), lambda i, b: (0, 0, i, 0)),
-            scratch_shapes=[pltpu.VMEM((NH, TOK, 128), bf16)] * 2
-            + [pltpu.VMEM((NH, 128, TOK), bf16)] * 2
-            + [pltpu.VMEM((NH, HD, TOK), f32)] * 3,
+            out_specs=pl.BlockSpec((PARTS, 3, count * HD, ROWS), lambda i, b: (0, 0, 0, 0)),
+            scratch_shapes=[pltpu.VMEM((count, TOK, 128), bf16)] * 2
+            + [pltpu.VMEM((count, 128, TOK), bf16)] * 2
+            + [pltpu.VMEM((count, HD, TOK), f32)] * 3,
         ),
         compiler_params=pltpu.CompilerParams(dimension_semantics=("arbitrary",), vmem_limit_bytes=60 << 20),
-        cost_estimate=pl.CostEstimate(flops=36 * 10**9, bytes_accessed=16 << 20, transcendentals=0),
+        cost_estimate=pl.CostEstimate(flops=count * 18 * 10**9, bytes_accessed=count * 8 << 20, transcendentals=0),
         name="attn_bwd",
     )(meta, scale, qkvt, qkvt, qkvt, grad, mixture, logsum)
 
 
 def mlp_kernel(meta, head_ref, tail_ref, rows_ref, cot_ref, gain_ref, out_ref, up_ref, down_ref, fd_ref, fu_ref,
-               hidden_ref, inner_ref, middle_ref, grad_ref, g0_ref, g1_ref, terms_ref, mixed, sums):
+               hidden_ref, inner_ref, middle_ref, grad_ref, g0_ref, g1_ref, keep_ref, send_ref, mixed, sums):
     step = pl.program_id(0)
 
     @pl.when(step == 0)
@@ -512,11 +515,12 @@
 
     @pl.when(step == 2)
     def _():
-        for n in range(4):
-            terms_ref[n * AR : (n + 1) * AR, :] = sums[n].astype(bf16)
-
-
-def mlp(meta, mixed_head, mixed_tail, rows, cotangent, gain, w_out, w_up, w_down, flat_down, flat_up):
+        for ref, half in ((keep_ref, meta[7]), (send_ref, 1 - meta[7])):
+            for n in range(2):
+                ref[n * AR : (n + 1) * AR, :] = sums[2 * half + n].astype(bf16)
+
+
+def mlp(meta, mixed_head, mixed_tail, rows, cotangent, gain, weights, flat_down, flat_up):
     whole = lambda shape: pl.BlockSpec(shape, lambda i, m: (0,) * len(shape))
     block = pl.BlockSpec((B, D), lambda i, m: (i, 0))
     pair = pl.BlockSpec((PARTS, PW, B), lambda i, m: (0, 0, i))
@@ -529,7 +533,8 @@
             jax.ShapeDtypeStruct((ROWS, D), f32),
             jax.ShapeDtypeStruct((PARTS, PW, ROWS), bf16),
             jax.ShapeDtypeStruct((PARTS, PW, ROWS), bf16),
-            jax.ShapeDtypeStruct((4 * AR, D), bf16),
+            jax.ShapeDtypeStruct((2 * AR, D), bf16),
+            jax.ShapeDtypeStruct((2 * AR, D), bf16),
         ],
         grid_spec=pltpu.PrefetchScalarGridSpec(
             num_scalar_prefetch=1,
@@ -540,19 +545,17 @@
                 block,
                 block,
                 whole((1, D)),
-                whole((D, D)),
-                whole((D, D)),
-                whole((D, D)),
+                *[pl.BlockSpec((D, D), lambda i, m, a=a: (0, a)) for a in range(3)],
                 whole((2, D, AR)),
                 whole((2, AR, D)),
             ],
-            out_specs=[block, pl.BlockSpec((B, AR), lambda i, m: (i, 0)), block, block, pair, pair, whole((4 * AR, D))],
+            out_specs=[block, pl.BlockSpec((B, AR), lambda i, m: (i, 0)), block, block, pair, pair] + [whole((2 * AR, D))] * 2,
             scratch_shapes=[pltpu.VMEM((D, B), bf16), pltpu.VMEM((4, AR, D), f32)],
         ),
         compiler_params=pltpu.CompilerParams(dimension_semantics=("arbitrary",), vmem_limit_bytes=60 << 20),
         cost_estimate=pl.CostEstimate(flops=17 * 10**9, bytes_accessed=32 << 20, transcendentals=0),
         name="mlp",
-    )(meta, mixed_head, mixed_tail, rows, cotangent, gain, w_out, w_up, w_down, flat_down, flat_up)
+    )(meta, mixed_head, mixed_tail, rows, cotangent, gain, weights, weights, weights, flat_down, flat_up)
 
 
 def exchange(value):
@@ -640,9 +643,7 @@
 
     weights_mine = jnp.concatenate([mine(query_weight), mine(key_weight), mine(value_weight)], axis=1)
     weights_mine = lax.all_gather(weights_mine, "fsdp", axis=0, tiled=True)
-    w_out = lax.all_gather(out_weight, "fsdp", axis=0, tiled=True)
-    w_up = lax.all_gather(up_weight, "fsdp", axis=0, tiled=True)
-    w_down = lax.all_gather(down_weight, "fsdp", axis=0, tiled=True)
+    weights_mlp = lax.all_gather(jnp.concatenate([out_weight, up_weight, down_weight], axis=1), "fsdp", axis=0, tiled=True)
     weights_all = lax.all_gather(jnp.concatenate([query_weight, key_weight, value_weight], axis=1), "fsdp", axis=0, tiled=True)
 
     down_pair = jnp.concatenate([flat_down[0], flat_down[1]], axis=1)
@@ -668,29 +669,33 @@
     mixed_tail = exchange(tail_sent)
     mixture = jnp.concatenate([head_mix, tail_mix], axis=2)
     logsum = jnp.concatenate([head_log, tail_log], axis=3)
-
-    hidden_low, inner_down, middle, grad_middle, grad_first_heads, grad_second_heads, terms = mlp(
+    mixture, logsum, up_mine, mixed_head = lax.optimization_barrier((mixture, logsum, up_mine, mixed_head))
+
+    hidden_low, inner_down, middle, grad_middle, grad_first_heads, grad_second_heads, mlp_keep, mlp_send = mlp(
         meta, mixed_head.reshape(D, -1), mixed_tail.reshape(D, -1), rows, cotangent[0], gain_mlp[None, :],
-        w_out, w_up, w_down, flat_down[2:], flat_up[2:],
+        weights_mlp, flat_down[2:], flat_up[2:],
     )
     grad_heads = [exchange(grad_first_heads), exchange(grad_second_heads)]
 
-    mlp_total = scatter_near(terms)
+    mlp_total = sum_low(mlp_keep, swap(mlp_send, "fsdp", 1))
     mlp_total, grad_heads[0] = lax.optimization_barrier((mlp_total, grad_heads[0]))
     mlp_total = scatter_heads(mlp_total)
-    grad_first_pair = attn_bwd(meta, scale_row[:, None], qkvt, grad_heads[0], mixture, logsum, 0)
-    mlp_total, grad_first_pair = lax.optimization_barrier((mlp_total, grad_first_pair))
-    arrived = [exchange(grad_first_pair.reshape(PARTS, 3 * PW, ROWS))]
+    scale_column = scale_row[:, None]
+    send_back = lambda g: exchange(g.reshape(PARTS, -1, ROWS)).reshape(g.shape)
+    grads, arrived = [], []
+    grads.append(attn_bwd(meta, scale_column, qkvt, grad_heads[0], mixture, logsum, 0, 2, 0))
+    mlp_total, grads[0] = lax.optimization_barrier((mlp_total, grads[0]))
+    arrived.append(send_back(grads[0]))
     mlp_total = sum_far(mlp_total)
-    meta, _ = lax.optimization_barrier((meta, grad_first_pair))
-    grad_second_pair = attn_bwd(meta, scale_row[:, None], qkvt, grad_heads[1], mixture, logsum, 1)
-    mlp_total, grad_second_pair = lax.optimization_barrier((mlp_total, grad_second_pair))
-    arrived.append(exchange(grad_second_pair.reshape(PARTS, 3 * PW, ROWS)))
+    meta, grads[0] = lax.optimization_barrier((meta, grads[0]))
+    grads.append(attn_bwd(meta, scale_column, qkvt, grad_heads[1], mixture, logsum, 2, 2, 0))
+    mlp_total, grads[1] = lax.optimization_barrier((mlp_total, grads[1]))
+    arrived.append(send_back(grads[1]))
 
     meta, arrived[0] = lax.optimization_barrier((meta, arrived[0]))
-    keep, send = adapter_grads(meta, [grad_first_pair, grad_second_pair], normed_all, inner_all, up_mine)
+    keep, send = adapter_grads(meta, grads, normed_all, inner_all, up_mine)
     hidden_late, inner_late, keep = lax.optimization_barrier((hidden_low, inner_down, keep))
-    outputs = (middle + (nn(hidden_late, w_down) + nn(inner_late, flat_up[3]))).astype(bf16)
+    outputs = (middle + (nn(hidden_late, weights_mlp[:, 2 * D :]) + nn(inner_late, flat_up[3]))).astype(bf16)
     total = sum_low(keep, swap(send, "fsdp", 1))
     total = jnp.concatenate([scatter_heads(total[:AR]), total[AR:]])
     total, arrived, outputs = lax.optimization_barrier((total, arrived, outputs))
@@ -698,7 +703,6 @@
     meta, total = lax.optimization_barrier((meta, total))
     own = jnp.concatenate([total, mlp_total])
     pieces = [own] + [swap(own, "heads", m) for m in (1, 2, 3)]
-    arrived = [a.reshape(PARTS, 3, PW, ROWS) for a in arrived]
     grad_inputs = back_inputs(meta, arrived, weights_all, flat_up[:2], down_pair, rows, gain_attn[None, :], grad_middle)
     pieces, grad_inputs = lax.optimization_barrier((pieces, grad_inputs))
     own = jnp.stack(pieces)

time: 428 us -> 421 us (0.984)
  waiting for transfers between devices: 86.4 us -> 71.2 us
  starting transfers between devices: 49.7 us -> 60.7 us
  local copies, waits for them, and re-layouts: 26.8 us -> 22.5 us
    all_gather x3 -> x1, waiting for transfers between devices: 13.5 us -> 0.01 us  [body(): lax.all_gather(jnp.concatenate([out_weight, up_weight, down_weight], axis...]
    ppermute x24, starting transfers between devices: 25 us -> 36.8 us  [swap(): return lax.ppermute(value, axis, [(i, i ^ mask) for i in range(count)])]
  transfers between devices with their start and end apart: 35 -> 33, of which waited for: 13 -> 12; matrix products, arithmetic and copies ran while one was open for 7% -> 7% of each run, Pallas kernels for 53% -> 54%
where the time goes in v1:
time: 421 us; the launch traced here: 413 us
  Pallas kernels  228 us (54%)
  waiting for transfers between devices  71.2 us (17%)
  starting transfers between devices  60.7 us (14%)
  local copies, waits for them, and re-layouts  22.5 us (5%)
  between operations  14.7 us (3%)
  other arithmetic  8.56 us (2%)
  matrix products  6.71 us (2%)
    pallas_call x2, Pallas kernels, attn_bwd(): pl.pallas_call(bwd_kernel, out_shape=jax.ShapeDtypeStruct((PARTS, 3, coun...  71.9 us
    pallas_call x2, Pallas kernels, attn_fwd(): pl.pallas_call(fwd_kernel, out_shape=(jax.ShapeDtypeStruct((PARTS, WIDTH,...  51.4 us
    ppermute x24, waiting for transfers between devices, swap(): return lax.ppermute(value, axis, [(i, i ^ mask) for i in range(count)])  51.3 us
    pallas_call x1, Pallas kernels, mlp(): pl.pallas_call(mlp_kernel, out_shape=[jax.ShapeDtypeStruct((ROWS, D), bf1...  37.6 us
    ppermute x24, starting transfers between devices, swap(): return lax.ppermute(value, axis, [(i, i ^ mask) for i in range(count)])  36.8 us
    pallas_call x4, Pallas kernels, qkv_project(): pl.pallas_call(qkv_kernel, out_shape=(jax.ShapeDtypeStruct((3 * WIDTH, TO...  32 us
    all_to_all x6, starting transfers between devices, exchange(): lax.all_to_all(value, 'heads', split_axis=0, concat_axis=0, tiled=True)  23.8 us
    pallas_call x1, Pallas kernels, back_inputs(): pl.pallas_call(back_kernel, out_shape=jax.ShapeDtypeStruct((ROWS, D), f32...  19.8 us
  transfers between devices with their start and end apart: 33, of which 12 were waited for; matrix products, arithmetic and copies ran while one was open for 7% of the time, Pallas kernels for 54%

profile of v1, /device:TPU:9, one launch (start us, length us, event | category | flops | bytes accessed | tf_op | source)
XLA Modules:
  0.0 412.7 jit_solution(4761886677572057651)
XLA Ops:
  22.9 14.8 %collective-permute-done.low_ref = bf16[384,1280]{1,0:T(8,128)(2,1)} collective-permute-done((bf16[384,1280]{1,0:T(8,128)(2,1)}, bf16[384,1280]{1,0:T(8,128)(2,1)}, u32[]{:S(2)}, u32[]{:S(2)}) %collective-permute-start) | collective-permute-done | bytes 983072 | tf_op jit(solution)/shard_map/ppermute | solution.py:567
  39.8 5.5 %all-gather.4.cloned.1.call-done = bf16[1280,960]{1,0:T(8,128)(2,1)} async-done(((bf16[160,960]{1,0:T(8,128)(2,1)}), bf16[1280,960]{1,0:T(8,128)(2,1)}) %all-gather.4.cloned.1.call-update) | async-done | bytes 2457616 | tf_op jit(solution)/shard_map/all_gather | solution.py:645
  45.3 4.3 %copy.56 = bf16[1280,960]{0,1:T(8,128)(2,1)} copy(bf16[1280,960]{1,0:T(8,128)(2,1)} %all-gather.4.cloned.1.call-done) | data formatting | bytes 4915200 | tf_op jit(solution)/shard_map/all_gather | solution.py:645
  49.6 8.0 %qkv_project.4 = (bf16[960,3072]{1,0:T(8,128)(2,1)}, bf16[3072,1280]{1,0:T(8,128)(2,1)}, bf16[3072,256]{1,0:T(8,128)(2,1)}) custom-call(s32[8]{0:T(128)} %pad_add_fusion.meta, s32[1]{0:T(128)} %bitcast.16.first, bf16[768,1280]{1,0:T(8,128)(2,1)} %bitcast.57, bf16[768,1280]{1,0:T(8,128)(2,1)} %bitcast.58, f32[1,1280]{1,0:T(1,128)} %reshape.83.gain_ref.refs_6_, ...), custom_call_target="tpu_custom_call" | custom-call | flops 2390753280 | bytes 8388608 | tf_op jit(solution)/shard_map/qkv_project/pallas_call | solution.py:84
  57.8 8.0 %qkv_project.5 = (bf16[960,3072]{1,0:T(8,128)(2,1)}, bf16[3072,1280]{1,0:T(8,128)(2,1)}, bf16[3072,256]{1,0:T(8,128)(2,1)}) custom-call(s32[8]{0:T(128)} %pad_add_fusion.meta, s32[1]{0:T(128)} %bitcast.15.first, bf16[384,1280]{1,0:T(8,128)(2,1)} %collective-permute-done.5.low_ref, ...), custom_call_target="tpu_custom_call", output_to_operand_aliasing={{0}: (9, {}), {1}: (10, {}), {2}: (11, {})} | custom-call | flops 2390753280 | bytes 8388608 | tf_op jit(solution)/shard_map/qkv_project/pallas_call | solution.py:84
  65.8 8.0 %qkv_project.6 = (bf16[960,3072]{1,0:T(8,128)(2,1)}, bf16[3072,1280]{1,0:T(8,128)(2,1)}, bf16[3072,256]{1,0:T(8,128)(2,1)}) custom-call(s32[8]{0:T(128)} %pad_add_fusion.meta, s32[1]{0:T(128)} %bitcast.14.first, bf16[384,1280]{1,0:T(8,128)(2,1)} %collective-permute-done.low_ref, ...), custom_call_target="tpu_custom_call", output_to_operand_aliasing={{0}: (9, {}), {1}: (10, {}), {2}: (11, {})} | custom-call | flops 2390753280 | bytes 8388608 | tf_op jit(solution)/shard_map/qkv_project/pallas_call | solution.py:84
  73.8 5.0 %collective-permute-done.1.low_ref = bf16[384,1280]{1,0:T(8,128)(2,1)S(1)} collective-permute-done((bf16[384,1280]{1,0:T(8,128)(2,1)}, bf16[384,1280]{1,0:T(8,128)(2,1)S(1)}, u32[]{:S(2)}, u32[]{:S(2)}) %collective-permute-start.1) | collective-permute-done | bytes 983072 | tf_op jit(solution)/shard_map/ppermute | solution.py:567
  79.8 8.0 %qkv_project.7 = (bf16[960,3072]{1,0:T(8,128)(2,1)}, bf16[3072,1280]{1,0:T(8,128)(2,1)}, bf16[3072,256]{1,0:T(8,128)(2,1)}) custom-call(s32[8]{0:T(128)} %pad_add_fusion.meta, s32[1]{0:T(128)} %bitcast.5.first, bf16[384,1280]{1,0:T(8,128)(2,1)} %copy-done.14, ...), custom_call_target="tpu_custom_call", output_to_operand_aliasing={{0}: (9, {}), {1}: (10, {}), {2}: (11, {})} | custom-call | flops 2390753280 | bytes 8388608 | tf_op jit(solution)/shard_map/qkv_project/pallas_call | solution.py:84
  87.8 31.1 %attn_fwd.2 = (bf16[4,320,512]{2,1,0:T(8,128)(2,1)}, f32[4,4,1,512]{3,2,1,0:T(1,128)}) custom-call(s32[2]{0:T(128)} %copy-done.30, bf16[960,3072]{1,0:T(8,128)(2,1)} %get-tuple-element.79.q_ref.k_ref.v_ref, bf16[960,3072]{1,0:T(8,128)(2,1)} %get-tuple-element.79.q_ref.k_ref.v_ref, bf16[960,3072]{1,0:T(8,128)(2,1)} %get-tuple-element.79.q_ref.k_ref.v_ref), custom_call_target="tpu_custom_call" | custom-call | flops 25999998976 | bytes 5242880 | tf_op jit(solution)/shard_map/attn_fwd/pallas_call | solution.py:336
  118.8 3.7 all-to-all-start
  122.6 20.4 %attn_fwd.3 = (bf16[4,320,256]{2,1,0:T(8,128)(2,1)}, f32[4,4,1,256]{3,2,1,0:T(1,128)}) custom-call(s32[2]{0:T(128)} %copy-done.30, bf16[960,3072]{1,0:T(8,128)(2,1)} %get-tuple-element.79.q_ref.k_ref.v_ref, bf16[960,3072]{1,0:T(8,128)(2,1)} %get-tuple-element.79.q_ref.k_ref.v_ref, bf16[960,3072]{1,0:T(8,128)(2,1)} %get-tuple-element.79.q_ref.k_ref.v_ref), custom_call_target="tpu_custom_call" | custom-call | flops 12999999488 | bytes 5242880 | tf_op jit(solution)/shard_map/attn_fwd/pallas_call | solution.py:336
  144.0 4.3 %all-to-all-start.1 = ((bf16[4,320,256]{2,1,0:T(8,128)(2,1)}), bf16[4,320,256]{2,1,0:T(8,128)(2,1)}, u32[]{:S(2)}, u32[]{:S(2)}) async-start(bf16[4,320,256]{2,1,0:T(8,128)(2,1)} %get-tuple-element.88), calls=%async_computation.1 | async-start | bytes 1310720 | tf_op jit(solution)/shard_map/all_to_all | solution.py:562
  156.6 37.6 %mlp.1 = (bf16[768,1280]{1,0:T(8,128)(2,1)}, bf16[768,128]{1,0:T(8,128)(2,1)}, f32[768,1280]{1,0:T(8,128)}, f32[768,1280]{1,0:T(8,128)}, bf16[4,160,768]{2,1,0:T...) custom-call(s32[8]{0:T(128)} %pad_add_fusion.meta, ...), custom_call_target="tpu_custom_call" | custom-call | flops 16999999488 | bytes 33554432 | tf_op jit(solution)/shard_map/mlp/pallas_call | solution.py:527
  196.4 3.5 all-to-all-start.2
  200.8 11.9 %all-to-all-done.2.do_ref = bf16[4,160,768]{2,1,0:T(8,128)(2,1)S(1)} async-done(((bf16[4,160,768]{2,1,0:T(8,128)(2,1)}), bf16[4,160,768]{2,1,0:T(8,128)(2,1)S(1)}, u32[]{:S(2)}, u32[]{:S(2)}) %all-to-all-start.2) | async-done | bytes 983072 | tf_op jit(solution)/shard_map/all_to_all | solution.py:562
  212.7 3.7 all-to-all-start.4
  219.3 35.9 %attn_bwd.2.refs_0_ = bf16[4,3,160,768]{3,2,1,0:T(8,128)(2,1)} custom-call(s32[8]{0:T(128)} %pad_add_fusion.meta, f32[80,1]{1,0:T(8,128)} %copy.68.scale_ref, bf16[960,3072]{1,0:T(8,128)(2,1)} %get-tuple-element.79.q_ref.k_ref.v_ref, bf16[960,3072]{1,0:T(8,128)(2,1)} %get-tuple-element.79.q_ref.k_ref.v_ref, ...), custom_call_target="tpu_custom_call" | custom-call | flops 35999997952 | bytes 16777216 | tf_op jit(solution)/shard_map/attn_bwd/pallas_call | solution.py:439
  257.5 6.3 %collective-permute-start.11 = (bf16[64,1280]{1,0:T(8,128)(2,1)S(1)}, bf16[64,1280]{1,0:T(8,128)(2,1)S(1)}, u32[]{:S(2)}, u32[]{:S(2)}) collective-permute-start(bf16[64,1280]{1,0:T(8,128)(2,1)S(1)} %add_convert_fusion.4), channel_id=1, source_target_pairs={{0,4},{1,5},{2,6},{3,7},{4,0},{5,1},{6,2},{7,3},{8,12},{9,13},{10,... | collective-permute-start | bytes 491528 | tf_op jit(solution)/shard_map/ppermute | solution.py:567
  264.8 3.7 all-to-all-start.3
  268.5 36.0 %attn_bwd.3.refs_1_ = bf16[4,3,160,768]{3,2,1,0:T(8,128)(2,1)} custom-call(s32[8]{0:T(128)} %pad_add_fusion.meta, f32[80,1]{1,0:T(8,128)} %copy.68.scale_ref, bf16[960,3072]{1,0:T(8,128)(2,1)} %get-tuple-element.79.q_ref.k_ref.v_ref, bf16[960,3072]{1,0:T(8,128)(2,1)} %get-tuple-element.79.q_ref.k_ref.v_ref, ...), custom_call_target="tpu_custom_call" | custom-call | flops 35999997952 | bytes 16777216 | tf_op jit(solution)/shard_map/attn_bwd/pallas_call | solution.py:439
  307.8 4.9 %all-to-all-start.5 = ((bf16[4,480,768]{2,1,0:T(8,128)(2,1)}), bf16[4,480,768]{2,1,0:T(8,128)(2,1)}, u32[]{:S(2)}, u32[]{:S(2)}) async-start(bf16[4,480,768]{2,1,0:T(8,128)(2,1)} %bitcast.51), calls=%async_computation.5 | async-start | bytes 5898240 | tf_op jit(solution)/shard_map/all_to_all | solution.py:562
  312.7 10.3 %adapter_grads.1 = (bf16[160,1280]{1,0:T(8,128)(2,1)}, bf16[160,1280]{1,0:T(8,128)(2,1)}) custom-call(s32[8]{0:T(128)} %pad_add_fusion.meta, bf16[4,3,160,768]{3,2,1,0:T(8,128)(2,1)} %attn_bwd.2.refs_0_, bf16[4,3,160,768]{3,2,1,0:T(8,128)(2,1)} %attn_bwd.3.refs_1_, bf16[3072,1280]{1,0:T(8,128)(2,1)} %get-tuple-element.105.refs_2_, ...), custom_call_target="tpu_custom_call" | custom-call | flops 4026531840 | bytes 20971520 | tf_op jit(solution)/shard_map/adapter_grads/pallas_call | solution.py:146
  323.1 2.9 collective-permute-start.13
  325.9 4.8 %fusion.2 = f32[768,1280]{1,0:T(8,128)S(1)} fusion(bf16[768,1280]{1,0:T(8,128)(2,1)S(1)} %copy-done.33, bf16[1280,3840]{1,0:T(8,128)(2,1)} %all-gather.6.cloned.1.call-done.out_ref.up_ref.down_ref), kind=kOutput, calls=%fused_computation.3 | convolution fusion | flops 2516582400 | bytes 9175040 | tf_op jit(solution)/shard_map/dot_general | solution.py:39
  336.0 9.8 %collective-permute-done.14 = bf16[32,1280]{1,0:T(8,128)(2,1)S(1)} collective-permute-done((bf16[32,1280]{1,0:T(8,128)(2,1)S(1)}, bf16[32,1280]{1,0:T(8,128)(2,1)S(1)}, u32[]{:S(2)}, u32[]{:S(2)}) %collective-permute-start.14) | collective-permute-done | bytes 81952 | tf_op jit(solution)/shard_map/ppermute | solution.py:567
  345.8 3.2 collective-permute-done.15
  350.3 6.8 %collective-permute-start.18 = (bf16[64,1280]{1,0:T(8,128)(2,1)S(1)}, bf16[64,1280]{1,0:T(8,128)(2,1)S(1)}, u32[]{:S(2)}, u32[]{:S(2)}) collective-permute-start(bf16[64,1280]{1,0:T(8,128)(2,1)S(1)} %pad_maximum_fusion.6), channel_id=1, source_target_pairs={{0,4},{1,5},{2,6},{3,7},{4,0},{5,1},{6,2},{7,3},{8,12},{9,13},{10,... | collective-permute-start | bytes 491528 | tf_op jit(solution)/shard_map/ppermute | solution.py:567
  357.3 9.7 %collective-permute-done.18 = bf16[64,1280]{1,0:T(8,128)(2,1)S(1)} collective-permute-done((bf16[64,1280]{1,0:T(8,128)(2,1)S(1)}, bf16[64,1280]{1,0:T(8,128)(2,1)S(1)}, u32[]{:S(2)}, u32[]{:S(2)}) %collective-permute-start.18) | collective-permute-done | bytes 163872 | tf_op jit(solution)/shard_map/ppermute | solution.py:567
  367.0 4.9 %collective-permute-done.19 = bf16[64,1280]{1,0:T(8,128)(2,1)S(1)} collective-permute-done((bf16[64,1280]{1,0:T(8,128)(2,1)S(1)}, bf16[64,1280]{1,0:T(8,128)(2,1)S(1)}, u32[]{:S(2)}, u32[]{:S(2)}) %collective-permute-start.19) | collective-permute-done | bytes 163872 | tf_op jit(solution)/shard_map/ppermute | solution.py:567
  374.8 19.8 %back_inputs.1 = f32[768,1280]{1,0:T(8,128)} custom-call(s32[8]{0:T(128)} %pad_add_fusion.meta, bf16[4,3,160,768]{3,2,1,0:T(8,128)(2,1)} %bitcast.53, bf16[4,3,160,768]{3,2,1,0:T(8,128)(2,1)} %bitcast.27.refs_1_, bf16[1280,3840]{1,0:T(8,128)(2,1)} %all-gather.8.cloned.1.call-done.refs_2_, bf16[2,128,1280]{2,1,0:T(8,128)(2,1)} %bitcast.63, ...), custom_call_target="tpu_custom_call" | custom-call | flops 7549747200 | bytes 25165824 | tf_op jit(solution)/shard_map/back_inputs/pallas_call | solution.py:208
  396.7 2.7 collective-permute-done.23.other_ref
  400.5 5.3 %assemble.1 = (f32[4,128,1280]{2,1,0:T(8,128)}, f32[4,128,1280]{2,1,0:T(8,128)}) custom-call(s32[8]{0:T(128)} %pad_add_fusion.meta, bf16[4,128,1280]{2,1,0:T(8,128)(2,1)} %copy-done, bf16[4,128,1280]{2,1,0:T(8,128)(2,1)} %copy-done.10), custom_call_target="tpu_custom_call" | custom-call | flops 1048576 | bytes 8388608 | tf_op jit(solution)/shard_map/assemble/pallas_call | solution.py:258
  (164 shorter events, 53.2 us)
Async XLA Ops:
  7.2 38.1 %all-gather.4.cloned.1.call-start = ((), (), s32[]{:S(2)}) async-start(), calls=%async_computation.6 | async-start | bytes 2949120 | tf_op jit(solution)/shard_map/all_gather | solution.py:645
  10.4 146.2 %all-gather.6.cloned.1.call-start = ((), (), s32[]{:S(2)}) async-start(), calls=%async_computation.7 | async-start | bytes 11059200 | tf_op jit(solution)/shard_map/all_gather | solution.py:646
  11.6 363.2 %all-gather.8.cloned.1.call-start = ((), (), s32[]{:S(2)}) async-start(), calls=%async_computation.8 | async-start | bytes 11059200 | tf_op jit(solution)/shard_map/all_gather | solution.py:647
  13.8 24.1 %collective-permute-start.2 = (bf16[384,1280]{1,0:T(8,128)(2,1)}, bf16[384,1280]{1,0:T(8,128)(2,1)S(1)}, u32[]{:S(2)}, u32[]{:S(2)}) collective-permute-start(bf16[384,1280]{1,0:T(8,128)(2,1)} %get-tuple-element.68), channel_id=1, source_target_pairs={{0,8},{8,0},{16,24},{24,16},{1,9},{9,1},{17,25},{25,17},{2,10},{10... | collective-permute-start | bytes 2949128 | tf_op jit(solution)/shard_map/ppermute | solution.py:567
  15.0 22.7 %collective-permute-start = (bf16[384,1280]{1,0:T(8,128)(2,1)}, bf16[384,1280]{1,0:T(8,128)(2,1)}, u32[]{:S(2)}, u32[]{:S(2)}) collective-permute-start(bf16[384,1280]{1,0:T(8,128)(2,1)} %get-tuple-element.69), channel_id=1, source_target_pairs={{0,16},{8,24},{16,0},{24,8},{1,17},{9,25},{17,1},{25,9},{2,18},{10... | collective-permute-start | bytes 2949128 | tf_op jit(solution)/shard_map/ppermute | solution.py:567
  17.6 40.2 %collective-permute-start.5 = (bf16[384,1280]{1,0:T(8,128)(2,1)}, bf16[384,1280]{1,0:T(8,128)(2,1)}, u32[]{:S(2)}, u32[]{:S(2)}) collective-permute-start(bf16[384,1280]{1,0:T(8,128)(2,1)} %get-tuple-element.69), channel_id=1, source_target_pairs={{0,8},{8,0},{16,24},{24,16},{1,9},{9,1},{17,25},{25,17},{2,10},{10... | collective-permute-start | bytes 2949128 | tf_op jit(solution)/shard_map/ppermute | solution.py:567
  17.9 47.9 %collective-permute-start.4 = (bf16[384,1280]{1,0:T(8,128)(2,1)}, bf16[384,1280]{1,0:T(8,128)(2,1)}, u32[]{:S(2)}, u32[]{:S(2)}) collective-permute-start(bf16[384,1280]{1,0:T(8,128)(2,1)} %get-tuple-element.68), channel_id=1, source_target_pairs={{0,16},{8,24},{16,0},{24,8},{1,17},{9,25},{17,1},{25,9},{2,18},{10... | collective-permute-start | bytes 2949128 | tf_op jit(solution)/shard_map/ppermute | solution.py:567
  37.6 41.2 %collective-permute-start.1 = (bf16[384,1280]{1,0:T(8,128)(2,1)}, bf16[384,1280]{1,0:T(8,128)(2,1)S(1)}, u32[]{:S(2)}, u32[]{:S(2)}) collective-permute-start(bf16[384,1280]{1,0:T(8,128)(2,1)} %collective-permute-done.low_ref), channel_id=1, source_target_pairs={{0,8},{8,0},{16,24},{24,16},{1,9},{9,1},{17,25},{25,17},{2,10},{10... | collective-permute-start | bytes 2949128 | tf_op jit(solution)/shard_map/ppermute | solution.py:567
  37.9 41.9 %collective-permute-start.3 = (bf16[384,1280]{1,0:T(8,128)(2,1)S(1)}, bf16[384,1280]{1,0:T(8,128)(2,1)}, u32[]{:S(2)}, u32[]{:S(2)}) collective-permute-start(bf16[384,1280]{1,0:T(8,128)(2,1)S(1)} %collective-permute-done.2.high_ref), channel_id=1, source_target_pairs={{0,16},{8,24},{16,0},{24,8},{1,17},{9,25},{17,1},{25,9},{2,18},{10... | collective-permute-start | bytes 2949128 | tf_op jit(solution)/shard_map/ppermute | solution.py:567
  118.8 24.1 %all-to-all-start = ((bf16[4,320,512]{2,1,0:T(8,128)(2,1)}), bf16[4,320,512]{2,1,0:T(8,128)(2,1)S(1)}, u32[]{:S(2)}, u32[]{:S(2)}) async-start(bf16[4,320,512]{2,1,0:T(8,128)(2,1)} %get-tuple-element.80), calls=%async_computation | async-start | bytes 2621440 | tf_op jit(solution)/shard_map/all_to_all | solution.py:562
  144.0 12.6 %all-to-all-start.1 = ((bf16[4,320,256]{2,1,0:T(8,128)(2,1)}), bf16[4,320,256]{2,1,0:T(8,128)(2,1)}, u32[]{:S(2)}, u32[]{:S(2)}) async-start(bf16[4,320,256]{2,1,0:T(8,128)(2,1)} %get-tuple-element.88), calls=%async_computation.1 | async-start | bytes 1310720 | tf_op jit(solution)/shard_map/all_to_all | solution.py:562
  194.2 6.4 %collective-permute-start.6 = (bf16[256,1280]{1,0:T(8,128)(2,1)}, bf16[256,1280]{1,0:T(8,128)(2,1)S(1)}, u32[]{:S(2)}, u32[]{:S(2)}) collective-permute-start(bf16[256,1280]{1,0:T(8,128)(2,1)} %get-tuple-element.92), channel_id=1, source_target_pairs={{0,1},{1,0},{2,3},{3,2},{4,5},{5,4},{6,7},{7,6},{8,9},{9,8},{10,11... | collective-permute-start | bytes 1966088 | tf_op jit(solution)/shard_map/ppermute | solution.py:567
  196.4 16.3 %all-to-all-start.2 = ((bf16[4,160,768]{2,1,0:T(8,128)(2,1)}), bf16[4,160,768]{2,1,0:T(8,128)(2,1)S(1)}, u32[]{:S(2)}, u32[]{:S(2)}) async-start(bf16[4,160,768]{2,1,0:T(8,128)(2,1)} %get-tuple-element.93), calls=%async_computation.2 | async-start | bytes 1966080 | tf_op jit(solution)/shard_map/all_to_all | solution.py:562
  212.7 51.1 %all-to-all-start.4 = ((bf16[4,160,768]{2,1,0:T(8,128)(2,1)}), bf16[4,160,768]{2,1,0:T(8,128)(2,1)S(1)}, u32[]{:S(2)}, u32[]{:S(2)}) async-start(bf16[4,160,768]{2,1,0:T(8,128)(2,1)} %get-tuple-element.103), calls=%async_computation.4 | async-start | bytes 1966080 | tf_op jit(solution)/shard_map/all_to_all | solution.py:562
  216.5 38.7 %collective-permute-start.7 = (bf16[64,1280]{1,0:T(8,128)(2,1)S(1)}, bf16[64,1280]{1,0:T(8,128)(2,1)S(1)}, u32[]{:S(2)}, u32[]{:S(2)}) collective-permute-start(bf16[64,1280]{1,0:T(8,128)(2,1)S(1)} %get-tuple-element.136), channel_id=1, source_target_pairs={{0,8},{8,0},{16,24},{24,16},{1,9},{9,1},{17,25},{25,17},{2,10},{10... | collective-permute-start | bytes 491528 | tf_op jit(solution)/shard_map/ppermute | solution.py:567
  218.0 37.2 %collective-permute-start.8 = (bf16[64,1280]{1,0:T(8,128)(2,1)S(1)}, bf16[64,1280]{1,0:T(8,128)(2,1)S(1)}, u32[]{:S(2)}, u32[]{:S(2)}) collective-permute-start(bf16[64,1280]{1,0:T(8,128)(2,1)S(1)} %get-tuple-element.138), channel_id=1, source_target_pairs={{0,16},{8,24},{16,0},{24,8},{1,17},{9,25},{17,1},{25,9},{2,18},{10... | collective-permute-start | bytes 491528 | tf_op jit(solution)/shard_map/ppermute | solution.py:567
  219.2 36.0 %collective-permute-start.9 = (bf16[64,1280]{1,0:T(8,128)(2,1)S(1)}, bf16[64,1280]{1,0:T(8,128)(2,1)S(1)}, u32[]{:S(2)}, u32[]{:S(2)}) collective-permute-start(bf16[64,1280]{1,0:T(8,128)(2,1)S(1)} %get-tuple-element.137), channel_id=1, source_target_pairs={{0,24},{8,16},{16,8},{24,0},{1,25},{9,17},{17,9},{25,1},{2,26},{10... | collective-permute-start | bytes 491528 | tf_op jit(solution)/shard_map/ppermute | solution.py:567
  255.3 49.2 %collective-permute-start.10 = (bf16[64,1280]{1,0:T(8,128)(2,1)S(1)}, bf16[64,1280]{1,0:T(8,128)(2,1)S(1)}, u32[]{:S(2)}, u32[]{:S(2)}) collective-permute-start(bf16[64,1280]{1,0:T(8,128)(2,1)S(1)} %add_convert_fusion.4), channel_id=1, source_target_pairs={{0,2},{1,3},{2,0},{3,1},{4,6},{5,7},{6,4},{7,5},{8,10},{9,11},{10,... | collective-permute-start | bytes 491528 | tf_op jit(solution)/shard_map/ppermute | solution.py:567
  257.5 47.0 %collective-permute-start.11 = (bf16[64,1280]{1,0:T(8,128)(2,1)S(1)}, bf16[64,1280]{1,0:T(8,128)(2,1)S(1)}, u32[]{:S(2)}, u32[]{:S(2)}) collective-permute-start(bf16[64,1280]{1,0:T(8,128)(2,1)S(1)} %add_convert_fusion.4), channel_id=1, source_target_pairs={{0,4},{1,5},{2,6},{3,7},{4,0},{5,1},{6,2},{7,3},{8,12},{9,13},{10,... | collective-permute-start | bytes 491528 | tf_op jit(solution)/shard_map/ppermute | solution.py:567
  263.8 41.3 %collective-permute-start.12 = (bf16[64,1280]{1,0:T(8,128)(2,1)S(1)}, bf16[64,1280]{1,0:T(8,128)(2,1)}, u32[]{:S(2)}, u32[]{:S(2)}) collective-permute-start(bf16[64,1280]{1,0:T(8,128)(2,1)S(1)} %add_convert_fusion.4), channel_id=1, source_target_pairs={{0,6},{1,7},{2,4},{3,5},{4,2},{5,3},{6,0},{7,1},{8,14},{9,15},{10,... | collective-permute-start | bytes 491528 | tf_op jit(solution)/shard_map/ppermute | solution.py:567
  264.8 41.4 %all-to-all-start.3 = ((bf16[4,480,768]{2,1,0:T(8,128)(2,1)}), bf16[4,480,768]{2,1,0:T(8,128)(2,1)S(1)}, u32[]{:S(2)}, u32[]{:S(2)}) async-start(bf16[4,480,768]{2,1,0:T(8,128)(2,1)} %bitcast.52), calls=%async_computation.3 | async-start | bytes 5898240 | tf_op jit(solution)/shard_map/all_to_all | solution.py:562
  307.8 41.2 %all-to-all-start.5 = ((bf16[4,480,768]{2,1,0:T(8,128)(2,1)}), bf16[4,480,768]{2,1,0:T(8,128)(2,1)}, u32[]{:S(2)}, u32[]{:S(2)}) async-start(bf16[4,480,768]{2,1,0:T(8,128)(2,1)} %bitcast.51), calls=%async_computation.5 | async-start | bytes 5898240 | tf_op jit(solution)/shard_map/all_to_all | solution.py:562
  323.1 7.7 %collective-permute-start.13 = (bf16[160,1280]{1,0:T(8,128)(2,1)}, bf16[160,1280]{1,0:T(8,128)(2,1)S(1)}, u32[]{:S(2)}, u32[]{:S(2)}) collective-permute-start(bf16[160,1280]{1,0:T(8,128)(2,1)} %get-tuple-element.110), channel_id=1, source_target_pairs={{0,1},{1,0},{2,3},{3,2},{4,5},{5,4},{6,7},{7,6},{8,9},{9,8},{10,11... | collective-permute-start | bytes 1228808 | tf_op jit(solution)/shard_map/ppermute | solution.py:567
  330.9 14.8 %collective-permute-start.14 = (bf16[32,1280]{1,0:T(8,128)(2,1)S(1)}, bf16[32,1280]{1,0:T(8,128)(2,1)S(1)}, u32[]{:S(2)}, u32[]{:S(2)}) collective-permute-start(bf16[32,1280]{1,0:T(8,128)(2,1)S(1)} %get-tuple-element.139), channel_id=1, source_target_pairs={{0,8},{8,0},{16,24},{24,16},{1,9},{9,1},{17,25},{25,17},{2,10},{10... | collective-permute-start | bytes 245768 | tf_op jit(solution)/shard_map/ppermute | solution.py:567
  332.8 16.2 %collective-permute-start.15 = (bf16[32,1280]{1,0:T(8,128)(2,1)S(1)}, bf16[32,1280]{1,0:T(8,128)(2,1)S(1)}, u32[]{:S(2)}, u32[]{:S(2)}) collective-permute-start(bf16[32,1280]{1,0:T(8,128)(2,1)S(1)} %get-tuple-element.141), channel_id=1, source_target_pairs={{0,16},{8,24},{16,0},{24,8},{1,17},{9,25},{17,1},{25,9},{2,18},{10... | collective-permute-start | bytes 245768 | tf_op jit(solution)/shard_map/ppermute | solution.py:567
  333.9 15.0 %collective-permute-start.16 = (bf16[32,1280]{1,0:T(8,128)(2,1)S(1)}, bf16[32,1280]{1,0:T(8,128)(2,1)S(1)}, u32[]{:S(2)}, u32[]{:S(2)}) collective-permute-start(bf16[32,1280]{1,0:T(8,128)(2,1)S(1)} %get-tuple-element.140), channel_id=1, source_target_pairs={{0,24},{8,16},{16,8},{24,0},{1,25},{9,17},{17,9},{25,1},{2,26},{10... | collective-permute-start | bytes 245768 | tf_op jit(solution)/shard_map/ppermute | solution.py:567
  349.0 8.3 %collective-permute-start.17 = (bf16[64,1280]{1,0:T(8,128)(2,1)S(1)}, bf16[64,1280]{1,0:T(8,128)(2,1)S(1)}, u32[]{:S(2)}, u32[]{:S(2)}) collective-permute-start(bf16[64,1280]{1,0:T(8,128)(2,1)S(1)} %pad_maximum_fusion.6), channel_id=1, source_target_pairs={{0,2},{1,3},{2,0},{3,1},{4,6},{5,7},{6,4},{7,5},{8,10},{9,11},{10,... | collective-permute-start | bytes 491528 | tf_op jit(solution)/shard_map/ppermute | solution.py:567
  350.3 16.7 %collective-permute-start.18 = (bf16[64,1280]{1,0:T(8,128)(2,1)S(1)}, bf16[64,1280]{1,0:T(8,128)(2,1)S(1)}, u32[]{:S(2)}, u32[]{:S(2)}) collective-permute-start(bf16[64,1280]{1,0:T(8,128)(2,1)S(1)} %pad_maximum_fusion.6), channel_id=1, source_target_pairs={{0,4},{1,5},{2,6},{3,7},{4,0},{5,1},{6,2},{7,3},{8,12},{9,13},{10,... | collective-permute-start | bytes 491528 | tf_op jit(solution)/shard_map/ppermute | solution.py:567
  357.1 14.8 %collective-permute-start.19 = (bf16[64,1280]{1,0:T(8,128)(2,1)S(1)}, bf16[64,1280]{1,0:T(8,128)(2,1)S(1)}, u32[]{:S(2)}, u32[]{:S(2)}) collective-permute-start(bf16[64,1280]{1,0:T(8,128)(2,1)S(1)} %pad_maximum_fusion.6), channel_id=1, source_target_pairs={{0,6},{1,7},{2,4},{3,5},{4,2},{5,3},{6,0},{7,1},{8,14},{9,15},{10,... | collective-permute-start | bytes 491528 | tf_op jit(solution)/shard_map/ppermute | solution.py:567
  372.1 22.5 %collective-permute-start.20 = (bf16[128,1280]{1,0:T(8,128)(2,1)S(1)}, bf16[128,1280]{1,0:T(8,128)(2,1)S(1)}, u32[]{:S(2)}, u32[]{:S(2)}) collective-permute-start(bf16[128,1280]{1,0:T(8,128)(2,1)S(1)} %constant_dynamic-update-slice_fusion), channel_id=1, source_target_pairs={{0,8},{8,0},{16,24},{24,16},{1,9},{9,1},{17,25},{25,17},{2,10},{10... | collective-permute-start | bytes 983048 | tf_op jit(solution)/shard_map/ppermute | solution.py:567
  372.4 22.2 %collective-permute-start.21 = (bf16[128,1280]{1,0:T(8,128)(2,1)S(1)}, bf16[128,1280]{1,0:T(8,128)(2,1)S(1)}, u32[]{:S(2)}, u32[]{:S(2)}) collective-permute-start(bf16[128,1280]{1,0:T(8,128)(2,1)S(1)} %constant_dynamic-update-slice_fusion), channel_id=1, source_target_pairs={{0,16},{8,24},{16,0},{24,8},{1,17},{9,25},{17,1},{25,9},{2,18},{10... | collective-permute-start | bytes 983048 | tf_op jit(solution)/shard_map/ppermute | solution.py:567
  372.7 21.9 %collective-permute-start.22 = (bf16[128,1280]{1,0:T(8,128)(2,1)S(1)}, bf16[128,1280]{1,0:T(8,128)(2,1)S(1)}, u32[]{:S(2)}, u32[]{:S(2)}) collective-permute-start(bf16[128,1280]{1,0:T(8,128)(2,1)S(1)} %constant_dynamic-update-slice_fusion), channel_id=1, source_target_pairs={{0,24},{8,16},{16,8},{24,0},{1,25},{9,17},{17,9},{25,1},{2,26},{10... | collective-permute-start | bytes 983048 | tf_op jit(solution)/shard_map/ppermute | solution.py:567
  (36 other events, 307.4 us)
Sparse Core Ops, SparseCore 0:
  10.5 34.7 all-gather.3
  47.5 90.7 all-gather.5
  140.0 92.3 all-gather.7

commit v2 on v1

--- a/solution.py
+++ b/solution.py
@@ -1,3 +1,5 @@
+import functools
+
 import jax
 import jax.numpy as jnp
 from jax import lax
@@ -359,7 +361,7 @@
     lo = (r - mid.astype(f32)).astype(bf16)
     return hi, mid, lo
 
-def bwd_kernel(meta, scale_ref, q_ref, k_ref, v_ref, do_ref, o_ref, lse_ref, out_ref, kp, vp, qt, dot, dkt, dvt, dqt):
+def bwd_kernel(meta, scale_ref, q_ref, k_ref, v_ref, head_ref, tail_ref, o_ref, lse_ref, out_ref, kp, vp, qt, dot, dkt, dvt, dqt):
     NH = kp.shape[0]
     b1, b2 = meta[0], meta[1]
     row16 = lax.broadcasted_iota(jnp.int32, (16, 128), 0)
@@ -372,15 +374,14 @@
         rest = jnp.where(row16 == 1, mid.astype(f32), jnp.where(row16 == 2, lo.astype(f32), 0.0))
         return jnp.where(row16 == 0, hi.astype(f32), rest).astype(bf16)
 
-    @pl.loop(0, 2 * PARTS)
-    def _(step):
-        chunk = step // 2
-        for t in range(3):
-            off = pl.multiple_of((step % 2) * HALF + t * 128, 128)
-            sl, here = pl.ds(pl.multiple_of(chunk * ROWS + off, 128), 128), pl.ds(off, 128)
+    @pl.loop(0, PARTS)
+    def _(chunk):
+        for off in range(0, ROWS, 128):
+            sl, here = pl.ds(pl.multiple_of(chunk * ROWS + off, 128), 128), slice(off, off + 128)
+            grad_ref, start = (head_ref, off) if off < 2 * B else (tail_ref, off - 2 * B)
             for h in range(NH):
                 own = slice(h * HD, (h + 1) * HD)
-                do, o = do_ref[chunk, own, here], o_ref[chunk, own, here]
+                do, o = grad_ref[chunk, own, start : start + 128], o_ref[chunk, own, here]
                 delta = jnp.sum(do.astype(f32) * o.astype(f32), axis=0, keepdims=True)
                 qt[h, :, sl] = jnp.concatenate([q_ref[own, sl], tail(lse_ref[h, chunk, :, here]), pad], axis=0)
                 dot[h, :, sl] = jnp.concatenate([do, tail(delta), pad], axis=0)
@@ -434,7 +435,7 @@
             out_ref[chunk, 2, own, here] = dvt[h, :, sl].astype(bf16)
 
 
-def attn_bwd(meta, scale, qkvt, grad, mixture, logsum, first, count, slot):
+def attn_bwd(meta, scale, qkvt, grad, mixture, logsum, first, count):
     rows = lambda a: pl.BlockSpec((count * HD, TOK), lambda i, b: ((LH * a + first) // count, 0))
     return pl.pallas_call(
         bwd_kernel,
@@ -447,7 +448,7 @@
                 rows(0),
                 rows(1),
                 rows(2),
-                pl.BlockSpec((PARTS, count * HD, ROWS), lambda i, b: (0, slot // count, 0)),
+                *[pl.BlockSpec((PARTS, count * HD, g.shape[2]), lambda i, b: (0, first // count, 0)) for g in grad],
                 pl.BlockSpec((PARTS, count * HD, ROWS), lambda i, b: (0, first // count, 0)),
                 pl.BlockSpec((count, PARTS, 1, ROWS), lambda i, b: (first // count, 0, 0, 0)),
             ],
@@ -459,31 +460,27 @@
         compiler_params=pltpu.CompilerParams(dimension_semantics=("arbitrary",), vmem_limit_bytes=60 << 20),
         cost_estimate=pl.CostEstimate(flops=count * 18 * 10**9, bytes_accessed=count * 8 << 20, transcendentals=0),
         name="attn_bwd",
-    )(meta, scale, qkvt, qkvt, qkvt, grad, mixture, logsum)
-
-
-def mlp_kernel(meta, head_ref, tail_ref, rows_ref, cot_ref, gain_ref, out_ref, up_ref, down_ref, fd_ref, fu_ref,
-               hidden_ref, inner_ref, middle_ref, grad_ref, g0_ref, g1_ref, keep_ref, send_ref, mixed, sums):
+    )(meta, scale, qkvt, qkvt, qkvt, *grad, mixture, logsum)
+
+
+def mlp_kernel(meta, mixed_ref, rows_ref, cot_ref, gain_ref, out_ref, up_ref, down_ref, fd_ref, fu_ref, *refs, first):
     step = pl.program_id(0)
-
-    @pl.when(step == 0)
-    def _():
-        sums[...] = jnp.zeros_like(sums)
-
-    @pl.when(step < 2)
-    def _():
-        mixed[...] = head_ref[...]
-
-    @pl.when(step == 2)
-    def _():
-        mixed[...] = tail_ref[...]
-
-    pos = meta[6] * ROWS + step * B + lax.broadcasted_iota(jnp.int32, (B, AR), 0)
+    if first:
+        hidden_ref, inner_ref, middle_ref, grad_ref, g_ref, keep_ref, send_ref, sums = refs[-8:]
+        sums[...] = refs[0][...]
+    else:
+        hidden_ref, inner_ref, middle_ref, grad_ref, g_ref, sums = refs
+
+        @pl.when(step == 0)
+        def _():
+            sums[...] = jnp.zeros_like(sums)
+
+    pos = meta[6] * ROWS + (first + step) * B + lax.broadcasted_iota(jnp.int32, (B, AR), 0)
     chosen = lax.broadcasted_iota(jnp.int32, (B, AR), 1) // RANK == token_adapter(pos, meta)
     choose = lambda x: jnp.where(chosen, x, 0.0).astype(bf16)
     gain = gain_ref[...]
 
-    middle = rows_ref[...].astype(f32) + nn(mixed[...].T, out_ref[...])
+    middle = rows_ref[...].astype(f32) + nn(mixed_ref[...].T, out_ref[...])
     middle_ref[...] = middle
     q = lax.rsqrt(jnp.mean(middle * middle, axis=1, keepdims=True) + EPSILON)
     normed = (middle * q * gain).astype(bf16)
@@ -507,55 +504,62 @@
     grad_ref[...] = grad_middle
     grad_mixed = nt(out_ref[...], grad_middle.astype(bf16)).astype(bf16)
     for s in range(PARTS):
-        g0_ref[s] = grad_mixed[2 * s * PW : (2 * s + 1) * PW]
-        g1_ref[s] = grad_mixed[(2 * s + 1) * PW : (2 * s + 2) * PW]
+        g_ref[s] = grad_mixed[s * WIDTH : (s + 1) * WIDTH]
 
     for n, (a, b) in enumerate(((spread_up, normed), (spread_down, hidden), (inner_up, grad_before), (inner_down, after))):
         sums[n] += nn(a.T, b)
 
-    @pl.when(step == 2)
-    def _():
+    if first:
         for ref, half in ((keep_ref, meta[7]), (send_ref, 1 - meta[7])):
             for n in range(2):
                 ref[n * AR : (n + 1) * AR, :] = sums[2 * half + n].astype(bf16)
 
 
-def mlp(meta, mixed_head, mixed_tail, rows, cotangent, gain, weights, flat_down, flat_up):
+def mlp(meta, mixed, rows, cotangent, gain, weights, flat_down, flat_up, first, sums=None, done=()):
     whole = lambda shape: pl.BlockSpec(shape, lambda i, m: (0,) * len(shape))
-    block = pl.BlockSpec((B, D), lambda i, m: (i, 0))
-    pair = pl.BlockSpec((PARTS, PW, B), lambda i, m: (0, 0, i))
+    block = lambda width: pl.BlockSpec((B, width), lambda i, m: (first + i, 0))
+    tokens = mixed.shape[1]
+    out_shape = [
+        jax.ShapeDtypeStruct((ROWS, D), bf16),
+        jax.ShapeDtypeStruct((ROWS, AR), bf16),
+        jax.ShapeDtypeStruct((ROWS, D), f32),
+        jax.ShapeDtypeStruct((ROWS, D), f32),
+        jax.ShapeDtypeStruct((PARTS, WIDTH, tokens), bf16),
+    ]
+    out_specs = [block(D), block(AR), block(D), block(D), pl.BlockSpec((PARTS, WIDTH, B), lambda i, m: (0, 0, i))]
+    if first:
+        out_shape += [jax.ShapeDtypeStruct((2 * AR, D), bf16)] * 2
+        out_specs += [whole((2 * AR, D))] * 2
+        extra, extra_specs = [sums, *done], [whole((4, AR, D))] + [pl.BlockSpec(memory_space=pl.ANY)] * 4
+        aliases, scratch = {11 + n: n for n in range(4)}, [pltpu.VMEM((4, AR, D), f32)]
+    else:
+        out_shape += [jax.ShapeDtypeStruct((4, AR, D), f32)]
+        out_specs += [whole((4, AR, D))]
+        extra, extra_specs, aliases, scratch = [], [], {}, []
     return pl.pallas_call(
-        mlp_kernel,
-        out_shape=[
-            jax.ShapeDtypeStruct((ROWS, D), bf16),
-            jax.ShapeDtypeStruct((ROWS, AR), bf16),
-            jax.ShapeDtypeStruct((ROWS, D), f32),
-            jax.ShapeDtypeStruct((ROWS, D), f32),
-            jax.ShapeDtypeStruct((PARTS, PW, ROWS), bf16),
-            jax.ShapeDtypeStruct((PARTS, PW, ROWS), bf16),
-            jax.ShapeDtypeStruct((2 * AR, D), bf16),
-            jax.ShapeDtypeStruct((2 * AR, D), bf16),
-        ],
+        functools.partial(mlp_kernel, first=first),
+        out_shape=out_shape,
         grid_spec=pltpu.PrefetchScalarGridSpec(
             num_scalar_prefetch=1,
-            grid=(ROWS // B,),
+            grid=(tokens // B,),
             in_specs=[
-                pl.BlockSpec((D, B), lambda i, m: (0, jnp.minimum(i, 1))),
-                whole((D, B)),
-                block,
-                block,
+                pl.BlockSpec((D, B), lambda i, m: (0, i)),
+                block(D),
+                block(D),
                 whole((1, D)),
                 *[pl.BlockSpec((D, D), lambda i, m, a=a: (0, a)) for a in range(3)],
                 whole((2, D, AR)),
                 whole((2, AR, D)),
-            ],
-            out_specs=[block, pl.BlockSpec((B, AR), lambda i, m: (i, 0)), block, block, pair, pair] + [whole((2 * AR, D))] * 2,
-            scratch_shapes=[pltpu.VMEM((D, B), bf16), pltpu.VMEM((4, AR, D), f32)],
+            ]
+            + extra_specs,
+            out_specs=out_specs,
+            scratch_shapes=scratch,
         ),
+        input_output_aliases=aliases,
         compiler_params=pltpu.CompilerParams(dimension_semantics=("arbitrary",), vmem_limit_bytes=60 << 20),
-        cost_estimate=pl.CostEstimate(flops=17 * 10**9, bytes_accessed=32 << 20, transcendentals=0),
+        cost_estimate=pl.CostEstimate(flops=tokens * 22 * 10**6, bytes_accessed=20 << 20, transcendentals=0),
         name="mlp",
-    )(meta, mixed_head, mixed_tail, rows, cotangent, gain, weights, weights, weights, flat_down, flat_up)
+    )(meta, mixed, rows, cotangent, gain, weights, weights, weights, flat_down, flat_up, *extra)
 
 
 def exchange(value):
@@ -667,28 +671,32 @@
     tail_mix, tail_log = attn_fwd(later, qkvt, 1)
     tail_sent, mixed_head = lax.optimization_barrier((tail_mix, mixed_head))
     mixed_tail = exchange(tail_sent)
-    mixture = jnp.concatenate([head_mix, tail_mix], axis=2)
-    logsum = jnp.concatenate([head_log, tail_log], axis=3)
-    mixture, logsum, up_mine, mixed_head = lax.optimization_barrier((mixture, logsum, up_mine, mixed_head))
-
-    hidden_low, inner_down, middle, grad_middle, grad_first_heads, grad_second_heads, mlp_keep, mlp_send = mlp(
-        meta, mixed_head.reshape(D, -1), mixed_tail.reshape(D, -1), rows, cotangent[0], gain_mlp[None, :],
-        weights_mlp, flat_down[2:], flat_up[2:],
+    up_mine, mixed_head = lax.optimization_barrier((up_mine, mixed_head))
+
+    shared = (rows, cotangent[0], gain_mlp[None, :], weights_mlp, flat_down[2:], flat_up[2:])
+    *done, grad_part, sums = mlp(meta, mixed_head.reshape(D, -1), *shared, 0)
+    grad_head = exchange(grad_part)
+    hidden_low, inner_down, middle, grad_middle, grad_part, mlp_keep, mlp_send = mlp(
+        meta, mixed_tail.reshape(D, -1), *shared, 2, sums, done
     )
-    grad_heads = [exchange(grad_first_heads), exchange(grad_second_heads)]
+    grad_part, grad_head = lax.optimization_barrier((grad_part, grad_head))
+    forward, grad_part = lax.optimization_barrier(((head_mix, tail_mix, head_log, tail_log), grad_part))
+    grad_heads = (grad_head, exchange(grad_part))
+    mixture = jnp.concatenate(forward[:2], axis=2)
+    logsum = jnp.concatenate(forward[2:], axis=3)
 
     mlp_total = sum_low(mlp_keep, swap(mlp_send, "fsdp", 1))
-    mlp_total, grad_heads[0] = lax.optimization_barrier((mlp_total, grad_heads[0]))
+    mlp_total, grad_heads = lax.optimization_barrier((mlp_total, grad_heads))
     mlp_total = scatter_heads(mlp_total)
     scale_column = scale_row[:, None]
     send_back = lambda g: exchange(g.reshape(PARTS, -1, ROWS)).reshape(g.shape)
     grads, arrived = [], []
-    grads.append(attn_bwd(meta, scale_column, qkvt, grad_heads[0], mixture, logsum, 0, 2, 0))
+    grads.append(attn_bwd(meta, scale_column, qkvt, grad_heads, mixture, logsum, 0, 2))
     mlp_total, grads[0] = lax.optimization_barrier((mlp_total, grads[0]))
     arrived.append(send_back(grads[0]))
     mlp_total = sum_far(mlp_total)
     meta, grads[0] = lax.optimization_barrier((meta, grads[0]))
-    grads.append(attn_bwd(meta, scale_column, qkvt, grad_heads[1], mixture, logsum, 2, 2, 0))
+    grads.append(attn_bwd(meta, scale_column, qkvt, grad_heads, mixture, logsum, 2, 2))
     mlp_total, grads[1] = lax.optimization_barrier((mlp_total, grads[1]))
     arrived.append(send_back(grads[1]))
 

time: 421 us -> 428 us (1.017)
  starting transfers between devices: 60.7 us -> 49.6 us
  Pallas kernels: 228 us -> 237 us
  waiting for transfers between devices: 71.2 us -> 79.2 us
    ppermute x24, starting transfers between devices: 36.8 us -> 25.8 us  [swap(): return lax.ppermute(value, axis, [(i, i ^ mask) for i in range(count)])]
    pallas_call x1 -> x2, Pallas kernels: 37.6 us -> 46 us  [mlp(): pl.pallas_call(functools.partial(mlp_kernel, first=first), out_shape=out_...]
    all_to_all x6, waiting for transfers between devices: 14.4 us -> 21.3 us  [exchange(): lax.all_to_all(value, 'heads', split_axis=0, concat_axis=0, tiled=True)]
    ppermute x24, waiting for transfers between devices: 51.3 us -> 57.2 us  [swap(): return lax.ppermute(value, axis, [(i, i ^ mask) for i in range(count)])]
    all_gather x1, waiting for transfers between devices: 5.54 us -> 0.61 us  [body(): weights_mine = lax.all_gather(weights_mine, 'fsdp', axis=0, tiled=True)]
  transfers between devices with their start and end apart: 33 -> 33, of which waited for: 12 -> 13; matrix products, arithmetic and copies ran while one was open for 7% -> 7% of each run, Pallas kernels for 54% -> 55%
where the time goes in v2:
time: 428 us; the launch traced here: 420 us
  Pallas kernels  237 us (55%)
  waiting for transfers between devices  79.2 us (19%)
  starting transfers between devices  49.6 us (12%)
  local copies, waits for them, and re-layouts  24.3 us (6%)
  between operations  14.5 us (3%)
  other arithmetic  8.69 us (2%)
  matrix products  6.71 us (2%)
    pallas_call x2, Pallas kernels, attn_bwd(): pl.pallas_call(bwd_kernel, out_shape=jax.ShapeDtypeStruct((PARTS, 3, coun...  71.7 us
    ppermute x24, waiting for transfers between devices, swap(): return lax.ppermute(value, axis, [(i, i ^ mask) for i in range(count)])  57.2 us
    pallas_call x2, Pallas kernels, attn_fwd(): pl.pallas_call(fwd_kernel, out_shape=(jax.ShapeDtypeStruct((PARTS, WIDTH,...  51.4 us
    pallas_call x2, Pallas kernels, mlp(): pl.pallas_call(functools.partial(mlp_kernel, first=first), out_shape=out_...  46 us
    pallas_call x4, Pallas kernels, qkv_project(): pl.pallas_call(qkv_kernel, out_shape=(jax.ShapeDtypeStruct((3 * WIDTH, TO...  32 us
    ppermute x24, starting transfers between devices, swap(): return lax.ppermute(value, axis, [(i, i ^ mask) for i in range(count)])  25.8 us
    all_to_all x6, starting transfers between devices, exchange(): lax.all_to_all(value, 'heads', split_axis=0, concat_axis=0, tiled=True)  23.7 us
    all_to_all x6, waiting for transfers between devices, exchange(): lax.all_to_all(value, 'heads', split_axis=0, concat_axis=0, tiled=True)  21.3 us
  transfers between devices with their start and end apart: 33, of which 13 were waited for; matrix products, arithmetic and copies ran while one was open for 7% of the time, Pallas kernels for 55%

profile of v2, /device:TPU:9, one launch (start us, length us, event | category | flops | bytes accessed | tf_op | source)
XLA Modules:
  0.0 419.7 jit_solution(17072038791601815438)
XLA Ops:
  22.7 15.0 %collective-permute-done.low_ref = bf16[384,1280]{1,0:T(8,128)(2,1)} collective-permute-done((bf16[384,1280]{1,0:T(8,128)(2,1)}, bf16[384,1280]{1,0:T(8,128)(2,1)}, u32[]{:S(2)}, u32[]{:S(2)}) %collective-permute-start) | collective-permute-done | bytes 983072 | tf_op jit(solution)/shard_map/ppermute | solution.py:571
  45.3 4.3 %copy.61 = bf16[1280,960]{0,1:T(8,128)(2,1)} copy(bf16[1280,960]{1,0:T(8,128)(2,1)} %all-gather.4.cloned.1.call-done) | data formatting | bytes 4915200 | tf_op jit(solution)/shard_map/all_gather | solution.py:649
  49.6 8.0 %qkv_project.4 = (bf16[960,3072]{1,0:T(8,128)(2,1)}, bf16[3072,1280]{1,0:T(8,128)(2,1)}, bf16[3072,256]{1,0:T(8,128)(2,1)}) custom-call(s32[8]{0:T(128)} %pad_add_fusion.meta, s32[1]{0:T(128)} %bitcast.16.first, bf16[768,1280]{1,0:T(8,128)(2,1)} %bitcast.53, bf16[768,1280]{1,0:T(8,128)(2,1)} %bitcast.54, f32[1,1280]{1,0:T(1,128)} %reshape.83.gain_ref.refs_6_, ...), custom_call_target="tpu_custom_call" | custom-call | flops 2390753280 | bytes 8388608 | tf_op jit(solution)/shard_map/qkv_project/pallas_call | solution.py:86
  57.8 8.0 %qkv_project.5 = (bf16[960,3072]{1,0:T(8,128)(2,1)}, bf16[3072,1280]{1,0:T(8,128)(2,1)}, bf16[3072,256]{1,0:T(8,128)(2,1)}) custom-call(s32[8]{0:T(128)} %pad_add_fusion.meta, s32[1]{0:T(128)} %bitcast.15.first, bf16[384,1280]{1,0:T(8,128)(2,1)} %collective-permute-done.5.low_ref, ...), custom_call_target="tpu_custom_call", output_to_operand_aliasing={{0}: (9, {}), {1}: (10, {}), {2}: (11, {})} | custom-call | flops 2390753280 | bytes 8388608 | tf_op jit(solution)/shard_map/qkv_project/pallas_call | solution.py:86
  65.8 8.0 %qkv_project.6 = (bf16[960,3072]{1,0:T(8,128)(2,1)}, bf16[3072,1280]{1,0:T(8,128)(2,1)}, bf16[3072,256]{1,0:T(8,128)(2,1)}) custom-call(s32[8]{0:T(128)} %pad_add_fusion.meta, s32[1]{0:T(128)} %bitcast.14.first, bf16[384,1280]{1,0:T(8,128)(2,1)} %collective-permute-done.low_ref, ...), custom_call_target="tpu_custom_call", output_to_operand_aliasing={{0}: (9, {}), {1}: (10, {}), {2}: (11, {})} | custom-call | flops 2390753280 | bytes 8388608 | tf_op jit(solution)/shard_map/qkv_project/pallas_call | solution.py:86
  73.8 5.0 %collective-permute-done.1.low_ref = bf16[384,1280]{1,0:T(8,128)(2,1)} collective-permute-done((bf16[384,1280]{1,0:T(8,128)(2,1)}, bf16[384,1280]{1,0:T(8,128)(2,1)}, u32[]{:S(2)}, u32[]{:S(2)}) %collective-permute-start.1) | collective-permute-done | bytes 983072 | tf_op jit(solution)/shard_map/ppermute | solution.py:571
  79.8 8.0 %qkv_project.7 = (bf16[960,3072]{1,0:T(8,128)(2,1)}, bf16[3072,1280]{1,0:T(8,128)(2,1)}, bf16[3072,256]{1,0:T(8,128)(2,1)}) custom-call(s32[8]{0:T(128)} %pad_add_fusion.meta, s32[1]{0:T(128)} %bitcast.5.first, bf16[384,1280]{1,0:T(8,128)(2,1)} %collective-permute-done.1.low_ref, ...), custom_call_target="tpu_custom_call", output_to_operand_aliasing={{0}: (9, {}), {1}: (10, {}), {2}: (11, {})} | custom-call | flops 2390753280 | bytes 8388608 | tf_op jit(solution)/shard_map/qkv_project/pallas_call | solution.py:86
  87.8 31.1 %attn_fwd.2 = (bf16[4,320,512]{2,1,0:T(8,128)(2,1)}, f32[4,4,1,512]{3,2,1,0:T(1,128)}) custom-call(s32[2]{0:T(128)} %copy-done.29, bf16[960,3072]{1,0:T(8,128)(2,1)} %get-tuple-element.90.q_ref.k_ref.v_ref, bf16[960,3072]{1,0:T(8,128)(2,1)} %get-tuple-element.90.q_ref.k_ref.v_ref, bf16[960,3072]{1,0:T(8,128)(2,1)} %get-tuple-element.90.q_ref.k_ref.v_ref), custom_call_target="tpu_custom_call" | custom-call | flops 25999998976 | bytes 5242880 | tf_op jit(solution)/shard_map/attn_fwd/pallas_call | solution.py:338
  118.9 3.8 all-to-all-start
  122.6 20.3 %attn_fwd.3 = (bf16[4,320,256]{2,1,0:T(8,128)(2,1)}, f32[4,4,1,256]{3,2,1,0:T(1,128)}) custom-call(s32[2]{0:T(128)} %copy-done.29, bf16[960,3072]{1,0:T(8,128)(2,1)} %get-tuple-element.90.q_ref.k_ref.v_ref, bf16[960,3072]{1,0:T(8,128)(2,1)} %get-tuple-element.90.q_ref.k_ref.v_ref, bf16[960,3072]{1,0:T(8,128)(2,1)} %get-tuple-element.90.q_ref.k_ref.v_ref), custom_call_target="tpu_custom_call" | custom-call | flops 12999999488 | bytes 5242880 | tf_op jit(solution)/shard_map/attn_fwd/pallas_call | solution.py:338
  144.1 3.6 all-to-all-start.1
  147.7 28.3 %mlp.2 = (bf16[768,1280]{1,0:T(8,128)(2,1)}, bf16[768,128]{1,0:T(8,128)(2,1)}, f32[768,1280]{1,0:T(8,128)}, f32[768,1280]{1,0:T(8,128)}, bf16[4,320,512]{2,1,0:T(8,128)(2,1)}, /*index=5*/f32[4,128,1280]{2,1,0:T(8,128)}) custom-call(s32[8]{0:T(128)} %pad_add_fusion.meta, bf16[1280,512]{1,0:T(8,128)(2,1)} %bitcast.74, bf16[768,1280]{1,0:T(8,128)(2,1)} %bitcast.55, ...), custom_call_target="tpu_custom_call" | custom-call | flops 11264000000 | bytes 20971520 | tf_op jit(solution)/shard_map/mlp/pallas_call | solution.py:539
  176.8 17.8 %mlp.3 = (bf16[768,1280]{1,0:T(8,128)(2,1)}, bf16[768,128]{1,0:T(8,128)(2,1)}, f32[768,1280]{1,0:T(8,128)}, f32[768,1280]{1,0:T(8,128)}, bf16[4,320,256]{2,1,0:T...) custom-call(s32[8]{0:T(128)} %pad_add_fusion.meta, ...), custom_call_target="tpu_custom_call", output_to_operand_aliasing={{0}: (11, {}), {1}: (12, {}), {2}: (13, {}), {3}: (14, {})} | custom-call | flops 5632000000 | bytes 20971520 | tf_op jit(solution)/shard_map/mlp/pallas_call | solution.py:539
  196.4 4.3 %all-to-all-start.2 = ((bf16[4,320,512]{2,1,0:T(8,128)(2,1)}), bf16[4,320,512]{2,1,0:T(8,128)(2,1)}, u32[]{:S(2)}, u32[]{:S(2)}) async-start(bf16[4,320,512]{2,1,0:T(8,128)(2,1)} %get-tuple-element.108), calls=%async_computation.2 | async-start | bytes 2621440 | tf_op jit(solution)/shard_map/all_to_all | solution.py:566
  202.8 14.4 %all-to-all-done.2.head_ref = bf16[4,320,512]{2,1,0:T(8,128)(2,1)} async-done(((bf16[4,320,512]{2,1,0:T(8,128)(2,1)}), bf16[4,320,512]{2,1,0:T(8,128)(2,1)}, u32[]{:S(2)}, u32[]{:S(2)}) %all-to-all-start.2) | async-done | bytes 1310752 | tf_op jit(solution)/shard_map/all_to_all | solution.py:566
  217.2 3.6 all-to-all-start.3
  222.9 6.9 %all-to-all-done.3.tail_ref = bf16[4,320,256]{2,1,0:T(8,128)(2,1)S(1)} async-done(((bf16[4,320,256]{2,1,0:T(8,128)(2,1)}), bf16[4,320,256]{2,1,0:T(8,128)(2,1)S(1)}, u32[]{:S(2)}, u32[]{:S(2)}) %all-to-all-start.3) | async-done | bytes 655392 | tf_op jit(solution)/shard_map/all_to_all | solution.py:566
  232.6 35.9 %attn_bwd.2.refs_0_ = bf16[4,3,160,768]{3,2,1,0:T(8,128)(2,1)} custom-call(s32[8]{0:T(128)} %pad_add_fusion.meta, f32[80,1]{1,0:T(8,128)} %copy.74.scale_ref, bf16[960,3072]{1,0:T(8,128)(2,1)} %get-tuple-element.90.q_ref.k_ref.v_ref, bf16[960,3072]{1,0:T(8,128)(2,1)} %get-tuple-element.90.q_ref.k_ref.v_ref, ...), custom_call_target="tpu_custom_call" | custom-call | flops 35999997952 | bytes 16777216 | tf_op jit(solution)/shard_map/attn_bwd/pallas_call | solution.py:440
  268.6 3.3 collective-permute-start.10
  271.9 2.5 collective-permute-start.11
  274.4 3.7 all-to-all-start.4
  278.1 35.8 %attn_bwd.3.refs_1_ = bf16[4,3,160,768]{3,2,1,0:T(8,128)(2,1)} custom-call(s32[8]{0:T(128)} %pad_add_fusion.meta, f32[80,1]{1,0:T(8,128)} %copy.74.scale_ref, bf16[960,3072]{1,0:T(8,128)(2,1)} %get-tuple-element.90.q_ref.k_ref.v_ref, bf16[960,3072]{1,0:T(8,128)(2,1)} %get-tuple-element.90.q_ref.k_ref.v_ref, ...), custom_call_target="tpu_custom_call" | custom-call | flops 35999997952 | bytes 16777216 | tf_op jit(solution)/shard_map/attn_bwd/pallas_call | solution.py:440
  317.3 4.8 %all-to-all-start.5 = ((bf16[4,480,768]{2,1,0:T(8,128)(2,1)}), bf16[4,480,768]{2,1,0:T(8,128)(2,1)}, u32[]{:S(2)}, u32[]{:S(2)}) async-start(bf16[4,480,768]{2,1,0:T(8,128)(2,1)} %bitcast.51), calls=%async_computation.5 | async-start | bytes 5898240 | tf_op jit(solution)/shard_map/all_to_all | solution.py:566
  322.1 10.3 %adapter_grads.1 = (bf16[160,1280]{1,0:T(8,128)(2,1)}, bf16[160,1280]{1,0:T(8,128)(2,1)}) custom-call(s32[8]{0:T(128)} %pad_add_fusion.meta, bf16[4,3,160,768]{3,2,1,0:T(8,128)(2,1)} %attn_bwd.2.refs_0_, bf16[4,3,160,768]{3,2,1,0:T(8,128)(2,1)} %attn_bwd.3.refs_1_, bf16[3072,1280]{1,0:T(8,128)(2,1)} %get-tuple-element.127.refs_2_, ...), custom_call_target="tpu_custom_call" | custom-call | flops 4026531840 | bytes 20971520 | tf_op jit(solution)/shard_map/adapter_grads/pallas_call | solution.py:148
  332.5 4.8 %fusion.2 = f32[768,1280]{1,0:T(8,128)S(1)} fusion(bf16[768,1280]{1,0:T(8,128)(2,1)S(1)} %copy-done.8, bf16[1280,3840]{1,0:T(8,128)(2,1)} %all-gather.6.cloned.1.call-done.out_ref.up_ref.down_ref), kind=kOutput, calls=%fused_computation.3 | convolution fusion | flops 2516582400 | bytes 9175040 | tf_op jit(solution)/shard_map/dot_general | solution.py:41
  342.3 15.7 %collective-permute-done.14 = bf16[32,1280]{1,0:T(8,128)(2,1)S(1)} collective-permute-done((bf16[32,1280]{1,0:T(8,128)(2,1)S(1)}, bf16[32,1280]{1,0:T(8,128)(2,1)S(1)}, u32[]{:S(2)}, u32[]{:S(2)}) %collective-permute-start.14) | collective-permute-done | bytes 81952 | tf_op jit(solution)/shard_map/ppermute | solution.py:571
  358.0 2.6 collective-permute-done.16
  366.5 8.3 %collective-permute-done.18 = bf16[64,1280]{1,0:T(8,128)(2,1)S(1)} collective-permute-done((bf16[64,1280]{1,0:T(8,128)(2,1)S(1)}, bf16[64,1280]{1,0:T(8,128)(2,1)S(1)}, u32[]{:S(2)}, u32[]{:S(2)}) %collective-permute-start.18) | collective-permute-done | bytes 163872 | tf_op jit(solution)/shard_map/ppermute | solution.py:571
  374.9 4.7 %collective-permute-done.19 = bf16[64,1280]{1,0:T(8,128)(2,1)S(1)} collective-permute-done((bf16[64,1280]{1,0:T(8,128)(2,1)S(1)}, bf16[64,1280]{1,0:T(8,128)(2,1)S(1)}, u32[]{:S(2)}, u32[]{:S(2)}) %collective-permute-start.19) | collective-permute-done | bytes 163872 | tf_op jit(solution)/shard_map/ppermute | solution.py:571
  382.4 19.8 %back_inputs.1 = f32[768,1280]{1,0:T(8,128)} custom-call(s32[8]{0:T(128)} %pad_add_fusion.meta, bf16[4,3,160,768]{3,2,1,0:T(8,128)(2,1)} %bitcast.58, bf16[4,3,160,768]{3,2,1,0:T(8,128)(2,1)} %bitcast.27.refs_1_, bf16[1280,3840]{1,0:T(8,128)(2,1)} %all-gather.8.cloned.1.call-done.refs_2_, bf16[2,128,1280]{2,1,0:T(8,128)(2,1)} %bitcast.69, ...), custom_call_target="tpu_custom_call" | custom-call | flops 7549747200 | bytes 25165824 | tf_op jit(solution)/shard_map/back_inputs/pallas_call | solution.py:210
  403.9 2.7 collective-permute-done.23.other_ref
  407.7 5.3 %assemble.1 = (f32[4,128,1280]{2,1,0:T(8,128)}, f32[4,128,1280]{2,1,0:T(8,128)}) custom-call(s32[8]{0:T(128)} %pad_add_fusion.meta, bf16[4,128,1280]{2,1,0:T(8,128)(2,1)} %copy-done.3, bf16[4,128,1280]{2,1,0:T(8,128)(2,1)} %copy-done.12), custom_call_target="tpu_custom_call" | custom-call | flops 1048576 | bytes 8388608 | tf_op jit(solution)/shard_map/assemble/pallas_call | solution.py:260
  (163 shorter events, 54.5 us)
Async XLA Ops:
  7.2 38.1 %all-gather.4.cloned.1.call-start = ((), (), s32[]{:S(2)}) async-start(), calls=%async_computation.6 | async-start | bytes 2949120 | tf_op jit(solution)/shard_map/all_gather | solution.py:649
  10.4 137.3 %all-gather.6.cloned.1.call-start = ((), (), s32[]{:S(2)}) async-start(), calls=%async_computation.7 | async-start | bytes 11059200 | tf_op jit(solution)/shard_map/all_gather | solution.py:650
  11.6 370.8 %all-gather.8.cloned.1.call-start = ((), (), s32[]{:S(2)}) async-start(), calls=%async_computation.8 | async-start | bytes 11059200 | tf_op jit(solution)/shard_map/all_gather | solution.py:651
  13.8 24.1 %collective-permute-start.2 = (bf16[384,1280]{1,0:T(8,128)(2,1)}, bf16[384,1280]{1,0:T(8,128)(2,1)}, u32[]{:S(2)}, u32[]{:S(2)}) collective-permute-start(bf16[384,1280]{1,0:T(8,128)(2,1)} %get-tuple-element.79), channel_id=1, source_target_pairs={{0,8},{8,0},{16,24},{24,16},{1,9},{9,1},{17,25},{25,17},{2,10},{10... | collective-permute-start | bytes 2949128 | tf_op jit(solution)/shard_map/ppermute | solution.py:571
  15.0 22.7 %collective-permute-start = (bf16[384,1280]{1,0:T(8,128)(2,1)}, bf16[384,1280]{1,0:T(8,128)(2,1)}, u32[]{:S(2)}, u32[]{:S(2)}) collective-permute-start(bf16[384,1280]{1,0:T(8,128)(2,1)} %get-tuple-element.80), channel_id=1, source_target_pairs={{0,16},{8,24},{16,0},{24,8},{1,17},{9,25},{17,1},{25,9},{2,18},{10... | collective-permute-start | bytes 2949128 | tf_op jit(solution)/shard_map/ppermute | solution.py:571
  17.6 40.2 %collective-permute-start.5 = (bf16[384,1280]{1,0:T(8,128)(2,1)}, bf16[384,1280]{1,0:T(8,128)(2,1)}, u32[]{:S(2)}, u32[]{:S(2)}) collective-permute-start(bf16[384,1280]{1,0:T(8,128)(2,1)} %get-tuple-element.80), channel_id=1, source_target_pairs={{0,8},{8,0},{16,24},{24,16},{1,9},{9,1},{17,25},{25,17},{2,10},{10... | collective-permute-start | bytes 2949128 | tf_op jit(solution)/shard_map/ppermute | solution.py:571
  17.9 47.9 %collective-permute-start.4 = (bf16[384,1280]{1,0:T(8,128)(2,1)}, bf16[384,1280]{1,0:T(8,128)(2,1)}, u32[]{:S(2)}, u32[]{:S(2)}) collective-permute-start(bf16[384,1280]{1,0:T(8,128)(2,1)} %get-tuple-element.79), channel_id=1, source_target_pairs={{0,16},{8,24},{16,0},{24,8},{1,17},{9,25},{17,1},{25,9},{2,18},{10... | collective-permute-start | bytes 2949128 | tf_op jit(solution)/shard_map/ppermute | solution.py:571
  37.7 41.2 %collective-permute-start.1 = (bf16[384,1280]{1,0:T(8,128)(2,1)}, bf16[384,1280]{1,0:T(8,128)(2,1)}, u32[]{:S(2)}, u32[]{:S(2)}) collective-permute-start(bf16[384,1280]{1,0:T(8,128)(2,1)} %collective-permute-done.low_ref), channel_id=1, source_target_pairs={{0,8},{8,0},{16,24},{24,16},{1,9},{9,1},{17,25},{25,17},{2,10},{10... | collective-permute-start | bytes 2949128 | tf_op jit(solution)/shard_map/ppermute | solution.py:571
  37.9 41.9 %collective-permute-start.3 = (bf16[384,1280]{1,0:T(8,128)(2,1)}, bf16[384,1280]{1,0:T(8,128)(2,1)}, u32[]{:S(2)}, u32[]{:S(2)}) collective-permute-start(bf16[384,1280]{1,0:T(8,128)(2,1)} %collective-permute-done.2.high_ref), channel_id=1, source_target_pairs={{0,16},{8,24},{16,0},{24,8},{1,17},{9,25},{17,1},{25,9},{2,18},{10... | collective-permute-start | bytes 2949128 | tf_op jit(solution)/shard_map/ppermute | solution.py:571
  118.9 24.1 %all-to-all-start = ((bf16[4,320,512]{2,1,0:T(8,128)(2,1)}), bf16[4,320,512]{2,1,0:T(8,128)(2,1)S(1)}, u32[]{:S(2)}, u32[]{:S(2)}) async-start(bf16[4,320,512]{2,1,0:T(8,128)(2,1)} %get-tuple-element.117), calls=%async_computation | async-start | bytes 2621440 | tf_op jit(solution)/shard_map/all_to_all | solution.py:566
  144.1 31.9 %all-to-all-start.1 = ((bf16[4,320,256]{2,1,0:T(8,128)(2,1)}), bf16[4,320,256]{2,1,0:T(8,128)(2,1)S(1)}, u32[]{:S(2)}, u32[]{:S(2)}) async-start(bf16[4,320,256]{2,1,0:T(8,128)(2,1)} %get-tuple-element.118), calls=%async_computation.1 | async-start | bytes 1310720 | tf_op jit(solution)/shard_map/all_to_all | solution.py:566
  194.6 7.0 %collective-permute-start.6 = (bf16[256,1280]{1,0:T(8,128)(2,1)}, bf16[256,1280]{1,0:T(8,128)(2,1)}, u32[]{:S(2)}, u32[]{:S(2)}) collective-permute-start(bf16[256,1280]{1,0:T(8,128)(2,1)} %get-tuple-element.106), channel_id=1, source_target_pairs={{0,1},{1,0},{2,3},{3,2},{4,5},{5,4},{6,7},{7,6},{8,9},{9,8},{10,11... | collective-permute-start | bytes 1966088 | tf_op jit(solution)/shard_map/ppermute | solution.py:571
  196.4 20.7 %all-to-all-start.2 = ((bf16[4,320,512]{2,1,0:T(8,128)(2,1)}), bf16[4,320,512]{2,1,0:T(8,128)(2,1)}, u32[]{:S(2)}, u32[]{:S(2)}) async-start(bf16[4,320,512]{2,1,0:T(8,128)(2,1)} %get-tuple-element.108), calls=%async_computation.2 | async-start | bytes 2621440 | tf_op jit(solution)/shard_map/all_to_all | solution.py:566
  217.2 12.6 %all-to-all-start.3 = ((bf16[4,320,256]{2,1,0:T(8,128)(2,1)}), bf16[4,320,256]{2,1,0:T(8,128)(2,1)S(1)}, u32[]{:S(2)}, u32[]{:S(2)}) async-start(bf16[4,320,256]{2,1,0:T(8,128)(2,1)} %get-tuple-element.113), calls=%async_computation.3 | async-start | bytes 1310720 | tf_op jit(solution)/shard_map/all_to_all | solution.py:566
  229.8 38.6 %collective-permute-start.7 = (bf16[64,1280]{1,0:T(8,128)(2,1)S(1)}, bf16[64,1280]{1,0:T(8,128)(2,1)S(1)}, u32[]{:S(2)}, u32[]{:S(2)}) collective-permute-start(bf16[64,1280]{1,0:T(8,128)(2,1)S(1)} %get-tuple-element.158), channel_id=1, source_target_pairs={{0,8},{8,0},{16,24},{24,16},{1,9},{9,1},{17,25},{25,17},{2,10},{10... | collective-permute-start | bytes 491528 | tf_op jit(solution)/shard_map/ppermute | solution.py:571
  230.6 37.8 %collective-permute-start.8 = (bf16[64,1280]{1,0:T(8,128)(2,1)S(1)}, bf16[64,1280]{1,0:T(8,128)(2,1)S(1)}, u32[]{:S(2)}, u32[]{:S(2)}) collective-permute-start(bf16[64,1280]{1,0:T(8,128)(2,1)S(1)} %get-tuple-element.160), channel_id=1, source_target_pairs={{0,16},{8,24},{16,0},{24,8},{1,17},{9,25},{17,1},{25,9},{2,18},{10... | collective-permute-start | bytes 491528 | tf_op jit(solution)/shard_map/ppermute | solution.py:571
  230.9 37.5 %collective-permute-start.9 = (bf16[64,1280]{1,0:T(8,128)(2,1)S(1)}, bf16[64,1280]{1,0:T(8,128)(2,1)S(1)}, u32[]{:S(2)}, u32[]{:S(2)}) collective-permute-start(bf16[64,1280]{1,0:T(8,128)(2,1)S(1)} %get-tuple-element.159), channel_id=1, source_target_pairs={{0,24},{8,16},{16,8},{24,0},{1,25},{9,17},{17,9},{25,1},{2,26},{10... | collective-permute-start | bytes 491528 | tf_op jit(solution)/shard_map/ppermute | solution.py:571
  268.6 45.4 %collective-permute-start.10 = (bf16[64,1280]{1,0:T(8,128)(2,1)S(1)}, bf16[64,1280]{1,0:T(8,128)(2,1)S(1)}, u32[]{:S(2)}, u32[]{:S(2)}) collective-permute-start(bf16[64,1280]{1,0:T(8,128)(2,1)S(1)} %add_convert_fusion.4), channel_id=1, source_target_pairs={{0,2},{1,3},{2,0},{3,1},{4,6},{5,7},{6,4},{7,5},{8,10},{9,11},{10,... | collective-permute-start | bytes 491528 | tf_op jit(solution)/shard_map/ppermute | solution.py:571
  271.9 42.1 %collective-permute-start.11 = (bf16[64,1280]{1,0:T(8,128)(2,1)S(1)}, bf16[64,1280]{1,0:T(8,128)(2,1)S(1)}, u32[]{:S(2)}, u32[]{:S(2)}) collective-permute-start(bf16[64,1280]{1,0:T(8,128)(2,1)S(1)} %add_convert_fusion.4), channel_id=1, source_target_pairs={{0,4},{1,5},{2,6},{3,7},{4,0},{5,1},{6,2},{7,3},{8,12},{9,13},{10,... | collective-permute-start | bytes 491528 | tf_op jit(solution)/shard_map/ppermute | solution.py:571
  274.4 40.2 %collective-permute-start.12 = (bf16[64,1280]{1,0:T(8,128)(2,1)S(1)}, bf16[64,1280]{1,0:T(8,128)(2,1)}, u32[]{:S(2)}, u32[]{:S(2)}) collective-permute-start(bf16[64,1280]{1,0:T(8,128)(2,1)S(1)} %add_convert_fusion.4), channel_id=1, source_target_pairs={{0,6},{1,7},{2,4},{3,5},{4,2},{5,3},{6,0},{7,1},{8,14},{9,15},{10,... | collective-permute-start | bytes 491528 | tf_op jit(solution)/shard_map/ppermute | solution.py:571
  274.4 41.3 %all-to-all-start.4 = ((bf16[4,480,768]{2,1,0:T(8,128)(2,1)}), bf16[4,480,768]{2,1,0:T(8,128)(2,1)S(1)}, u32[]{:S(2)}, u32[]{:S(2)}) async-start(bf16[4,480,768]{2,1,0:T(8,128)(2,1)} %bitcast.52), calls=%async_computation.4 | async-start | bytes 5898240 | tf_op jit(solution)/shard_map/all_to_all | solution.py:566
  317.3 43.4 %all-to-all-start.5 = ((bf16[4,480,768]{2,1,0:T(8,128)(2,1)}), bf16[4,480,768]{2,1,0:T(8,128)(2,1)}, u32[]{:S(2)}, u32[]{:S(2)}) async-start(bf16[4,480,768]{2,1,0:T(8,128)(2,1)} %bitcast.51), calls=%async_computation.5 | async-start | bytes 5898240 | tf_op jit(solution)/shard_map/all_to_all | solution.py:566
  332.4 4.8 %collective-permute-start.13 = (bf16[160,1280]{1,0:T(8,128)(2,1)}, bf16[160,1280]{1,0:T(8,128)(2,1)S(1)}, u32[]{:S(2)}, u32[]{:S(2)}) collective-permute-start(bf16[160,1280]{1,0:T(8,128)(2,1)} %get-tuple-element.132), channel_id=1, source_target_pairs={{0,1},{1,0},{2,3},{3,2},{4,5},{5,4},{6,7},{7,6},{8,9},{9,8},{10,11... | collective-permute-start | bytes 1228808 | tf_op jit(solution)/shard_map/ppermute | solution.py:571
  337.5 20.6 %collective-permute-start.14 = (bf16[32,1280]{1,0:T(8,128)(2,1)S(1)}, bf16[32,1280]{1,0:T(8,128)(2,1)S(1)}, u32[]{:S(2)}, u32[]{:S(2)}) collective-permute-start(bf16[32,1280]{1,0:T(8,128)(2,1)S(1)} %get-tuple-element.161), channel_id=1, source_target_pairs={{0,8},{8,0},{16,24},{24,16},{1,9},{9,1},{17,25},{25,17},{2,10},{10... | collective-permute-start | bytes 245768 | tf_op jit(solution)/shard_map/ppermute | solution.py:571
  339.1 18.9 %collective-permute-start.15 = (bf16[32,1280]{1,0:T(8,128)(2,1)S(1)}, bf16[32,1280]{1,0:T(8,128)(2,1)S(1)}, u32[]{:S(2)}, u32[]{:S(2)}) collective-permute-start(bf16[32,1280]{1,0:T(8,128)(2,1)S(1)} %get-tuple-element.163), channel_id=1, source_target_pairs={{0,16},{8,24},{16,0},{24,8},{1,17},{9,25},{17,1},{25,9},{2,18},{10... | collective-permute-start | bytes 245768 | tf_op jit(solution)/shard_map/ppermute | solution.py:571
  340.2 20.4 %collective-permute-start.16 = (bf16[32,1280]{1,0:T(8,128)(2,1)S(1)}, bf16[32,1280]{1,0:T(8,128)(2,1)S(1)}, u32[]{:S(2)}, u32[]{:S(2)}) collective-permute-start(bf16[32,1280]{1,0:T(8,128)(2,1)S(1)} %get-tuple-element.162), channel_id=1, source_target_pairs={{0,24},{8,16},{16,8},{24,0},{1,25},{9,17},{17,9},{25,1},{2,26},{10... | collective-permute-start | bytes 245768 | tf_op jit(solution)/shard_map/ppermute | solution.py:571
  360.7 5.8 %collective-permute-start.17 = (bf16[64,1280]{1,0:T(8,128)(2,1)S(1)}, bf16[64,1280]{1,0:T(8,128)(2,1)S(1)}, u32[]{:S(2)}, u32[]{:S(2)}) collective-permute-start(bf16[64,1280]{1,0:T(8,128)(2,1)S(1)} %pad_maximum_fusion.5), channel_id=1, source_target_pairs={{0,2},{1,3},{2,0},{3,1},{4,6},{5,7},{6,4},{7,5},{8,10},{9,11},{10,... | collective-permute-start | bytes 491528 | tf_op jit(solution)/shard_map/ppermute | solution.py:571
  362.1 12.7 %collective-permute-start.18 = (bf16[64,1280]{1,0:T(8,128)(2,1)S(1)}, bf16[64,1280]{1,0:T(8,128)(2,1)S(1)}, u32[]{:S(2)}, u32[]{:S(2)}) collective-permute-start(bf16[64,1280]{1,0:T(8,128)(2,1)S(1)} %pad_maximum_fusion.5), channel_id=1, source_target_pairs={{0,4},{1,5},{2,6},{3,7},{4,0},{5,1},{6,2},{7,3},{8,12},{9,13},{10,... | collective-permute-start | bytes 491528 | tf_op jit(solution)/shard_map/ppermute | solution.py:571
  364.3 15.2 %collective-permute-start.19 = (bf16[64,1280]{1,0:T(8,128)(2,1)S(1)}, bf16[64,1280]{1,0:T(8,128)(2,1)S(1)}, u32[]{:S(2)}, u32[]{:S(2)}) collective-permute-start(bf16[64,1280]{1,0:T(8,128)(2,1)S(1)} %pad_maximum_fusion.5), channel_id=1, source_target_pairs={{0,6},{1,7},{2,4},{3,5},{4,2},{5,3},{6,0},{7,1},{8,14},{9,15},{10,... | collective-permute-start | bytes 491528 | tf_op jit(solution)/shard_map/ppermute | solution.py:571
  379.7 22.5 %collective-permute-start.20 = (bf16[128,1280]{1,0:T(8,128)(2,1)S(1)}, bf16[128,1280]{1,0:T(8,128)(2,1)S(1)}, u32[]{:S(2)}, u32[]{:S(2)}) collective-permute-start(bf16[128,1280]{1,0:T(8,128)(2,1)S(1)} %constant_dynamic-update-slice_fusion.4), channel_id=1, source_target_pairs={{0,8},{8,0},{16,24},{24,16},{1,9},{9,1},{17,25},{25,17},{2,10},{10... | collective-permute-start | bytes 983048 | tf_op jit(solution)/shard_map/ppermute | solution.py:571
  380.0 22.2 %collective-permute-start.21 = (bf16[128,1280]{1,0:T(8,128)(2,1)S(1)}, bf16[128,1280]{1,0:T(8,128)(2,1)S(1)}, u32[]{:S(2)}, u32[]{:S(2)}) collective-permute-start(bf16[128,1280]{1,0:T(8,128)(2,1)S(1)} %constant_dynamic-update-slice_fusion.4), channel_id=1, source_target_pairs={{0,16},{8,24},{16,0},{24,8},{1,17},{9,25},{17,1},{25,9},{2,18},{10... | collective-permute-start | bytes 983048 | tf_op jit(solution)/shard_map/ppermute | solution.py:571
  380.3 22.0 %collective-permute-start.22 = (bf16[128,1280]{1,0:T(8,128)(2,1)S(1)}, bf16[128,1280]{1,0:T(8,128)(2,1)S(1)}, u32[]{:S(2)}, u32[]{:S(2)}) collective-permute-start(bf16[128,1280]{1,0:T(8,128)(2,1)S(1)} %constant_dynamic-update-slice_fusion.4), channel_id=1, source_target_pairs={{0,24},{8,16},{16,8},{24,0},{1,25},{9,17},{17,9},{25,1},{2,26},{10... | collective-permute-start | bytes 983048 | tf_op jit(solution)/shard_map/ppermute | solution.py:571
  (34 other events, 271.3 us)
Sparse Core Ops, SparseCore 0:
  10.5 34.7 all-gather.3
  47.5 90.7 all-gather.5
  140.0 92.3 all-gather.7

commit v3 on v1

--- a/solution.py
+++ b/solution.py
@@ -690,7 +690,6 @@
     meta, grads[0] = lax.optimization_barrier((meta, grads[0]))
     grads.append(attn_bwd(meta, scale_column, qkvt, grad_heads[1], mixture, logsum, 2, 2, 0))
     mlp_total, grads[1] = lax.optimization_barrier((mlp_total, grads[1]))
-    arrived.append(send_back(grads[1]))
 
     meta, arrived[0] = lax.optimization_barrier((meta, arrived[0]))
     keep, send = adapter_grads(meta, grads, normed_all, inner_all, up_mine)
@@ -698,9 +697,9 @@
     outputs = (middle + (nn(hidden_late, weights_mlp[:, 2 * D :]) + nn(inner_late, flat_up[3]))).astype(bf16)
     total = sum_low(keep, swap(send, "fsdp", 1))
     total = jnp.concatenate([scatter_heads(total[:AR]), total[AR:]])
-    total, arrived, outputs = lax.optimization_barrier((total, arrived, outputs))
-    total = sum_far(total)
-    meta, total = lax.optimization_barrier((meta, total))
+    total, sent = lax.optimization_barrier((total, grads[1]))
+    arrived.append(send_back(sent))
+    total, outputs = lax.optimization_barrier((sum_far(total), outputs))
     own = jnp.concatenate([total, mlp_total])
     pieces = [own] + [swap(own, "heads", m) for m in (1, 2, 3)]
     grad_inputs = back_inputs(meta, arrived, weights_all, flat_up[:2], down_pair, rows, gain_attn[None, :], grad_middle)

time: 421 us -> 421 us (level)
  the two profiles are of different devices: /device:TPU:9 before, /device:TPU:27 now
where the time goes in v3:
time: 421 us; the launch traced here: 413 us
  Pallas kernels  229 us (54%)
  starting transfers between devices  66.4 us (16%)
  waiting for transfers between devices  62.2 us (15%)
  local copies, waits for them, and re-layouts  23.4 us (6%)
  between operations  14.6 us (3%)
  other arithmetic  10.8 us (3%)
  matrix products  7.3 us (2%)
    pallas_call x2, Pallas kernels, attn_bwd(): pl.pallas_call(bwd_kernel, out_shape=jax.ShapeDtypeStruct((PARTS, 3, coun...  71.9 us
    pallas_call x2, Pallas kernels, attn_fwd(): pl.pallas_call(fwd_kernel, out_shape=(jax.ShapeDtypeStruct((PARTS, WIDTH,...  51.3 us
    ppermute x24, starting transfers between devices, swap(): return lax.ppermute(value, axis, [(i, i ^ mask) for i in range(count)])  41.7 us
    pallas_call x1, Pallas kernels, mlp(): pl.pallas_call(mlp_kernel, out_shape=[jax.ShapeDtypeStruct((ROWS, D), bf1...  37.6 us
    ppermute x24, waiting for transfers between devices, swap(): return lax.ppermute(value, axis, [(i, i ^ mask) for i in range(count)])  36.1 us
    pallas_call x4, Pallas kernels, qkv_project(): pl.pallas_call(qkv_kernel, out_shape=(jax.ShapeDtypeStruct((3 * WIDTH, TO...  32.2 us
    all_to_all x6, starting transfers between devices, exchange(): lax.all_to_all(value, 'heads', split_axis=0, concat_axis=0, tiled=True)  24.6 us
    all_to_all x6, waiting for transfers between devices, exchange(): lax.all_to_all(value, 'heads', split_axis=0, concat_axis=0, tiled=True)  21.9 us
  transfers between devices with their start and end apart: 33, of which 13 were waited for; matrix products, arithmetic and copies ran while one was open for 7% of the time, Pallas kernels for 54%

profile of v3, /device:TPU:27, one launch (start us, length us, event | category | flops | bytes accessed | tf_op | source)
XLA Modules:
  0.0 413.3 jit_solution(4807847975106724153)
XLA Ops:
  22.9 13.8 %collective-permute-done.low_ref = bf16[384,1280]{1,0:T(8,128)(2,1)} collective-permute-done((bf16[384,1280]{1,0:T(8,128)(2,1)}, bf16[384,1280]{1,0:T(8,128)(2,1)}, u32[]{:S(2)}, u32[]{:S(2)}) %collective-permute-start) | collective-permute-done | bytes 983072 | tf_op jit(solution)/shard_map/ppermute | solution.py:567
  39.7 4.1 all-gather.4.cloned.1.call-done
  43.8 4.3 %copy.56 = bf16[1280,960]{0,1:T(8,128)(2,1)} copy(bf16[1280,960]{1,0:T(8,128)(2,1)} %all-gather.4.cloned.1.call-done) | data formatting | bytes 4915200 | tf_op jit(solution)/shard_map/all_gather | solution.py:645
  48.1 8.0 %qkv_project.4 = (bf16[960,3072]{1,0:T(8,128)(2,1)}, bf16[3072,1280]{1,0:T(8,128)(2,1)}, bf16[3072,256]{1,0:T(8,128)(2,1)}) custom-call(s32[8]{0:T(128)} %pad_add_fusion.meta, s32[1]{0:T(128)} %bitcast.16.first, bf16[768,1280]{1,0:T(8,128)(2,1)} %bitcast.57, bf16[768,1280]{1,0:T(8,128)(2,1)} %bitcast.58, f32[1,1280]{1,0:T(1,128)} %reshape.83.gain_ref.refs_6_, ...), custom_call_target="tpu_custom_call" | custom-call | flops 2390753280 | bytes 8388608 | tf_op jit(solution)/shard_map/qkv_project/pallas_call | solution.py:84
  57.8 8.0 %qkv_project.5 = (bf16[960,3072]{1,0:T(8,128)(2,1)}, bf16[3072,1280]{1,0:T(8,128)(2,1)}, bf16[3072,256]{1,0:T(8,128)(2,1)}) custom-call(s32[8]{0:T(128)} %pad_add_fusion.meta, s32[1]{0:T(128)} %bitcast.15.first, bf16[384,1280]{1,0:T(8,128)(2,1)} %collective-permute-done.5.low_ref, ...), custom_call_target="tpu_custom_call", output_to_operand_aliasing={{0}: (9, {}), {1}: (10, {}), {2}: (11, {})} | custom-call | flops 2390753280 | bytes 8388608 | tf_op jit(solution)/shard_map/qkv_project/pallas_call | solution.py:84
  65.8 8.1 %qkv_project.6 = (bf16[960,3072]{1,0:T(8,128)(2,1)}, bf16[3072,1280]{1,0:T(8,128)(2,1)}, bf16[3072,256]{1,0:T(8,128)(2,1)}) custom-call(s32[8]{0:T(128)} %pad_add_fusion.meta, s32[1]{0:T(128)} %bitcast.14.first, bf16[384,1280]{1,0:T(8,128)(2,1)} %collective-permute-done.low_ref, ...), custom_call_target="tpu_custom_call", output_to_operand_aliasing={{0}: (9, {}), {1}: (10, {}), {2}: (11, {})} | custom-call | flops 2390753280 | bytes 8388608 | tf_op jit(solution)/shard_map/qkv_project/pallas_call | solution.py:84
  73.9 4.9 %collective-permute-done.1.low_ref = bf16[384,1280]{1,0:T(8,128)(2,1)S(1)} collective-permute-done((bf16[384,1280]{1,0:T(8,128)(2,1)}, bf16[384,1280]{1,0:T(8,128)(2,1)S(1)}, u32[]{:S(2)}, u32[]{:S(2)}) %collective-permute-start.1) | collective-permute-done | bytes 983072 | tf_op jit(solution)/shard_map/ppermute | solution.py:567
  79.8 8.0 %qkv_project.7 = (bf16[960,3072]{1,0:T(8,128)(2,1)}, bf16[3072,1280]{1,0:T(8,128)(2,1)}, bf16[3072,256]{1,0:T(8,128)(2,1)}) custom-call(s32[8]{0:T(128)} %pad_add_fusion.meta, s32[1]{0:T(128)} %bitcast.5.first, bf16[384,1280]{1,0:T(8,128)(2,1)} %copy-done.15, ...), custom_call_target="tpu_custom_call", output_to_operand_aliasing={{0}: (9, {}), {1}: (10, {}), {2}: (11, {})} | custom-call | flops 2390753280 | bytes 8388608 | tf_op jit(solution)/shard_map/qkv_project/pallas_call | solution.py:84
  87.8 31.0 %attn_fwd.2 = (bf16[4,320,512]{2,1,0:T(8,128)(2,1)}, f32[4,4,1,512]{3,2,1,0:T(1,128)}) custom-call(s32[2]{0:T(128)} %copy-done.30, bf16[960,3072]{1,0:T(8,128)(2,1)} %get-tuple-element.77.q_ref.k_ref.v_ref, bf16[960,3072]{1,0:T(8,128)(2,1)} %get-tuple-element.77.q_ref.k_ref.v_ref, bf16[960,3072]{1,0:T(8,128)(2,1)} %get-tuple-element.77.q_ref.k_ref.v_ref), custom_call_target="tpu_custom_call" | custom-call | flops 25999998976 | bytes 5242880 | tf_op jit(solution)/shard_map/attn_fwd/pallas_call | solution.py:336
  118.8 3.9 all-to-all-start
  122.7 20.4 %attn_fwd.3 = (bf16[4,320,256]{2,1,0:T(8,128)(2,1)}, f32[4,4,1,256]{3,2,1,0:T(1,128)}) custom-call(s32[2]{0:T(128)} %copy-done.30, bf16[960,3072]{1,0:T(8,128)(2,1)} %get-tuple-element.77.q_ref.k_ref.v_ref, bf16[960,3072]{1,0:T(8,128)(2,1)} %get-tuple-element.77.q_ref.k_ref.v_ref, bf16[960,3072]{1,0:T(8,128)(2,1)} %get-tuple-element.77.q_ref.k_ref.v_ref), custom_call_target="tpu_custom_call" | custom-call | flops 12999999488 | bytes 5242880 | tf_op jit(solution)/shard_map/attn_fwd/pallas_call | solution.py:336
  144.2 4.3 %all-to-all-start.1 = ((bf16[4,320,256]{2,1,0:T(8,128)(2,1)}), bf16[4,320,256]{2,1,0:T(8,128)(2,1)}, u32[]{:S(2)}, u32[]{:S(2)}) async-start(bf16[4,320,256]{2,1,0:T(8,128)(2,1)} %get-tuple-element.86), calls=%async_computation.1 | async-start | bytes 1310720 | tf_op jit(solution)/shard_map/all_to_all | solution.py:562
  154.7 37.6 %mlp.1 = (bf16[768,1280]{1,0:T(8,128)(2,1)}, bf16[768,128]{1,0:T(8,128)(2,1)}, f32[768,1280]{1,0:T(8,128)}, f32[768,1280]{1,0:T(8,128)}, bf16[4,160,768]{2,1,0:T...) custom-call(s32[8]{0:T(128)} %pad_add_fusion.meta, ...), custom_call_target="tpu_custom_call" | custom-call | flops 16999999488 | bytes 33554432 | tf_op jit(solution)/shard_map/mlp/pallas_call | solution.py:527
  192.4 5.5 %collective-permute-start.6 = (bf16[256,1280]{1,0:T(8,128)(2,1)}, bf16[256,1280]{1,0:T(8,128)(2,1)S(1)}, u32[]{:S(2)}, u32[]{:S(2)}) collective-permute-start(bf16[256,1280]{1,0:T(8,128)(2,1)} %get-tuple-element.90), channel_id=1, source_target_pairs={{0,1},{1,0},{2,3},{3,2},{4,5},{5,4},{6,7},{7,6},{8,9},{9,8},{10,11... | collective-permute-start | bytes 1966088 | tf_op jit(solution)/shard_map/ppermute | solution.py:567
  197.9 3.8 all-to-all-start.2
  202.6 11.8 %all-to-all-done.2.do_ref = bf16[4,160,768]{2,1,0:T(8,128)(2,1)S(1)} async-done(((bf16[4,160,768]{2,1,0:T(8,128)(2,1)}), bf16[4,160,768]{2,1,0:T(8,128)(2,1)S(1)}, u32[]{:S(2)}, u32[]{:S(2)}) %all-to-all-start.2) | async-done | bytes 983072 | tf_op jit(solution)/shard_map/all_to_all | solution.py:562
  214.4 4.0 all-to-all-start.4
  221.2 35.9 %attn_bwd.2.refs_0_ = bf16[4,3,160,768]{3,2,1,0:T(8,128)(2,1)} custom-call(s32[8]{0:T(128)} %pad_add_fusion.meta, f32[80,1]{1,0:T(8,128)} %copy.68.scale_ref, bf16[960,3072]{1,0:T(8,128)(2,1)} %get-tuple-element.77.q_ref.k_ref.v_ref, bf16[960,3072]{1,0:T(8,128)(2,1)} %get-tuple-element.77.q_ref.k_ref.v_ref, ...), custom_call_target="tpu_custom_call" | custom-call | flops 35999997952 | bytes 16777216 | tf_op jit(solution)/shard_map/attn_bwd/pallas_call | solution.py:439
  257.2 4.5 %collective-permute-start.10 = (bf16[64,1280]{1,0:T(8,128)(2,1)S(1)}, bf16[64,1280]{1,0:T(8,128)(2,1)S(1)}, u32[]{:S(2)}, u32[]{:S(2)}) collective-permute-start(bf16[64,1280]{1,0:T(8,128)(2,1)S(1)} %add_convert_fusion.4), channel_id=1, source_target_pairs={{0,2},{1,3},{2,0},{3,1},{4,6},{5,7},{6,4},{7,5},{8,10},{9,11},{10,... | collective-permute-start | bytes 491528 | tf_op jit(solution)/shard_map/ppermute | solution.py:567
  264.9 3.7 all-to-all-start.3
  268.6 35.9 %attn_bwd.3.refs_1_ = bf16[4,3,160,768]{3,2,1,0:T(8,128)(2,1)} custom-call(s32[8]{0:T(128)} %pad_add_fusion.meta, f32[80,1]{1,0:T(8,128)} %copy.68.scale_ref, bf16[960,3072]{1,0:T(8,128)(2,1)} %get-tuple-element.77.q_ref.k_ref.v_ref, bf16[960,3072]{1,0:T(8,128)(2,1)} %get-tuple-element.77.q_ref.k_ref.v_ref, ...), custom_call_target="tpu_custom_call" | custom-call | flops 35999997952 | bytes 16777216 | tf_op jit(solution)/shard_map/attn_bwd/pallas_call | solution.py:439
  306.3 10.5 %adapter_grads.1 = (bf16[160,1280]{1,0:T(8,128)(2,1)}, bf16[160,1280]{1,0:T(8,128)(2,1)}) custom-call(s32[8]{0:T(128)} %pad_add_fusion.meta, bf16[4,3,160,768]{3,2,1,0:T(8,128)(2,1)} %attn_bwd.2.refs_0_, bf16[4,3,160,768]{3,2,1,0:T(8,128)(2,1)} %attn_bwd.3.refs_1_, bf16[3072,1280]{1,0:T(8,128)(2,1)} %get-tuple-element.103.refs_2_, ...), custom_call_target="tpu_custom_call" | custom-call | flops 4026531840 | bytes 20971520 | tf_op jit(solution)/shard_map/adapter_grads/pallas_call | solution.py:146
  316.8 6.8 %collective-permute-start.13 = (bf16[160,1280]{1,0:T(8,128)(2,1)}, bf16[160,1280]{1,0:T(8,128)(2,1)S(1)}, u32[]{:S(2)}, u32[]{:S(2)}) collective-permute-start(bf16[160,1280]{1,0:T(8,128)(2,1)} %get-tuple-element.108), channel_id=1, source_target_pairs={{0,1},{1,0},{2,3},{3,2},{4,5},{5,4},{6,7},{7,6},{8,9},{9,8},{10,11... | collective-permute-start | bytes 1228808 | tf_op jit(solution)/shard_map/ppermute | solution.py:567
  332.5 4.8 %all-to-all-start.5 = ((bf16[4,480,768]{2,1,0:T(8,128)(2,1)}), bf16[4,480,768]{2,1,0:T(8,128)(2,1)S(1)}, u32[]{:S(2)}, u32[]{:S(2)}) async-start(bf16[4,480,768]{2,1,0:T(8,128)(2,1)} %bitcast.28), calls=%async_computation.5 | async-start | bytes 5898240 | tf_op jit(solution)/shard_map/all_to_all | solution.py:562
  337.3 5.4 %fusion.2 = f32[768,1280]{1,0:T(8,128)S(1)} fusion(bf16[768,1280]{1,0:T(8,128)(2,1)} %get-tuple-element.111, bf16[1280,3840]{1,0:T(8,128)(2,1)} %all-gather.6.cloned.1.call-done.out_ref.up_ref.down_ref), kind=kOutput, calls=%fused_computation.3 | convolution fusion | flops 2516582400 | bytes 9175040 | tf_op jit(solution)/shard_map/dot_general | solution.py:39
  343.2 3.2 collective-permute-start.19
  348.3 8.2 %collective-permute-done.18 = bf16[64,1280]{1,0:T(8,128)(2,1)S(1)} collective-permute-done((bf16[64,1280]{1,0:T(8,128)(2,1)S(1)}, bf16[64,1280]{1,0:T(8,128)(2,1)S(1)}, u32[]{:S(2)}, u32[]{:S(2)}) %collective-permute-start.18) | collective-permute-done | bytes 163872 | tf_op jit(solution)/shard_map/ppermute | solution.py:567
  359.3 9.7 %all-to-all-done.5 = bf16[4,480,768]{2,1,0:T(8,128)(2,1)S(1)} async-done(((bf16[4,480,768]{2,1,0:T(8,128)(2,1)}), bf16[4,480,768]{2,1,0:T(8,128)(2,1)S(1)}, u32[]{:S(2)}, u32[]{:S(2)}) %all-to-all-start.5) | async-done | bytes 2949152 | tf_op jit(solution)/shard_map/all_to_all | solution.py:562
  370.6 19.8 %back_inputs.1 = f32[768,1280]{1,0:T(8,128)} custom-call(s32[8]{0:T(128)} %pad_add_fusion.meta, bf16[4,3,160,768]{3,2,1,0:T(8,128)(2,1)} %bitcast.52, bf16[4,3,160,768]{3,2,1,0:T(8,128)(2,1)} %bitcast.53, bf16[1280,3840]{1,0:T(8,128)(2,1)} %all-gather.8.cloned.1.call-done.refs_2_, bf16[2,128,1280]{2,1,0:T(8,128)(2,1)} %bitcast.63, ...), custom_call_target="tpu_custom_call" | custom-call | flops 7549747200 | bytes 25165824 | tf_op jit(solution)/shard_map/back_inputs/pallas_call | solution.py:208
  391.7 5.5 %collective-permute-start.23 = (bf16[4,128,1280]{2,1,0:T(8,128)(2,1)S(1)}, bf16[4,128,1280]{2,1,0:T(8,128)(2,1)S(1)}, u32[]{:S(2)}, u32[]{:S(2)}) collective-permute-start(bf16[4,128,1280]{2,1,0:T(8,128)(2,1)S(1)} %pad_maximum_fusion.1.own_ref), channel_id=1, source_target_pairs={{0,1},{1,0},{2,3},{3,2},{4,5},{5,4},{6,7},{7,6},{8,9},{9,8},{10,11... | collective-permute-start | bytes 3932168 | tf_op jit(solution)/shard_map/ppermute | solution.py:567
  397.3 2.7 collective-permute-done.23.other_ref
  401.0 5.3 %assemble.1 = (f32[4,128,1280]{2,1,0:T(8,128)}, f32[4,128,1280]{2,1,0:T(8,128)}) custom-call(s32[8]{0:T(128)} %pad_add_fusion.meta, bf16[4,128,1280]{2,1,0:T(8,128)(2,1)} %copy-done, bf16[4,128,1280]{2,1,0:T(8,128)(2,1)} %copy-done.11), custom_call_target="tpu_custom_call" | custom-call | flops 1048576 | bytes 8388608 | tf_op jit(solution)/shard_map/assemble/pallas_call | solution.py:258
  (162 shorter events, 55.1 us)
Async XLA Ops:
  7.2 36.6 %all-gather.4.cloned.1.call-start = ((), (), s32[]{:S(2)}) async-start(), calls=%async_computation.6 | async-start | bytes 2949120 | tf_op jit(solution)/shard_map/all_gather | solution.py:645
  10.4 144.3 %all-gather.6.cloned.1.call-start = ((), (), s32[]{:S(2)}) async-start(), calls=%async_computation.7 | async-start | bytes 11059200 | tf_op jit(solution)/shard_map/all_gather | solution.py:646
  11.6 347.7 %all-gather.8.cloned.1.call-start = ((), (), s32[]{:S(2)}) async-start(), calls=%async_computation.8 | async-start | bytes 11059200 | tf_op jit(solution)/shard_map/all_gather | solution.py:647
  13.7 24.1 %collective-permute-start.2 = (bf16[384,1280]{1,0:T(8,128)(2,1)}, bf16[384,1280]{1,0:T(8,128)(2,1)S(1)}, u32[]{:S(2)}, u32[]{:S(2)}) collective-permute-start(bf16[384,1280]{1,0:T(8,128)(2,1)} %get-tuple-element.66), channel_id=1, source_target_pairs={{0,8},{8,0},{16,24},{24,16},{1,9},{9,1},{17,25},{25,17},{2,10},{10... | collective-permute-start | bytes 2949128 | tf_op jit(solution)/shard_map/ppermute | solution.py:567
  14.0 22.7 %collective-permute-start = (bf16[384,1280]{1,0:T(8,128)(2,1)}, bf16[384,1280]{1,0:T(8,128)(2,1)}, u32[]{:S(2)}, u32[]{:S(2)}) collective-permute-start(bf16[384,1280]{1,0:T(8,128)(2,1)} %get-tuple-element.67), channel_id=1, source_target_pairs={{0,16},{8,24},{16,0},{24,8},{1,17},{9,25},{17,1},{25,9},{2,18},{10... | collective-permute-start | bytes 2949128 | tf_op jit(solution)/shard_map/ppermute | solution.py:567
  16.7 41.1 %collective-permute-start.5 = (bf16[384,1280]{1,0:T(8,128)(2,1)}, bf16[384,1280]{1,0:T(8,128)(2,1)}, u32[]{:S(2)}, u32[]{:S(2)}) collective-permute-start(bf16[384,1280]{1,0:T(8,128)(2,1)} %get-tuple-element.67), channel_id=1, source_target_pairs={{0,8},{8,0},{16,24},{24,16},{1,9},{9,1},{17,25},{25,17},{2,10},{10... | collective-permute-start | bytes 2949128 | tf_op jit(solution)/shard_map/ppermute | solution.py:567
  17.8 47.9 %collective-permute-start.4 = (bf16[384,1280]{1,0:T(8,128)(2,1)}, bf16[384,1280]{1,0:T(8,128)(2,1)}, u32[]{:S(2)}, u32[]{:S(2)}) collective-permute-start(bf16[384,1280]{1,0:T(8,128)(2,1)} %get-tuple-element.66), channel_id=1, source_target_pairs={{0,16},{8,24},{16,0},{24,8},{1,17},{9,25},{17,1},{25,9},{2,18},{10... | collective-permute-start | bytes 2949128 | tf_op jit(solution)/shard_map/ppermute | solution.py:567
  36.7 42.2 %collective-permute-start.1 = (bf16[384,1280]{1,0:T(8,128)(2,1)}, bf16[384,1280]{1,0:T(8,128)(2,1)S(1)}, u32[]{:S(2)}, u32[]{:S(2)}) collective-permute-start(bf16[384,1280]{1,0:T(8,128)(2,1)} %collective-permute-done.low_ref), channel_id=1, source_target_pairs={{0,8},{8,0},{16,24},{24,16},{1,9},{9,1},{17,25},{25,17},{2,10},{10... | collective-permute-start | bytes 2949128 | tf_op jit(solution)/shard_map/ppermute | solution.py:567
  37.9 40.9 %collective-permute-start.3 = (bf16[384,1280]{1,0:T(8,128)(2,1)S(1)}, bf16[384,1280]{1,0:T(8,128)(2,1)}, u32[]{:S(2)}, u32[]{:S(2)}) collective-permute-start(bf16[384,1280]{1,0:T(8,128)(2,1)S(1)} %collective-permute-done.2.high_ref), channel_id=1, source_target_pairs={{0,16},{8,24},{16,0},{24,8},{1,17},{9,25},{17,1},{25,9},{2,18},{10... | collective-permute-start | bytes 2949128 | tf_op jit(solution)/shard_map/ppermute | solution.py:567
  118.8 24.3 %all-to-all-start = ((bf16[4,320,512]{2,1,0:T(8,128)(2,1)}), bf16[4,320,512]{2,1,0:T(8,128)(2,1)S(1)}, u32[]{:S(2)}, u32[]{:S(2)}) async-start(bf16[4,320,512]{2,1,0:T(8,128)(2,1)} %get-tuple-element.78), calls=%async_computation | async-start | bytes 2621440 | tf_op jit(solution)/shard_map/all_to_all | solution.py:562
  144.2 10.6 %all-to-all-start.1 = ((bf16[4,320,256]{2,1,0:T(8,128)(2,1)}), bf16[4,320,256]{2,1,0:T(8,128)(2,1)}, u32[]{:S(2)}, u32[]{:S(2)}) async-start(bf16[4,320,256]{2,1,0:T(8,128)(2,1)} %get-tuple-element.86), calls=%async_computation.1 | async-start | bytes 1310720 | tf_op jit(solution)/shard_map/all_to_all | solution.py:562
  192.4 10.1 %collective-permute-start.6 = (bf16[256,1280]{1,0:T(8,128)(2,1)}, bf16[256,1280]{1,0:T(8,128)(2,1)S(1)}, u32[]{:S(2)}, u32[]{:S(2)}) collective-permute-start(bf16[256,1280]{1,0:T(8,128)(2,1)} %get-tuple-element.90), channel_id=1, source_target_pairs={{0,1},{1,0},{2,3},{3,2},{4,5},{5,4},{6,7},{7,6},{8,9},{9,8},{10,11... | collective-permute-start | bytes 1966088 | tf_op jit(solution)/shard_map/ppermute | solution.py:567
  197.9 16.5 %all-to-all-start.2 = ((bf16[4,160,768]{2,1,0:T(8,128)(2,1)}), bf16[4,160,768]{2,1,0:T(8,128)(2,1)S(1)}, u32[]{:S(2)}, u32[]{:S(2)}) async-start(bf16[4,160,768]{2,1,0:T(8,128)(2,1)} %get-tuple-element.91), calls=%async_computation.2 | async-start | bytes 1966080 | tf_op jit(solution)/shard_map/all_to_all | solution.py:562
  214.4 49.5 %all-to-all-start.4 = ((bf16[4,160,768]{2,1,0:T(8,128)(2,1)}), bf16[4,160,768]{2,1,0:T(8,128)(2,1)S(1)}, u32[]{:S(2)}, u32[]{:S(2)}) async-start(bf16[4,160,768]{2,1,0:T(8,128)(2,1)} %get-tuple-element.101), calls=%async_computation.4 | async-start | bytes 1966080 | tf_op jit(solution)/shard_map/all_to_all | solution.py:562
  218.5 38.7 %collective-permute-start.7 = (bf16[64,1280]{1,0:T(8,128)(2,1)S(1)}, bf16[64,1280]{1,0:T(8,128)(2,1)S(1)}, u32[]{:S(2)}, u32[]{:S(2)}) collective-permute-start(bf16[64,1280]{1,0:T(8,128)(2,1)S(1)} %get-tuple-element.132), channel_id=1, source_target_pairs={{0,8},{8,0},{16,24},{24,16},{1,9},{9,1},{17,25},{25,17},{2,10},{10... | collective-permute-start | bytes 491528 | tf_op jit(solution)/shard_map/ppermute | solution.py:567
  218.6 38.6 %collective-permute-start.8 = (bf16[64,1280]{1,0:T(8,128)(2,1)S(1)}, bf16[64,1280]{1,0:T(8,128)(2,1)S(1)}, u32[]{:S(2)}, u32[]{:S(2)}) collective-permute-start(bf16[64,1280]{1,0:T(8,128)(2,1)S(1)} %get-tuple-element.134), channel_id=1, source_target_pairs={{0,16},{8,24},{16,0},{24,8},{1,17},{9,25},{17,1},{25,9},{2,18},{10... | collective-permute-start | bytes 491528 | tf_op jit(solution)/shard_map/ppermute | solution.py:567
  220.0 37.1 %collective-permute-start.9 = (bf16[64,1280]{1,0:T(8,128)(2,1)S(1)}, bf16[64,1280]{1,0:T(8,128)(2,1)S(1)}, u32[]{:S(2)}, u32[]{:S(2)}) collective-permute-start(bf16[64,1280]{1,0:T(8,128)(2,1)S(1)} %get-tuple-element.133), channel_id=1, source_target_pairs={{0,24},{8,16},{16,8},{24,0},{1,25},{9,17},{17,9},{25,1},{2,26},{10... | collective-permute-start | bytes 491528 | tf_op jit(solution)/shard_map/ppermute | solution.py:567
  257.2 47.3 %collective-permute-start.10 = (bf16[64,1280]{1,0:T(8,128)(2,1)S(1)}, bf16[64,1280]{1,0:T(8,128)(2,1)S(1)}, u32[]{:S(2)}, u32[]{:S(2)}) collective-permute-start(bf16[64,1280]{1,0:T(8,128)(2,1)S(1)} %add_convert_fusion.4), channel_id=1, source_target_pairs={{0,2},{1,3},{2,0},{3,1},{4,6},{5,7},{6,4},{7,5},{8,10},{9,11},{10,... | collective-permute-start | bytes 491528 | tf_op jit(solution)/shard_map/ppermute | solution.py:567
  261.7 42.8 %collective-permute-start.11 = (bf16[64,1280]{1,0:T(8,128)(2,1)S(1)}, bf16[64,1280]{1,0:T(8,128)(2,1)S(1)}, u32[]{:S(2)}, u32[]{:S(2)}) collective-permute-start(bf16[64,1280]{1,0:T(8,128)(2,1)S(1)} %add_convert_fusion.4), channel_id=1, source_target_pairs={{0,4},{1,5},{2,6},{3,7},{4,0},{5,1},{6,2},{7,3},{8,12},{9,13},{10,... | collective-permute-start | bytes 491528 | tf_op jit(solution)/shard_map/ppermute | solution.py:567
  261.7 43.5 %collective-permute-start.12 = (bf16[64,1280]{1,0:T(8,128)(2,1)S(1)}, bf16[64,1280]{1,0:T(8,128)(2,1)}, u32[]{:S(2)}, u32[]{:S(2)}) collective-permute-start(bf16[64,1280]{1,0:T(8,128)(2,1)S(1)} %add_convert_fusion.4), channel_id=1, source_target_pairs={{0,6},{1,7},{2,4},{3,5},{4,2},{5,3},{6,0},{7,1},{8,14},{9,15},{10,... | collective-permute-start | bytes 491528 | tf_op jit(solution)/shard_map/ppermute | solution.py:567
  264.9 41.4 %all-to-all-start.3 = ((bf16[4,480,768]{2,1,0:T(8,128)(2,1)}), bf16[4,480,768]{2,1,0:T(8,128)(2,1)S(1)}, u32[]{:S(2)}, u32[]{:S(2)}) async-start(bf16[4,480,768]{2,1,0:T(8,128)(2,1)} %bitcast.51), calls=%async_computation.3 | async-start | bytes 5898240 | tf_op jit(solution)/shard_map/all_to_all | solution.py:562
  316.8 8.4 %collective-permute-start.13 = (bf16[160,1280]{1,0:T(8,128)(2,1)}, bf16[160,1280]{1,0:T(8,128)(2,1)S(1)}, u32[]{:S(2)}, u32[]{:S(2)}) collective-permute-start(bf16[160,1280]{1,0:T(8,128)(2,1)} %get-tuple-element.108), channel_id=1, source_target_pairs={{0,1},{1,0},{2,3},{3,2},{4,5},{5,4},{6,7},{7,6},{8,9},{9,8},{10,11... | collective-permute-start | bytes 1228808 | tf_op jit(solution)/shard_map/ppermute | solution.py:567
  326.4 3.7 collective-permute-start.14
  327.9 4.5 %collective-permute-start.16 = (bf16[32,1280]{1,0:T(8,128)(2,1)S(1)}, bf16[32,1280]{1,0:T(8,128)(2,1)S(1)}, u32[]{:S(2)}, u32[]{:S(2)}) collective-permute-start(bf16[32,1280]{1,0:T(8,128)(2,1)S(1)} %get-tuple-element.136), channel_id=1, source_target_pairs={{0,24},{8,16},{16,8},{24,0},{1,25},{9,17},{17,9},{25,1},{2,26},{10... | collective-permute-start | bytes 245768 | tf_op jit(solution)/shard_map/ppermute | solution.py:567
  332.5 36.5 %all-to-all-start.5 = ((bf16[4,480,768]{2,1,0:T(8,128)(2,1)}), bf16[4,480,768]{2,1,0:T(8,128)(2,1)S(1)}, u32[]{:S(2)}, u32[]{:S(2)}) async-start(bf16[4,480,768]{2,1,0:T(8,128)(2,1)} %bitcast.28), calls=%async_computation.5 | async-start | bytes 5898240 | tf_op jit(solution)/shard_map/all_to_all | solution.py:562
  342.7 5.6 %collective-permute-start.17 = (bf16[64,1280]{1,0:T(8,128)(2,1)S(1)}, bf16[64,1280]{1,0:T(8,128)(2,1)S(1)}, u32[]{:S(2)}, u32[]{:S(2)}) collective-permute-start(bf16[64,1280]{1,0:T(8,128)(2,1)S(1)} %pad_maximum_fusion.6), channel_id=1, source_target_pairs={{0,2},{1,3},{2,0},{3,1},{4,6},{5,7},{6,4},{7,5},{8,10},{9,11},{10,... | collective-permute-start | bytes 491528 | tf_op jit(solution)/shard_map/ppermute | solution.py:567
  343.2 13.3 %collective-permute-start.18 = (bf16[64,1280]{1,0:T(8,128)(2,1)S(1)}, bf16[64,1280]{1,0:T(8,128)(2,1)S(1)}, u32[]{:S(2)}, u32[]{:S(2)}) collective-permute-start(bf16[64,1280]{1,0:T(8,128)(2,1)S(1)} %pad_maximum_fusion.6), channel_id=1, source_target_pairs={{0,4},{1,5},{2,6},{3,7},{4,0},{5,1},{6,2},{7,3},{8,12},{9,13},{10,... | collective-permute-start | bytes 491528 | tf_op jit(solution)/shard_map/ppermute | solution.py:567
  343.2 13.3 %collective-permute-start.19 = (bf16[64,1280]{1,0:T(8,128)(2,1)S(1)}, bf16[64,1280]{1,0:T(8,128)(2,1)S(1)}, u32[]{:S(2)}, u32[]{:S(2)}) collective-permute-start(bf16[64,1280]{1,0:T(8,128)(2,1)S(1)} %pad_maximum_fusion.6), channel_id=1, source_target_pairs={{0,6},{1,7},{2,4},{3,5},{4,2},{5,3},{6,0},{7,1},{8,14},{9,15},{10,... | collective-permute-start | bytes 491528 | tf_op jit(solution)/shard_map/ppermute | solution.py:567
  356.6 33.8 %collective-permute-start.20 = (bf16[128,1280]{1,0:T(8,128)(2,1)S(1)}, bf16[128,1280]{1,0:T(8,128)(2,1)}, u32[]{:S(2)}, u32[]{:S(2)}) collective-permute-start(bf16[128,1280]{1,0:T(8,128)(2,1)S(1)} %constant_dynamic-update-slice_fusion), channel_id=1, source_target_pairs={{0,8},{8,0},{16,24},{24,16},{1,9},{9,1},{17,25},{25,17},{2,10},{10... | collective-permute-start | bytes 983048 | tf_op jit(solution)/shard_map/ppermute | solution.py:567
  356.7 33.7 %collective-permute-start.21 = (bf16[128,1280]{1,0:T(8,128)(2,1)S(1)}, bf16[128,1280]{1,0:T(8,128)(2,1)}, u32[]{:S(2)}, u32[]{:S(2)}) collective-permute-start(bf16[128,1280]{1,0:T(8,128)(2,1)S(1)} %constant_dynamic-update-slice_fusion), channel_id=1, source_target_pairs={{0,16},{8,24},{16,0},{24,8},{1,17},{9,25},{17,1},{25,9},{2,18},{10... | collective-permute-start | bytes 983048 | tf_op jit(solution)/shard_map/ppermute | solution.py:567
  358.1 32.2 %collective-permute-start.22 = (bf16[128,1280]{1,0:T(8,128)(2,1)S(1)}, bf16[128,1280]{1,0:T(8,128)(2,1)}, u32[]{:S(2)}, u32[]{:S(2)}) collective-permute-start(bf16[128,1280]{1,0:T(8,128)(2,1)S(1)} %constant_dynamic-update-slice_fusion), channel_id=1, source_target_pairs={{0,24},{8,16},{16,8},{24,0},{1,25},{9,17},{17,9},{25,1},{2,26},{10... | collective-permute-start | bytes 983048 | tf_op jit(solution)/shard_map/ppermute | solution.py:567
  391.7 8.2 %collective-permute-start.23 = (bf16[4,128,1280]{2,1,0:T(8,128)(2,1)S(1)}, bf16[4,128,1280]{2,1,0:T(8,128)(2,1)S(1)}, u32[]{:S(2)}, u32[]{:S(2)}) collective-permute-start(bf16[4,128,1280]{2,1,0:T(8,128)(2,1)S(1)} %pad_maximum_fusion.1.own_ref), channel_id=1, source_target_pairs={{0,1},{1,0},{2,3},{3,2},{4,5},{5,4},{6,7},{7,6},{8,9},{9,8},{10,11... | collective-permute-start | bytes 3932168 | tf_op jit(solution)/shard_map/ppermute | solution.py:567
  (35 other events, 315.9 us)
Sparse Core Ops, SparseCore 0:
  10.5 33.2 all-gather.3
  46.0 92.1 all-gather.5
  139.9 92.3 all-gather.7
